TPU v7x, 32 devices: a whole 2x2x4 slice. The times are simulated.
32 devices in a mesh: groups: 2 (over x), seq: 16 (over z, y, core).
Axes of the slice: x: 2, y: 2, z: 4, core: 2. Of those that a mesh axis runs over, the one named last changes fastest.
Arguments:
- inputs: bfloat16 [2, 32768, 256], P('groups', 'seq'), parts along dimension 0, may hold values from -6 to 6
- cotangent: bfloat16 [2, 32768, 256], P('groups', 'seq'), parts along dimension 0, may hold values from -6 to 6
- taps_first: bfloat16 [3, 256, 256], replicated, may hold values from -0.21875 to 0.21875
- taps_second: bfloat16 [3, 256, 256], replicated, may hold values from -0.21875 to 0.21875
- bias_first: float32 [256], replicated, may hold values from -3 to 3
- bias_second: float32 [256], replicated, may hold values from -3 to 3
- proj_first: bfloat16 [256, 256], replicated, may hold values from -0.375 to 0.375
- proj_second: bfloat16 [256, 256], replicated, may hold values from -0.375 to 0.375
- gain_first: float32 [256], replicated, may hold values from 0.2 to 1.8
- gain_second: float32 [256], replicated, may hold values from 0.2 to 1.8
Outputs:
- outputs: bfloat16 [2, 32768, 256], P('groups', 'seq'), parts along dimension 0
- input_grad: bfloat16 [2, 32768, 256], P('groups', 'seq'), parts along dimension 0
- taps_grad_first: float32 [6, 256, 256], P('groups'), parts along dimension 0
- taps_grad_second: float32 [6, 256, 256], P('groups'), parts along dimension 0
- proj_grad_first: float32 [512, 256], P('groups'), parts along dimension 0
- proj_grad_second: float32 [512, 256], P('groups'), parts along dimension 0
There are 2 independent parts, one for each index of `groups`. A program takes and returns all parts, laid end to end along the dimension named above; an argument that names none is the same for every part. Nothing has to cross between parts.
All inputs are finite; a program needn't handle non-finite values.
Results may differ from a plain program's by a relative error of at most 0.0068.
Values may be sent and summed in bfloat16 or wider, within the bound.
No kernel may reach another device: no remote copies, remote signals or barrier semaphores. Data moves between devices by JAX's collectives and lax.ppermute only.
A program may use at most 64 MiB of HBM per device.

v0:
```python
import math

import jax
import jax.numpy as jnp
from jax import lax
from jax.sharding import PartitionSpec as P

HOP1 = 4
HOP2 = 8


gelu_coef = 0.7978845608028654


def from_behind_2(block, axis, distance):
    devices = range(lax.axis_size(axis))
    route = [(i - distance, i) for i in devices if i - distance in devices]
    return lax.ppermute(block, axis, route)


def gelu_tanh(values):
    inner = jnp.tanh(gelu_coef * (values + 0.044715 * values * values * values))
    return 0.5 * values * (1.0 + inner)


def gelu_slope(values):
    inner = jnp.tanh(gelu_coef * (values + 0.044715 * values * values * values))
    return 0.5 * (1.0 + inner) + 0.5 * values * (1.0 - inner * inner) * gelu_coef * (
        1.0 + 3.0 * 0.044715 * values * values
    )


def matmul(left, right):
    return jnp.dot(left, right, preferred_element_type=jnp.float32)


def row_product(left, right):
    left_rows = left.reshape(-1, left.shape[-1])
    right_rows = right.reshape(-1, right.shape[-1])
    return lax.dot_general(
        left_rows, right_rows, (((0,), (0,)), ((), ())), preferred_element_type=jnp.float32
    )


def norm_input(source, gain_vec):
    x_wide = source.astype(jnp.float32)
    inv_rms = lax.rsqrt(jnp.mean(x_wide * x_wide, axis=-1, keepdims=True) + 1e-06)
    return (x_wide, inv_rms, x_wide * inv_rms * gain_vec)


def layer_forward(source, params, move):
    kernel, bias_vec, project, gain_vec, jumps = params
    x_wide, inv_rms, normed = norm_input(source, gain_vec)
    activations = gelu_tanh(normed).astype(jnp.bfloat16)
    earlier = move(activations, jumps)
    ahead = move(activations, -jumps)
    hidden = (
        matmul(earlier, kernel[0])
        + matmul(activations, kernel[1])
        + matmul(ahead, kernel[2])
        + bias_vec
    )
    gelled = gelu_tanh(hidden).astype(jnp.bfloat16)
    result = (x_wide + matmul(gelled, project)).astype(jnp.bfloat16)
    return (result, (activations, earlier, ahead, hidden, gelled))


def layer_backward(source, grad_out, params, stored, move):
    kernel, bias_vec, project, gain_vec, jumps = params
    activations, earlier, ahead, hidden, gelled = stored
    proj_grad = row_product(gelled, grad_out)
    grad_hidden = (matmul(grad_out, project.T) * gelu_slope(hidden)).astype(jnp.bfloat16)
    tap_grad = jnp.stack(
        [
            row_product(earlier, grad_hidden),
            row_product(activations, grad_hidden),
            row_product(ahead, grad_hidden),
        ]
    )
    from_ahead = move(grad_hidden, -jumps)
    from_behind = move(grad_hidden, jumps)
    grad_acts = (
        matmul(grad_hidden, kernel[1].T)
        + matmul(from_ahead, kernel[0].T)
        + matmul(from_behind, kernel[2].T)
    )
    x_wide, inv_rms, normed = norm_input(source, gain_vec)
    weighted = grad_acts * gelu_slope(normed) * gain_vec
    grad_in = (
        grad_out.astype(jnp.float32)
        + inv_rms * weighted
        - x_wide * inv_rms * inv_rms * inv_rms * jnp.mean(x_wide * weighted, axis=-1, keepdims=True)
    )
    return (grad_in.astype(jnp.bfloat16), tap_grad, proj_grad)


def run_layers(source, grad_out, first, second, act_move, grad_move):
    middle, stored_first = layer_forward(source, first, act_move)
    result, stored_second = layer_forward(middle, second, act_move)
    middle_grad, taps_two, proj_two = layer_backward(
        middle, grad_out, second, stored_second, grad_move
    )
    grad_in, taps_one, proj_one = layer_backward(
        source, middle_grad, first, stored_first, grad_move
    )
    return (result, grad_in, (taps_one, taps_two, proj_one, proj_two))


def on_device(
    inputs,
    cotangent,
    taps_first,
    taps_second,
    bias_first,
    bias_second,
    proj_first,
    proj_second,
    gain_first,
    gain_second,
):
    devices = lax.axis_size("seq")
    weight_scale = 1.0 / math.sqrt(inputs.shape[0] * inputs.shape[1] * devices)
    first = (taps_first, bias_first, proj_first, gain_first, HOP1)
    second = (taps_second, bias_second, proj_second, gain_second, HOP2)

    def act_move(values, offset):
        return from_behind_2(values, "seq", offset)

    def grad_move(values, offset):
        return from_behind_2(values, "seq", offset)

    result, grad_in, grads = run_layers(inputs, cotangent, first, second, act_move, grad_move)
    summed = lax.psum((grads[0], grads[1], grads[2], grads[3]), "seq")
    return (result, grad_in) + tuple((member * weight_scale for member in summed))


def solution(mesh):
    return jax.shard_map(
        on_device,
        mesh=mesh,
        in_specs=(
            P("groups", "seq", None),
            P("groups", "seq", None),
            P(),
            P(),
            P(),
            P(),
            P(),
            P(),
            P(),
            P(),
        ),
        out_specs=(
            P("groups", "seq", None),
            P("groups", "seq", None),
            P("groups", None, None),
            P("groups", None, None),
            P("groups", None),
            P("groups", None),
        ),
        check_vma=False,
    )
```

profile of v0, /device:TPU:0, one launch (start us, length us, event | category | flops | bytes accessed | tf_op | source)
XLA Modules:
  0.0 281.1 jit_solution(11711721093031718170)
XLA Ops:
  7.2 1.5 copy.16
  9.0 0.9 fusion.24
  9.9 1.3 collective-permute-start.1
  11.2 5.6 %collective-permute-start = (bf16[1,2048,256]{1,2,0:T(8,128)(2,1)S(1)}, bf16[1,2048,256]{1,2,0:T(8,128)(2,1)S(1)}, u32[]{:S(2)}, u32[]{:S(2)}) collective-permute-start(bf16[1,2048,256]{1,2,0:T(8,128)(2,1)S(1)} %fusion.24), channel_id=1, source_target_pairs={{0,4},{1,5},{2,6},{3,7},{4,8},{5,9},{6,10},{7,11},{8,12},{9,13},{1... | collective-permute-start | bytes 3145736 | tf_op jit(solution)/shard_map/ppermute | solution.py:18
  17.3 20.6 %collective-permute-done.1 = bf16[1,2048,256]{1,2,0:T(8,128)(2,1)S(1)} collective-permute-done((bf16[1,2048,256]{1,2,0:T(8,128)(2,1)S(1)}, bf16[1,2048,256]{1,2,0:T(8,128)(2,1)S(1)}, u32[]{:S(2)}, u32[]{:S(2)}) %collective-permute-start.1) | collective-permute-done | bytes 1048608 | tf_op jit(solution)/shard_map/ppermute | solution.py:18
  38.0 0.5 fusion.79
  38.5 0.7 collective-permute-done
  39.2 0.5 fusion.5
  40.2 1.1 fusion.58
  41.5 0.9 fusion.28
  42.5 1.3 collective-permute-start.3
  43.8 7.7 %collective-permute-start.2 = (bf16[1,2048,256]{1,2,0:T(8,128)(2,1)S(1)}, bf16[1,2048,256]{1,2,0:T(8,128)(2,1)}, u32[]{:S(2)}, u32[]{:S(2)}) collective-permute-start(bf16[1,2048,256]{1,2,0:T(8,128)(2,1)S(1)} %fusion.28), channel_id=1, source_target_pairs={{0,8},{1,9},{2,10},{3,11},{4,12},{5,13},{6,14},{7,15},{16,24},{17,... | collective-permute-start | bytes 3145736 | tf_op jit(solution)/shard_map/ppermute | solution.py:18
  51.4 2.3 copy.18
  53.7 1.5 fusion.74
  55.2 36.8 %collective-permute-done.3 = bf16[1,2048,256]{1,2,0:T(8,128)(2,1)} collective-permute-done((bf16[1,2048,256]{1,2,0:T(8,128)(2,1)S(1)}, bf16[1,2048,256]{1,2,0:T(8,128)(2,1)}, u32[]{:S(2)}, u32[]{:S(2)}) %collective-permute-start.3) | collective-permute-done | bytes 1048608 | tf_op jit(solution)/shard_map/ppermute | solution.py:18
  92.0 1.7 fusion.71
  93.7 1.9 fusion.3
  95.7 1.5 fusion.12
  97.1 0.5 copy-done.2
  98.1 1.3 collective-permute-start.4
  99.4 7.4 %collective-permute-start.5 = (bf16[1,2048,256]{2,1,0:T(8,128)(2,1)S(1)}, bf16[1,2048,256]{2,1,0:T(8,128)(2,1)}, u32[]{:S(2)}, u32[]{:S(2)}) collective-permute-start(bf16[1,2048,256]{2,1,0:T(8,128)(2,1)S(1)} %bitcast.143), channel_id=1, source_target_pairs={{0,8},{1,9},{2,10},{3,11},{4,12},{5,13},{6,14},{7,15},{16,24},{17,... | collective-permute-start | bytes 3145736 | tf_op jit(solution)/shard_map/ppermute | solution.py:18
  106.8 2.0 fusion.11
  108.8 1.7 convolution_bitcast_fusion.2
  110.5 1.7 convolution_bitcast_fusion.4
  112.2 0.9 pad_maximum_fusion.1
  113.1 2.3 copy.19
  115.4 1.5 fusion.88
  117.3 1.5 fusion.67
  118.8 27.8 %collective-permute-done.4 = bf16[1,2048,256]{2,1,0:T(8,128)(2,1)} collective-permute-done((bf16[1,2048,256]{2,1,0:T(8,128)(2,1)S(1)}, bf16[1,2048,256]{2,1,0:T(8,128)(2,1)}, u32[]{:S(2)}, u32[]{:S(2)}) %collective-permute-start.4) | collective-permute-done | bytes 1048608 | tf_op jit(solution)/shard_map/ppermute | solution.py:18
  146.6 1.7 convolution_add_fusion.3
  148.4 3.3 %fusion.59 = (f32[2048]{0:T(1024)S(1)}, f32[1,2048,256]{1,2,0:T(8,128)S(1)}) fusion(bf16[1,2048,256]{1,2,0:T(8,128)(2,1)S(1)} %copy-done.10, f32[256]{0:T(256)S(1)} %copy-done.23, f32[2048]{0:T(1024)S(1)} %add_rsqrt_fusion, f32[2048,256]{0,1:T(8,128)S(1)} %convolution_add_fusion.3, bf16[3,256,256]{2,1,0:T(8,128)(2,1)S(1)} %copy-done.18, ...), kind=kOutput, calls=%fused_computation.85 | convolution fusion | flops 281540608 | bytes 6439936 | tf_op jit(solution)/shard_map/dot_general | solution.py:34
  151.7 0.7 fusion.35
  152.4 0.9 copy-done.14
  153.3 1.5 fusion.13
  155.3 1.4 collective-permute-start.6
  156.7 5.5 %collective-permute-start.7 = (bf16[1,2048,256]{2,1,0:T(8,128)(2,1)S(1)}, bf16[1,2048,256]{2,1,0:T(8,128)(2,1)}, u32[]{:S(2)}, u32[]{:S(2)}) collective-permute-start(bf16[1,2048,256]{2,1,0:T(8,128)(2,1)S(1)} %bitcast.141), channel_id=1, source_target_pairs={{0,4},{1,5},{2,6},{3,7},{4,8},{5,9},{6,10},{7,11},{8,12},{9,13},{1... | collective-permute-start | bytes 3145736 | tf_op jit(solution)/shard_map/ppermute | solution.py:18
  163.2 0.9 pad_maximum_fusion
  164.1 1.6 fusion.62
  165.7 1.0 copy-done.20
  167.2 23.4 %collective-permute-done.6 = bf16[1,2048,256]{2,1,0:T(8,128)(2,1)} collective-permute-done((bf16[1,2048,256]{2,1,0:T(8,128)(2,1)S(1)}, bf16[1,2048,256]{2,1,0:T(8,128)(2,1)}, u32[]{:S(2)}, u32[]{:S(2)}) %collective-permute-start.6) | collective-permute-done | bytes 1048608 | tf_op jit(solution)/shard_map/ppermute | solution.py:18
  190.6 1.7 convolution_add_fusion.1
  192.3 2.7 collective-permute-done.7
  195.0 3.2 %fusion.57 = (f32[2048]{0:T(1024)S(1)}, f32[1,2048,256]{1,2,0:T(8,128)S(1)}) fusion(bf16[1,2048,256]{1,2,0:T(8,128)(2,1)S(1)} %copy.16, f32[256]{0:T(256)S(1)} %copy-done.24, f32[2048]{0:T(1024)S(1)} %add_rsqrt_fusion.1, f32[2048,256]{0,1:T(8,128)S(1)} %convolution_add_fusion.1, bf16[3,256,256]{2,1,0:T(8,128)(2,1)S(1)} %copy-done.20, ...), kind=kOutput, calls=%fused_computation.83 | convolution fusion | flops 281540608 | bytes 6439936 | tf_op jit(solution)/shard_map/dot_general | solution.py:34
  198.2 0.7 fusion.39
  199.0 1.3 copy.20
  200.3 69.4 %all-reduce.3.cloned.1.call-done = (f32[3,256,256]{2,1,0:T(8,128)}, f32[3,256,256]{2,1,0:T(8,128)}, f32[256,256]{1,0:T(8,128)}, f32[256,256]{1,0:T(8,128)}) async-done(((f32[3,256,256]{2,1,0:T(8,128)}, f32[3,256,256]{2,1,0:T(8,128)}, f32[256,256]{1,0:T(8,128)}, f32[256,256]{1,0:T(8,128)}), (f32[3,256,256]{2,1,0:T(8,128)}, f32[3,256,256]{2,1,0:T(8,128)}, f32[256,256]{1,0:T(8,128)}, ...) | async-done | bytes 2097168 | tf_op jit(solution)/shard_map/psum | solution.py:133
  269.7 1.9 broadcast_multiply_fusion.2
  271.6 2.7 broadcast_multiply_fusion
  (68 shorter events, 4.3 us)
Async XLA Ops:
  7.2 33.0 %copy-start = (bf16[256,256]{1,0:T(8,128)(2,1)S(1)}, bf16[256,256]{1,0:T(8,128)(2,1)}, u32[]{:S(2)}) copy-start(bf16[256,256]{1,0:T(8,128)(2,1)} %param.16) | copy-start | bytes 393220
  7.2 1.8 copy-start.24
  7.2 262.5 %all-reduce.3.cloned.1.call-start = ((), (), s32[]{:S(2)}) async-start(), calls=%async_computation | async-start | bytes 4194304 | tf_op jit(solution)/shard_map/psum | solution.py:133
  8.7 8.1 %copy-start.19 = (bf16[3,256,256]{2,1,0:T(8,128)(2,1)S(1)}, bf16[3,256,256]{2,1,0:T(8,128)(2,1)}, u32[]{:S(2)}) copy-start(bf16[3,256,256]{2,1,0:T(8,128)(2,1)} %param.12) | copy-start | bytes 1179652
  9.9 28.1 %collective-permute-start.1 = (bf16[1,2048,256]{1,2,0:T(8,128)(2,1)S(1)}, bf16[1,2048,256]{1,2,0:T(8,128)(2,1)S(1)}, u32[]{:S(2)}, u32[]{:S(2)}) collective-permute-start(bf16[1,2048,256]{1,2,0:T(8,128)(2,1)S(1)} %fusion.24), channel_id=1, source_target_pairs={{4,0},{5,1},{6,2},{7,3},{8,4},{9,5},{10,6},{11,7},{12,8},{13,9},{1... | collective-permute-start | bytes 3145736 | tf_op jit(solution)/shard_map/ppermute | solution.py:18
  11.2 28.0 %collective-permute-start = (bf16[1,2048,256]{1,2,0:T(8,128)(2,1)S(1)}, bf16[1,2048,256]{1,2,0:T(8,128)(2,1)S(1)}, u32[]{:S(2)}, u32[]{:S(2)}) collective-permute-start(bf16[1,2048,256]{1,2,0:T(8,128)(2,1)S(1)} %fusion.24), channel_id=1, source_target_pairs={{0,4},{1,5},{2,6},{3,7},{4,8},{5,9},{6,10},{7,11},{8,12},{9,13},{1... | collective-permute-start | bytes 3145736 | tf_op jit(solution)/shard_map/ppermute | solution.py:18
  17.3 21.8 %copy-start.25 = (f32[256]{0:T(256)S(1)}, f32[256]{0:T(256)}, u32[]{:S(2)}) copy-start(f32[256]{0:T(256)} %param.14) | copy-start | bytes 3076
  38.0 1.7 copy-start.5
  39.2 1.0 copy-start.11
  40.2 1.3 copy-start.13
  40.2 1.4 copy-start.23
  41.5 1.0 copy-start.8
  42.5 12.7 %copy-start.1 = (bf16[1,2048,256]{1,2,0:T(8,128)(2,1)}, bf16[1,2048,256]{1,2,0:T(8,128)(2,1)S(1)}, u32[]{:S(2)}) copy-start(bf16[1,2048,256]{1,2,0:T(8,128)(2,1)S(1)} %fusion.28) | copy-start | bytes 3145732
  42.5 49.5 %collective-permute-start.3 = (bf16[1,2048,256]{1,2,0:T(8,128)(2,1)S(1)}, bf16[1,2048,256]{1,2,0:T(8,128)(2,1)}, u32[]{:S(2)}, u32[]{:S(2)}) collective-permute-start(bf16[1,2048,256]{1,2,0:T(8,128)(2,1)S(1)} %fusion.28), channel_id=1, source_target_pairs={{8,0},{9,1},{10,2},{11,3},{12,4},{13,5},{14,6},{15,7},{24,16},{25,... | collective-permute-start | bytes 3145736 | tf_op jit(solution)/shard_map/ppermute | solution.py:18
  43.8 49.9 %collective-permute-start.2 = (bf16[1,2048,256]{1,2,0:T(8,128)(2,1)S(1)}, bf16[1,2048,256]{1,2,0:T(8,128)(2,1)}, u32[]{:S(2)}, u32[]{:S(2)}) collective-permute-start(bf16[1,2048,256]{1,2,0:T(8,128)(2,1)S(1)} %fusion.28), channel_id=1, source_target_pairs={{0,8},{1,9},{2,10},{3,11},{4,12},{5,13},{6,14},{7,15},{16,24},{17,... | collective-permute-start | bytes 3145736 | tf_op jit(solution)/shard_map/ppermute | solution.py:18
  53.7 38.3 %copy-start.17 = (bf16[3,256,256]{2,1,0:T(8,128)(2,1)S(1)}, bf16[3,256,256]{2,1,0:T(8,128)(2,1)}, u32[]{:S(2)}) copy-start(bf16[3,256,256]{2,1,0:T(8,128)(2,1)} %param.13) | copy-start | bytes 1179652
  55.2 38.5 %copy-start.26 = (f32[256]{0:T(256)S(1)}, f32[256]{0:T(256)}, u32[]{:S(2)}) copy-start(f32[256]{0:T(256)} %param.15) | copy-start | bytes 3076
  93.7 2.0 copy-start.21
  93.7 1.9 copy-start.27
  95.6 11.2 %copy-start.15 = (f32[2048,256]{1,0:T(8,128)}, f32[2048,256]{1,0:T(8,128)S(1)}, u32[]{:S(2)}) copy-start(f32[2048,256]{1,0:T(8,128)S(1)} %fusion.3) | copy-start | bytes 6291460
  95.7 2.0 copy-start.2
  97.6 9.2 %copy-start.9 = (bf16[1,2048,256]{1,2,0:T(8,128)(2,1)S(1)}, bf16[1,2048,256]{1,2,0:T(8,128)(2,1)}, u32[]{:S(2)}) copy-start(bf16[1,2048,256]{1,2,0:T(8,128)(2,1)} %copy-done.8) | copy-start | bytes 3145732
  98.1 48.5 %collective-permute-start.4 = (bf16[1,2048,256]{2,1,0:T(8,128)(2,1)S(1)}, bf16[1,2048,256]{2,1,0:T(8,128)(2,1)}, u32[]{:S(2)}, u32[]{:S(2)}) collective-permute-start(bf16[1,2048,256]{2,1,0:T(8,128)(2,1)S(1)} %bitcast.142), channel_id=1, source_target_pairs={{8,0},{9,1},{10,2},{11,3},{12,4},{13,5},{14,6},{15,7},{24,16},{25,... | collective-permute-start | bytes 3145736 | tf_op jit(solution)/shard_map/ppermute | solution.py:18
  99.4 49.0 %collective-permute-start.5 = (bf16[1,2048,256]{2,1,0:T(8,128)(2,1)S(1)}, bf16[1,2048,256]{2,1,0:T(8,128)(2,1)}, u32[]{:S(2)}, u32[]{:S(2)}) collective-permute-start(bf16[1,2048,256]{2,1,0:T(8,128)(2,1)S(1)} %bitcast.143), channel_id=1, source_target_pairs={{0,8},{1,9},{2,10},{3,11},{4,12},{5,13},{6,14},{7,15},{16,24},{17,... | collective-permute-start | bytes 3145736 | tf_op jit(solution)/shard_map/ppermute | solution.py:18
  115.3 1.7 copy-start.16
  115.3 1.9 copy-start.22
  117.3 29.4 %copy-start.18 = (bf16[3,256,256]{2,1,0:T(8,128)(2,1)S(1)}, bf16[3,256,256]{2,1,0:T(8,128)(2,1)}, u32[]{:S(2)}) copy-start(bf16[3,256,256]{2,1,0:T(8,128)(2,1)} %param.13) | copy-start | bytes 1179652
  118.8 29.5 %copy-start.10 = (bf16[1,2048,256]{1,2,0:T(8,128)(2,1)S(1)}, bf16[1,2048,256]{1,2,0:T(8,128)(2,1)}, u32[]{:S(2)}) copy-start(bf16[1,2048,256]{1,2,0:T(8,128)(2,1)} %copy-done.8) | copy-start | bytes 3145732
  148.3 3.4 %copy-start.7 = (bf16[1,2048,256]{1,2,0:T(8,128)(2,1)S(1)}, bf16[1,2048,256]{1,2,0:T(8,128)(2,1)}, u32[]{:S(2)}) copy-start(bf16[1,2048,256]{1,2,0:T(8,128)(2,1)} %copy.18) | copy-start | bytes 3145732
  151.7 1.6 copy-start.14
  153.3 10.8 %copy-start.3 = (bf16[1,2048,256]{1,2,0:T(8,128)(2,1)}, bf16[1,2048,256]{1,2,0:T(8,128)(2,1)S(1)}, u32[]{:S(2)}) copy-start(bf16[1,2048,256]{1,2,0:T(8,128)(2,1)S(1)} %fusion.35) | copy-start | bytes 3145732
  154.9 7.4 %copy-start.6 = (bf16[1,2048,256]{1,2,0:T(8,128)(2,1)S(1)}, bf16[1,2048,256]{1,2,0:T(8,128)(2,1)}, u32[]{:S(2)}) copy-start(bf16[1,2048,256]{1,2,0:T(8,128)(2,1)} %copy-done.5) | copy-start | bytes 3145732
  154.9 7.9 %copy-start.12 = (bf16[1,2048,256]{1,2,0:T(8,128)(2,1)S(1)}, bf16[1,2048,256]{1,2,0:T(8,128)(2,1)}, u32[]{:S(2)}) copy-start(bf16[1,2048,256]{1,2,0:T(8,128)(2,1)} %copy-done.11) | copy-start | bytes 3145732
  155.3 35.3 %collective-permute-start.6 = (bf16[1,2048,256]{2,1,0:T(8,128)(2,1)S(1)}, bf16[1,2048,256]{2,1,0:T(8,128)(2,1)}, u32[]{:S(2)}, u32[]{:S(2)}) collective-permute-start(bf16[1,2048,256]{2,1,0:T(8,128)(2,1)S(1)} %bitcast.140), channel_id=1, source_target_pairs={{4,0},{5,1},{6,2},{7,3},{8,4},{9,5},{10,6},{11,7},{12,8},{13,9},{1... | collective-permute-start | bytes 3145736 | tf_op jit(solution)/shard_map/ppermute | solution.py:18
  156.7 38.2 %collective-permute-start.7 = (bf16[1,2048,256]{2,1,0:T(8,128)(2,1)S(1)}, bf16[1,2048,256]{2,1,0:T(8,128)(2,1)}, u32[]{:S(2)}, u32[]{:S(2)}) collective-permute-start(bf16[1,2048,256]{2,1,0:T(8,128)(2,1)S(1)} %bitcast.141), channel_id=1, source_target_pairs={{0,4},{1,5},{2,6},{3,7},{4,8},{5,9},{6,10},{7,11},{8,12},{9,13},{1... | collective-permute-start | bytes 3145736 | tf_op jit(solution)/shard_map/ppermute | solution.py:18
  165.7 1.0 copy-start.20
  192.3 5.9 %copy-start.4 = (bf16[1,2048,256]{1,2,0:T(8,128)(2,1)S(1)}, bf16[1,2048,256]{1,2,0:T(8,128)(2,1)}, u32[]{:S(2)}) copy-start(bf16[1,2048,256]{1,2,0:T(8,128)(2,1)} %copy-done.3) | copy-start | bytes 3145732
Sparse Core Ops, SparseCore 0:
  165.9 103.7 all-reduce.2
where the time goes:
time: 282 us; the launch traced here: 281 us
  waiting for transfers between devices  181 us (64%)
  matrix products  32.8 us (12%)
  starting transfers between devices  31.5 us (11%)
  between operations  14.5 us (5%)
  local copies, waits for them, and re-layouts  10.9 us (4%)
  other arithmetic  9.88 us (4%)
    ppermute x8, waiting for transfers between devices, from_behind_2(): return lax.ppermute(block, axis, route)  112 us
    psum x1, waiting for transfers between devices, on_device(): summed = lax.psum((grads[0], grads[1], grads[2], grads[3]), 'seq')  69.4 us
    ppermute x8, starting transfers between devices, from_behind_2(): return lax.ppermute(block, axis, route)  31.5 us
    dot_general x16, matrix products, matmul(): return jnp.dot(left, right, preferred_element_type=jnp.float32)  24.6 us
    unnamed x60, local copies, waits for them, and re-layouts  10.9 us
    dot_general x8, matrix products, row_product(): lax.dot_general(left_rows, right_rows, (((0,), (0,)), ((), ())), preferre...  8.22 us
  transfers between devices with their start and end apart: 9, of which 7 were waited for; matrix products, arithmetic and copies ran while one was open for 11% of the time, Pallas kernels for 0%

commit v1 on v0

v1 whole, which is shorter than its diff:
```python
import functools
import math

import jax
import jax.numpy as jnp
from jax import lax
from jax.experimental import pallas as pl
from jax.experimental.pallas import tpu as pltpu
from jax.sharding import Mesh
from jax.sharding import PartitionSpec as P

HOP1 = 4
HOP2 = 8

GELU_COEF = 0.7978845608028654
CUBIC = 0.044715
BF16 = jnp.bfloat16
F32 = jnp.float32


def gelu_parts(v):
    square = v * v
    th = jnp.tanh(v * (GELU_COEF + (GELU_COEF * CUBIC) * square))
    half = 0.5 + 0.5 * th
    value = v * half
    slope = half + value * (1.0 - th) * (GELU_COEF + (3.0 * CUBIC * GELU_COEF) * square)
    return value, slope


def inverse_rms(x):
    return lax.rsqrt(jnp.mean(x * x, axis=-1, keepdims=True) + 1e-06)


def dot(left, right):
    return jnp.dot(left, right, preferred_element_type=F32)


def row_dot(left, right):
    return lax.dot_general(left, right, (((0,), (0,)), ((), ())), preferred_element_type=F32)


def conv_at(parts, taps, p, hop):
    n, width = len(parts), parts[0].shape[-1]
    low = 0 if p - hop >= 0 else 1
    high = 3 if p + hop < n else 2
    left = jnp.concatenate([parts[p + (k - 1) * hop] for k in range(low, high)], axis=-1)
    return dot(left, taps[low * width : high * width, :])


def forward_kernel(hops, x_ref, *refs):
    weights, outs = refs[:8], refs[8:]
    n, tile, width = x_ref.shape
    source = [x_ref[p].astype(F32) for p in range(n)]
    for block in range(2):
        taps, bias, project, gain = weights[4 * block : 4 * block + 4]
        act_out, norm_slope_out, gelled_out, hidden_slope_out, result_out = outs[
            5 * block : 5 * block + 5
        ]
        gain_row = gain[...]
        acts = []
        for p in range(n):
            normed = source[p] * inverse_rms(source[p]) * gain_row
            value, slope = gelu_parts(normed)
            act = value.astype(BF16)
            acts.append(act)
            act_out[p] = act
            norm_slope_out[p] = (slope * gain_row).astype(BF16)
        results = []
        for p in range(n):
            hidden = conv_at(acts, taps, p, hops[block]) + bias[...]
            value, slope = gelu_parts(hidden)
            gelled = value.astype(BF16)
            gelled_out[p] = gelled
            hidden_slope_out[p] = slope.astype(BF16)
            result = (source[p] + dot(gelled, project[...])).astype(BF16)
            result_out[p] = result
            results.append(result.astype(F32))
        source = results


def backward_kernel(hops, y_ref, *refs):
    stored, weights = refs[:10], refs[10:14]
    grad_in_out, grads_out = refs[14], refs[15]
    sums = refs[16]
    n, tile, width = y_ref.shape

    @pl.when(pl.program_id(0) == 0)
    def _():
        sums[...] = jnp.zeros_like(sums)

    grads = [y_ref[p] for p in range(n)]
    for block in (1, 0):
        source, act, norm_slope, gelled, hidden_slope = stored[5 * block : 5 * block + 5]
        taps_t, project_t = weights[2 * block : 2 * block + 2]
        hop = hops[block]
        hidden_grads = []
        for p in range(n):
            hidden = dot(grads[p], project_t[...]) * hidden_slope[p].astype(F32)
            hidden_grads.append(hidden.astype(BF16))
        proj_sum = row_dot(gelled[...].reshape(n * tile, width), jnp.concatenate(grads, axis=0))
        sums[4 * block + 3] += proj_sum
        stacked = jnp.concatenate(hidden_grads, axis=0)
        flat = act[...].reshape(n * tile, width)
        cut = hop * tile
        sums[4 * block] += row_dot(flat[: n * tile - cut], stacked[cut:])
        sums[4 * block + 1] += row_dot(flat, stacked)
        sums[4 * block + 2] += row_dot(flat[cut:], stacked[: n * tile - cut])
        for p in range(n):
            weighted = conv_at(hidden_grads, taps_t, p, hop) * norm_slope[p].astype(F32)
            x = source[p].astype(F32)
            inv = inverse_rms(x)
            unit = x * inv
            mean = jnp.mean(unit * weighted, axis=-1, keepdims=True)
            grads[p] = (grads[p].astype(F32) + inv * (weighted - unit * mean)).astype(BF16)
    for p in range(n):
        grad_in_out[p] = grads[p]

    @pl.when(pl.program_id(0) == pl.num_programs(0) - 1)
    def _():
        grads_out[...] = sums[...].astype(BF16)


def tile_of(n, rows):
    tile = max(16, 512 // n)
    while rows % tile:
        tile //= 2
    return tile


def whole(array):
    zeros = (0,) * array.ndim
    return pl.BlockSpec(array.shape, lambda i: zeros)


def run_forward(x, weights, hops):
    n, rows, width = x.shape
    tile = tile_of(n, rows)
    spec = pl.BlockSpec((n, tile, width), lambda i: (0, i, 0))
    return pl.pallas_call(
        functools.partial(forward_kernel, hops),
        name="forward",
        grid=(rows // tile,),
        in_specs=[spec] + [whole(w) for w in weights],
        out_specs=[spec] * 10,
        out_shape=[jax.ShapeDtypeStruct(x.shape, BF16)] * 10,
        compiler_params=pltpu.CompilerParams(vmem_limit_bytes=48 << 20),
        cost_estimate=pl.CostEstimate(
            flops=16 * x.size * width, bytes_accessed=22 * x.size, transcendentals=4 * x.size
        ),
    )(x, *weights)


def run_backward(y, stored, weights, hops):
    n, rows, width = y.shape
    tile = tile_of(n, rows)
    spec = pl.BlockSpec((n, tile, width), lambda i: (0, i, 0))
    sums = jax.ShapeDtypeStruct((8, width, width), BF16)
    return pl.pallas_call(
        functools.partial(backward_kernel, hops),
        name="backward",
        grid=(rows // tile,),
        in_specs=[spec] * 11 + [whole(w) for w in weights],
        out_specs=[spec, whole(sums)],
        out_shape=[jax.ShapeDtypeStruct(y.shape, BF16), sums],
        scratch_shapes=[pltpu.VMEM((8, width, width), F32)],
        compiler_params=pltpu.CompilerParams(vmem_limit_bytes=48 << 20),
        cost_estimate=pl.CostEstimate(
            flops=32 * y.size * width, bytes_accessed=24 * y.size, transcendentals=0
        ),
    )(y, *stored, *weights)


def exchange(blocks):
    return lax.all_to_all(blocks, "chain", 0, 0, tiled=True)


def reduce_over(values, axis):
    size = lax.axis_size(axis)
    parts = values.reshape((size, values.shape[0] // size) + values.shape[1:])
    parts = lax.all_to_all(parts, axis, 0, 0, tiled=True)
    return parts.astype(F32).sum(0).astype(BF16)


def on_device(
    inputs,
    cotangent,
    taps_first,
    taps_second,
    bias_first,
    bias_second,
    proj_first,
    proj_second,
    gain_first,
    gain_second,
):
    n = lax.axis_size("chain")
    hops = (1, HOP2 // HOP1)
    shape = inputs.shape
    width = shape[-1]
    blocks = (n, shape[0] * shape[1] // n, width)
    weight_scale = 1.0 / math.sqrt(shape[0] * shape[1] * n * HOP1)

    x = exchange(inputs.reshape(blocks))
    y = exchange(cotangent.reshape(blocks))
    flat = (3 * width, width)
    forward_weights = (
        taps_first.reshape(flat), bias_first[None], proj_first, gain_first[None],
        taps_second.reshape(flat), bias_second[None], proj_second, gain_second[None],
    )
    backward_weights = (
        taps_first[::-1].transpose(0, 2, 1).reshape(flat), proj_first.T,
        taps_second[::-1].transpose(0, 2, 1).reshape(flat), proj_second.T,
    )
    act1, norm1, gelled1, hidden1, middle, act2, norm2, gelled2, hidden2, result = run_forward(
        x, forward_weights, hops
    )
    result = exchange(result).reshape(shape)
    stored = (x, act1, norm1, gelled1, hidden1, middle, act2, norm2, gelled2, hidden2)
    grad_in, grads = run_backward(y, stored, backward_weights, hops)
    grad_in = exchange(grad_in).reshape(shape)

    grads = reduce_over(grads.reshape(8 * width, width), "lane")
    grads = reduce_over(grads, "chain")
    grads = lax.all_gather(grads, "chain", axis=0, tiled=True)
    grads = lax.all_gather(grads, "lane", axis=0, tiled=True)
    grads = grads.reshape(2, 4, width, width).astype(F32) * weight_scale
    return (result, grad_in, grads[0, :3], grads[1, :3], grads[0, 3], grads[1, 3])


def solution(mesh):
    groups, seq = mesh.shape["groups"], mesh.shape["seq"]
    own = Mesh(
        mesh.devices.reshape(groups, seq // HOP1, HOP1), ("groups", "chain", "lane")
    )
    split = P("groups", ("chain", "lane"), None)
    return jax.shard_map(
        on_device,
        mesh=own,
        in_specs=(split, split) + (P(),) * 8,
        out_specs=(
            split,
            split,
            P("groups", None, None),
            P("groups", None, None),
            P("groups", None),
            P("groups", None),
        ),
        check_vma=False,
    )
```

time: 282 us -> 203 us (0.72)
  waiting for transfers between devices: 181 us -> 47.7 us
  blocking collectives: 0 us -> 94 us
  matrix products: 32.8 us -> 0 us
  Pallas kernels: 0 us -> 20.8 us
  starting transfers between devices: 31.5 us -> 10.7 us
  other arithmetic: 9.88 us -> 1.71 us
    ppermute x8 -> x0, waiting for transfers between devices: 112 us -> none  [from_behind_2(): return lax.ppermute(block, axis, route)]
    psum x1 -> x0, waiting for transfers between devices: 69.4 us -> none  [on_device(): summed = lax.psum((grads[0], grads[1], grads[2], grads[3]), 'seq')]
    all_to_all x0 -> x3, blocking collectives: none -> 60.5 us  [the longest x1 32.3 us: exchange(): return lax.all_to_all(blocks, 'chain', 0, 0, tiled=True)]
    all_gather x0 -> x1, blocking collectives: none -> 33.5 us  [on_device(): grads = lax.all_gather(grads, 'chain', axis=0, tiled=True)]
    dot_general x24 -> x0, matrix products: 32.8 us -> none  [the longest x16 24.6 us: matmul(): return jnp.dot(left, right, preferred_element_type=jnp.float32)]
    ppermute x8 -> x0, starting transfers between devices: 31.5 us -> none  [from_behind_2(): return lax.ppermute(block, axis, route)]
    all_to_all x0 -> x3, waiting for transfers between devices: none -> 30.9 us  [exchange(): return lax.all_to_all(blocks, 'chain', 0, 0, tiled=True)]
    pallas_call x0 -> x2, Pallas kernels: none -> 20.8 us  [the longest x1 11.5 us: run_forward(): pl.pallas_call(functools.partial(forward_kernel, hops), name='forward', g...]
  transfers between devices with their start and end apart: 9 -> 4, of which waited for: 7 -> 3; matrix products, arithmetic and copies ran while one was open for 11% -> 1% of each run, Pallas kernels for 0% -> 6%
where the time goes in v1:
time: 203 us
  blocking collectives  94 us (46%)
  waiting for transfers between devices  47.7 us (23%)
  Pallas kernels  20.8 us (10%)
  between operations  14.2 us (7%)
  local copies, waits for them, and re-layouts  13.6 us (7%)
  starting transfers between devices  10.7 us (5%)
    all_gather x1, blocking collectives, on_device(): grads = lax.all_gather(grads, 'chain', axis=0, tiled=True)  33.5 us
    all_to_all x1, blocking collectives, exchange(): return lax.all_to_all(blocks, 'chain', 0, 0, tiled=True)  32.3 us
    all_to_all x3, waiting for transfers between devices, exchange(): return lax.all_to_all(blocks, 'chain', 0, 0, tiled=True)  30.9 us
    all_to_all x2, blocking collectives, reduce_over(): parts = lax.all_to_all(parts, axis, 0, 0, tiled=True)  28.2 us
    all_gather x1, waiting for transfers between devices, on_device(): grads = lax.all_gather(grads, 'lane', axis=0, tiled=True)  16.7 us
    pallas_call x1, Pallas kernels, run_forward(): pl.pallas_call(functools.partial(forward_kernel, hops), name='forward', g...  11.5 us
    all_to_all x3, starting transfers between devices, exchange(): return lax.all_to_all(blocks, 'chain', 0, 0, tiled=True)  10.7 us
    unnamed x36, local copies, waits for them, and re-layouts  10.4 us
  transfers between devices with their start and end apart: 4, of which 3 were waited for; matrix products, arithmetic and copies ran while one was open for 1% of the time, Pallas kernels for 6%

profile of v1, /device:TPU:0, one launch (start us, length us, event | category | flops | bytes accessed | tf_op | source)
XLA Modules:
  0.0 202.7 jit_solution(6542620131980903062)
XLA Ops:
  7.2 0.0 copy-start.1
  7.2 32.3 %all_to_all.30.x_ref.refs_0_ = bf16[4,512,256]{2,1,0:T(8,128)(2,1)} all-to-all(bf16[4,512,256]{2,1,0:T(8,128)(2,1)} %bitcast.45), channel_id=1, replica_groups=mesh['groups'=2,'chain'=4,'lane'=4] {'chain'}, dimensions={0} | all-to-all | bytes 2097152 | tf_op jit(solution)/shard_map/all_to_all | solution.py:174
  39.5 3.6 %all-to-all-start.2 = ((bf16[4,512,256]{2,1,0:T(8,128)(2,1)}), bf16[4,512,256]{2,1,0:T(8,128)(2,1)S(1)}, u32[]{:S(2)}, u32[]{:S(2)}) async-start(bf16[4,512,256]{2,1,0:T(8,128)(2,1)} %bitcast.8), calls=%async_computation.2 | async-start | bytes 2097152 | tf_op jit(solution)/shard_map/all_to_all | solution.py:174
  43.1 0.0 copy-done.1
  43.1 0.0 copy-start.5
  43.2 0.0 copy-start.8
  43.2 0.0 copy-start.9
  43.2 0.0 copy-start.10
  43.2 0.0 copy-start.11
  43.2 0.2 copy.20
  43.4 0.0 copy-done.4
  43.4 0.8 copy.21
  44.2 0.0 copy-done.2
  44.2 0.9 copy.22
  45.1 0.0 copy-done.5
  45.1 0.8 copy.23
  45.9 0.0 copy-done.8
  45.9 0.0 copy-done.9
  45.9 0.0 copy-done.10
  45.9 0.0 copy-done.11
  45.9 0.0 copy-start
  45.9 11.5 %forward.1 = (bf16[4,512,256]{2,1,0:T(8,128)(2,1)S(1)}, bf16[4,512,256]{2,1,0:T(8,128)(2,1)S(1)}, bf16[4,512,256]{2,1,0:T(8,128)(2,1)S(1)}, bf16[4,512,256]{2,1,...) custom-call(bf16[4,512,256]{2,1,0:T(8,128)(2,1)} %all_to_all.30.x_re, ...), custom_call_target="tpu_custom_call" | custom-call | flops 2147483648 | bytes 11534336 | tf_op jit(solution)/shard_map/forward/pallas_call | solution.py:139
  57.4 1.0 copy-done.12
  58.4 1.0 copy-done.13
  59.3 1.1 copy-done.14
  60.4 1.1 copy-done.15
  61.4 6.5 %all-to-all-done.2.y_ref = bf16[4,512,256]{2,1,0:T(8,128)(2,1)S(1)} async-done(((bf16[4,512,256]{2,1,0:T(8,128)(2,1)}), bf16[4,512,256]{2,1,0:T(8,128)(2,1)S(1)}, u32[]{:S(2)}, u32[]{:S(2)}) %all-to-all-start.2) | async-done | bytes 1048608 | tf_op jit(solution)/shard_map/all_to_all | solution.py:174
  68.0 0.0 copy-done
  68.0 1.0 copy-done.3
  69.0 0.9 copy-done.6
  69.9 0.9 copy-done.7
  70.8 9.3 %backward.1 = (bf16[4,512,256]{2,1,0:T(8,128)(2,1)}, bf16[8,256,256]{2,1,0:T(8,128)(2,1)S(1)}) custom-call(bf16[4,512,256]{2,1,0:T(8,128)(2,1)S(1)} %all-to-all-done.2.y_ref, bf16[4,512,256]{2,1,0:T(8,128)(2,1)S(1)} %copy-done, bf16[4,512,256]{2,1,0:T(8,128)(2,1)} %copy-done.12, bf16[4,512,256]{2,1,0:T(8,128)(2,1)} %copy-done.13, ...), custom_call_target="tpu_custom_call" | custom-call | flops 4294967296 | bytes 12582912 | tf_op jit(solution)/shard_map/backward/pallas_call | solution.py:158
  80.1 17.0 %all_to_all.31 = bf16[4,512,256]{2,1,0:T(8,128)(2,1)S(1)} all-to-all(bf16[4,512,256]{2,1,0:T(8,128)(2,1)S(1)} %bitcast.29), channel_id=1, replica_groups=mesh['groups'=2,'chain'=4,'lane'=4] {'lane'}, dimensions={0} | all-to-all | bytes 2097152 | tf_op jit(solution)/shard_map/all_to_all | solution.py:180
  97.2 0.3 reduce_sum.24
  97.4 11.2 %all_to_all.32 = bf16[4,128,256]{2,1,0:T(8,128)(2,1)S(1)} all-to-all(bf16[4,128,256]{2,1,0:T(8,128)(2,1)S(1)} %bitcast.44), channel_id=1, replica_groups=mesh['groups'=2,'chain'=4,'lane'=4] {'chain'}, dimensions={0} | all-to-all | bytes 524288 | tf_op jit(solution)/shard_map/all_to_all | solution.py:180
  108.6 3.5 %all-to-all-start.1 = ((bf16[4,512,256]{2,1,0:T(8,128)(2,1)}), bf16[4,512,256]{2,1,0:T(8,128)(2,1)S(1)}, u32[]{:S(2)}, u32[]{:S(2)}) async-start(bf16[4,512,256]{2,1,0:T(8,128)(2,1)} %get-tuple-element.18), calls=%async_computation.1 | async-start | bytes 2097152 | tf_op jit(solution)/shard_map/all_to_all | solution.py:174
  112.2 24.4 %all-to-all-done.1 = bf16[4,512,256]{2,1,0:T(8,128)(2,1)S(1)} async-done(((bf16[4,512,256]{2,1,0:T(8,128)(2,1)}), bf16[4,512,256]{2,1,0:T(8,128)(2,1)S(1)}, u32[]{:S(2)}, u32[]{:S(2)}) %all-to-all-start.1) | async-done | bytes 1048608 | tf_op jit(solution)/shard_map/all_to_all | solution.py:174
  136.6 3.5 %all-to-all-start.3 = ((bf16[4,512,256]{2,1,0:T(8,128)(2,1)}), bf16[4,512,256]{2,1,0:T(8,128)(2,1)S(1)}, u32[]{:S(2)}, u32[]{:S(2)}) async-start(bf16[4,512,256]{2,1,0:T(8,128)(2,1)} %get-tuple-element.28), calls=%async_computation.3 | async-start | bytes 2097152 | tf_op jit(solution)/shard_map/all_to_all | solution.py:174
  140.1 0.0 all-gather.2.cloned.1.call-start
  140.1 33.5 %all_gather.6 = bf16[512,256]{1,0:T(8,128)(2,1)} all-gather(bf16[128,256]{1,0:T(8,128)(2,1)S(1)} %reduce_sum.25), channel_id=1, replica_groups=mesh['groups'=2,'chain'=4,'lane'=4] {'chain'}, dimensions={0}, use_global_device_ids=true | all-gather | bytes 327680 | tf_op jit(solution)/shard_map/all_gather | solution.py:224
  173.7 0.0 all-gather.2.cloned.1.call-update
  173.7 0.0 all-to-all-done.3
  173.7 16.7 %all-gather.2.cloned.1.call-done = bf16[2048,256]{1,0:T(8,128)(2,1)} async-done(((bf16[512,256]{1,0:T(8,128)(2,1)}), bf16[2048,256]{1,0:T(8,128)(2,1)}) %all-gather.2.cloned.1.call-update) | async-done | bytes 1048592 | tf_op jit(solution)/shard_map/all_gather | solution.py:225
  190.4 1.4 convert_multiply_fusion
  191.8 1.2 slice_bitcast_fusion
  193.1 0.8 slice_bitcast_fusion.2
  193.9 1.0 copy.26
  194.9 1.0 copy.27
  (12 shorter events, 0.1 us)
Async XLA Ops:
  7.2 36.0 %copy-start.1 = (bf16[3,256,256]{2,1,0:T(8,128)(2,1)S(1)}, bf16[3,256,256]{2,1,0:T(8,128)(2,1)}, u32[]{:S(2)}) copy-start(bf16[3,256,256]{2,1,0:T(8,128)(2,1)} %param.12) | copy-start | bytes 1179652
  39.5 3.9 %copy-start.4 = (bf16[256,256]{1,0:T(8,128)(2,1)S(1)}, bf16[256,256]{1,0:T(8,128)(2,1)}, u32[]{:S(2)}) copy-start(bf16[256,256]{1,0:T(8,128)(2,1)} %refs_2_.1) | copy-start | bytes 393220
  39.5 4.7 %copy-start.2 = (bf16[3,256,256]{2,1,0:T(8,128)(2,1)S(1)}, bf16[3,256,256]{2,1,0:T(8,128)(2,1)}, u32[]{:S(2)}) copy-start(bf16[3,256,256]{2,1,0:T(8,128)(2,1)} %param.13) | copy-start | bytes 1179652
  39.5 28.5 %all-to-all-start.2 = ((bf16[4,512,256]{2,1,0:T(8,128)(2,1)}), bf16[4,512,256]{2,1,0:T(8,128)(2,1)S(1)}, u32[]{:S(2)}, u32[]{:S(2)}) async-start(bf16[4,512,256]{2,1,0:T(8,128)(2,1)} %bitcast.8), calls=%async_computation.2 | async-start | bytes 2097152 | tf_op jit(solution)/shard_map/all_to_all | solution.py:174
  43.1 2.0 copy-start.5
  43.2 2.7 %copy-start.8 = (f32[256]{0:T(256)S(1)}, f32[256]{0:T(256)}, u32[]{:S(2)}) copy-start(f32[256]{0:T(256)} %param.14) | copy-start | bytes 3076
  43.2 2.7 %copy-start.9 = (f32[256]{0:T(256)S(1)}, f32[256]{0:T(256)}, u32[]{:S(2)}) copy-start(f32[256]{0:T(256)} %param.18) | copy-start | bytes 3076
  43.2 2.7 %copy-start.10 = (f32[256]{0:T(256)S(1)}, f32[256]{0:T(256)}, u32[]{:S(2)}) copy-start(f32[256]{0:T(256)} %param.15) | copy-start | bytes 3076
  43.2 2.7 %copy-start.11 = (f32[256]{0:T(256)S(1)}, f32[256]{0:T(256)}, u32[]{:S(2)}) copy-start(f32[256]{0:T(256)} %param.19) | copy-start | bytes 3076
  45.9 22.1 %copy-start = (bf16[4,512,256]{2,1,0:T(8,128)(2,1)S(1)}, bf16[4,512,256]{2,1,0:T(8,128)(2,1)}, u32[]{:S(2)}) copy-start(bf16[4,512,256]{2,1,0:T(8,128)(2,1)} %all_to_all.30.x_ref.refs_0_) | copy-start | bytes 3145732
  57.4 1.0 copy-start.12
  58.4 1.0 copy-start.13
  59.3 1.1 copy-start.14
  60.4 1.1 copy-start.15
  68.0 1.0 copy-start.3
  69.0 0.9 copy-start.6
  69.9 0.9 copy-start.7
  108.6 28.0 %all-to-all-start.1 = ((bf16[4,512,256]{2,1,0:T(8,128)(2,1)}), bf16[4,512,256]{2,1,0:T(8,128)(2,1)S(1)}, u32[]{:S(2)}, u32[]{:S(2)}) async-start(bf16[4,512,256]{2,1,0:T(8,128)(2,1)} %get-tuple-element.18), calls=%async_computation.1 | async-start | bytes 2097152 | tf_op jit(solution)/shard_map/all_to_all | solution.py:174
  136.6 37.1 %all-to-all-start.3 = ((bf16[4,512,256]{2,1,0:T(8,128)(2,1)}), bf16[4,512,256]{2,1,0:T(8,128)(2,1)S(1)}, u32[]{:S(2)}, u32[]{:S(2)}) async-start(bf16[4,512,256]{2,1,0:T(8,128)(2,1)} %get-tuple-element.28), calls=%async_computation.3 | async-start | bytes 2097152 | tf_op jit(solution)/shard_map/all_to_all | solution.py:174
  140.1 50.3 %all-gather.2.cloned.1.call-start = ((), (), s32[]{:S(2)}) async-start(), calls=%async_computation.6 | async-start | bytes 1310720 | tf_op jit(solution)/shard_map/all_gather | solution.py:225
Sparse Core Ops, SparseCore 0:
  173.8 16.5 all-gather.1

commit v2 on v1

v2 whole, which is shorter than its diff:
```python
import functools
import math

import jax
import jax.numpy as jnp
from jax import lax
from jax.experimental import pallas as pl
from jax.experimental.pallas import tpu as pltpu
from jax.sharding import Mesh
from jax.sharding import PartitionSpec as P

HOP1 = 4
HOP2 = 8

GELU_COEF = 0.7978845608028654
CUBIC = 0.044715
CHUNKS = 2
FLOPS = 1000
VMEM_LIMIT = 60 << 20
BF16 = jnp.bfloat16
F32 = jnp.float32


def gelu_parts(v):
    square = v * v
    th = jnp.tanh(v * (GELU_COEF + (GELU_COEF * CUBIC) * square))
    half = 0.5 + 0.5 * th
    value = v * half
    slope = half + value * (1.0 - th) * (GELU_COEF + (3.0 * CUBIC * GELU_COEF) * square)
    return value, slope


def inverse_rms(x):
    return lax.rsqrt(jnp.mean(x * x, axis=-1, keepdims=True) + 1e-06)


def dot(left, right):
    return jnp.dot(left, right, preferred_element_type=F32)


def row_dot(left, right):
    return lax.dot_general(left, right, (((0,), (0,)), ((), ())), preferred_element_type=F32)


def conv_at(parts, tile, taps, p, n, hop):
    width = parts.shape[-1]
    low = 0 if p - hop >= 0 else 1
    high = 3 if p + hop < n else 2
    left = jnp.concatenate(
        [parts[pl.ds((p + (k - 1) * hop) * tile, tile), :] for k in range(low, high)], axis=-1
    )
    return dot(left, taps[low * width : high * width, :])


def over_rows(total, body, step=64):
    def one(i, carry):
        body(pl.ds(pl.multiple_of(i * step, step), step))
        return carry

    lax.fori_loop(0, total // step, one, 0, unroll=2)


def chunk_kernel(n, hops, last, me_ref, *refs):
    own_ref, pieces, weights = refs[0], refs[1:n], refs[n : n + 12]
    refs = refs[n + 12 :]
    if last:
        before, refs = refs[0], refs[1:]
    own_out, piece_outs, refs = refs[0], refs[1:n], refs[n:]
    if last:
        keep_out, send_out, sums = refs[:3]
        refs = refs[3:]
    else:
        sums, refs = refs[0], refs[1:]
    sources, grad, wide, hidden_grad, acts, gelleds, norm_slopes, hidden_slopes = refs
    me, core = me_ref[0], me_ref[1]
    tile, width = own_ref.shape[1:]
    total = n * tile

    for s in range(n):
        piece = own_ref if s == 0 else pieces[s - 1]
        rows = pl.ds(pl.multiple_of((me ^ s) * tile, tile), tile)
        sources[0, rows, :] = piece[0]
        grad[rows, :] = piece[1]

    for block in range(2):
        taps, bias, project, gain = weights[4 * block : 4 * block + 4]
        gain_row, bias_row = gain[...], bias[...]

        def before_conv(rows):
            x = sources[block, rows, :].astype(F32)
            value, slope = gelu_parts(x * inverse_rms(x) * gain_row)
            acts[block, rows, :] = value.astype(BF16)
            norm_slopes[block, rows, :] = slope * gain_row

        over_rows(total, before_conv)
        for p in range(n):
            wide[pl.ds(p * tile, tile), :] = conv_at(
                acts.at[block], tile, taps, p, n, hops[block]
            )

        def after_conv(rows):
            value, slope = gelu_parts(wide[rows, :] + bias_row)
            gelleds[block, rows, :] = value.astype(BF16)
            hidden_slopes[block, rows, :] = slope

        over_rows(total, after_conv)
        sources[block + 1] = (
            sources[block].astype(F32) + dot(gelleds[block], project[...])
        ).astype(BF16)

    def send(source, k):
        for s in range(n):
            piece = own_out if s == 0 else piece_outs[s - 1]
            piece[k] = source[pl.ds(pl.multiple_of((me ^ s) * tile, tile), tile), :]

    send(sources.at[2], 0)

    def add(k, value):
        sums[k] = before[k] + value if last else value

    for block in (1, 0):
        taps_t, project_t = weights[8 + 2 * block : 10 + 2 * block]
        hop = hops[block]
        cut = hop * tile
        add(4 * block + 3, row_dot(gelleds[block], grad[...]))
        wide[...] = dot(grad[...], project_t[...])

        def hidden_rows(rows):
            hidden_grad[rows, :] = (wide[rows, :] * hidden_slopes[block, rows, :]).astype(BF16)

        over_rows(total, hidden_rows)
        add(4 * block, row_dot(acts[block, : total - cut, :], hidden_grad[cut:, :]))
        add(4 * block + 1, row_dot(acts[block], hidden_grad[...]))
        add(4 * block + 2, row_dot(acts[block, cut:, :], hidden_grad[: total - cut, :]))
        for p in range(n):
            wide[pl.ds(p * tile, tile), :] = conv_at(hidden_grad, tile, taps_t, p, n, hop)

        def source_rows(rows):
            weighted = wide[rows, :] * norm_slopes[block, rows, :]
            x = sources[block, rows, :].astype(F32)
            inv = inverse_rms(x)
            unit = x * inv
            mean = jnp.mean(unit * weighted, axis=-1, keepdims=True)
            grad[rows, :] = (
                grad[rows, :].astype(F32) + inv * (weighted - unit * mean)
            ).astype(BF16)

        over_rows(total, source_rows)

    send(grad, 1)
    if last:
        keep_out[...] = sums[pl.ds(4 * core, 4)]
        send_out[...] = sums[pl.ds(4 * (1 - core), 4)].astype(BF16)


def run_chunk(me, pieces, weights, before, hops):
    n, (_, rows, width) = len(pieces), pieces[0].shape
    last = before is not None
    total = n * rows
    full = jax.ShapeDtypeStruct((8, width, width), F32)
    half = (4, width, width)
    sums = [jax.ShapeDtypeStruct(half, F32), jax.ShapeDtypeStruct(half, BF16)]
    scratch = [pltpu.VMEM(full.shape, F32)] if last else []
    operands = [*pieces, *weights] + ([before] if last else [])
    outs = pl.pallas_call(
        functools.partial(chunk_kernel, n, hops, last),
        name="chunk",
        in_specs=[pl.BlockSpec(memory_space=pltpu.SMEM)]
        + [pl.BlockSpec(operand.shape, None) for operand in operands],
        out_shape=[jax.ShapeDtypeStruct(pieces[0].shape, BF16)] * n + (sums if last else [full]),
        scratch_shapes=scratch
        + [
            pltpu.VMEM((3, total, width), BF16),
            pltpu.VMEM((total, width), BF16),
            pltpu.VMEM((total, width), F32),
            pltpu.VMEM((total, width), BF16),
            pltpu.VMEM((2, total, width), BF16),
            pltpu.VMEM((2, total, width), BF16),
            pltpu.VMEM((2, total, width), F32),
            pltpu.VMEM((2, total, width), F32),
        ],
        compiler_params=pltpu.CompilerParams(vmem_limit_bytes=VMEM_LIMIT),
        cost_estimate=pl.CostEstimate(flops=FLOPS, bytes_accessed=FLOPS, transcendentals=0),
    )(me, *operands)
    return list(outs[:n]), list(outs[n:])


def take(array, index):
    return lax.dynamic_index_in_dim(array, index, 0, keepdims=False)


def swap(values, axis, s=1):
    return lax.ppermute(values, axis, [(i, i ^ s) for i in range(lax.axis_size(axis))])


def spread(array, me):
    n = array.shape[0]
    return [swap(take(array, me ^ s), "chain", s) for s in range(1, n)]


def assemble(pieces, me):
    out = jnp.stack(pieces)
    return jnp.take(out, me ^ jnp.arange(len(pieces)), axis=0)


def on_device(
    inputs,
    cotangent,
    taps_first,
    taps_second,
    bias_first,
    bias_second,
    proj_first,
    proj_second,
    gain_first,
    gain_second,
):
    n = lax.axis_size("chain")
    place, pair, core = (lax.axis_index(axis) for axis in ("chain", "pair", "core"))
    me = jnp.stack([place, core]).astype(jnp.int32)
    hops = (1, HOP2 // HOP1)
    shape = inputs.shape
    width = shape[-1]
    weight_scale = 1.0 / math.sqrt(shape[0] * shape[1] * n * HOP1)
    rows = shape[0] * shape[1] // (CHUNKS * n)
    both = jnp.stack([inputs, cotangent]).reshape(2, CHUNKS, n, rows, width)

    def block_of(chunk, s):
        start = (0, chunk, place ^ s, 0, 0)
        return lax.dynamic_slice(both, start, (2, 1, 1, rows, width)).reshape(2, rows, width)

    flat = (3 * width, width)
    weights = (
        taps_first.reshape(flat), bias_first[None], proj_first, gain_first[None],
        taps_second.reshape(flat), bias_second[None], proj_second, gain_second[None],
        taps_first[::-1].transpose(0, 2, 1).reshape(flat), proj_first.T,
        taps_second[::-1].transpose(0, 2, 1).reshape(flat), proj_second.T,
    )
    order = sorted(range(1, n), reverse=True)
    arrived = [{}, {}]
    for s in order:
        arrived[0][s] = swap(block_of(0, s), "chain", s)
    for s in order:
        arrived[0][s], block = lax.optimization_barrier((arrived[0][s], block_of(1, s)))
        arrived[1][s] = swap(block, "chain", s)

    def pieces_of(chunk):
        return [block_of(chunk, 0)] + [arrived[chunk][s] for s in range(1, n)]

    def send_back(pieces):
        return pieces[:1] + [swap(pieces[s], "chain", s) for s in range(1, n)]

    results = [None, None]
    pieces, before = run_chunk(me, pieces_of(0), weights, None, hops)
    pieces, last_pieces = lax.optimization_barrier((pieces, pieces_of(1)))
    results[0] = send_back(pieces)
    pieces, (keep, send) = run_chunk(me, last_pieces, weights, before[0], hops)
    results[1] = send_back(pieces)

    results[0][3], send = lax.optimization_barrier((results[0][3], send))
    got = swap(send, "core")
    half = (keep + got).reshape(2, 2 * width, width)
    got = swap(take(half, 1 - pair).astype(BF16), "pair")
    quarter = (take(half, pair) + got).reshape(n, 2 * width // n, width)
    results[0], quarter = lax.optimization_barrier((results[0], quarter))
    got = spread(quarter.astype(BF16), place)
    total = take(quarter, place)
    for part in got:
        total = total + part
    total = (total * weight_scale).astype(BF16)

    quarter = assemble([total] + [swap(total, "chain", s) for s in range(1, n)], place)
    results[1][3], quarter = lax.optimization_barrier((results[1][3], quarter))
    quarter = quarter.reshape(2 * width, width)
    half = jnp.stack([quarter, swap(quarter, "pair")])
    half = jnp.where(pair == 0, half, half[::-1]).reshape(4, width, width)
    other = swap(half, "core")
    first = jnp.where(core == 0, half, other).astype(F32)
    second = jnp.where(core == 0, other, half).astype(F32)
    outputs = jnp.stack([assemble(pieces, place) for pieces in results])
    return (
        outputs[:, :, 0].reshape(shape),
        outputs[:, :, 1].reshape(shape),
        first[:3],
        second[:3],
        first[3],
        second[3],
    )


def solution(mesh):
    groups, seq = mesh.shape["groups"], mesh.shape["seq"]
    own = Mesh(
        mesh.devices.reshape(groups, seq // HOP1, HOP1 // 2, 2),
        ("groups", "chain", "pair", "core"),
    )
    split = P("groups", ("chain", "pair", "core"), None)
    return jax.shard_map(
        on_device,
        mesh=own,
        in_specs=(split, split) + (P(),) * 8,
        out_specs=(
            split,
            split,
            P("groups", None, None),
            P("groups", None, None),
            P("groups", None),
            P("groups", None),
        ),
        check_vma=False,
    )
```

time: 203 us -> 143 us (0.70)
  blocking collectives: 94 us -> 0 us
  starting transfers between devices: 10.7 us -> 33.6 us
  between operations: 14.2 us -> 0.94 us
  Pallas kernels: 20.8 us -> 31.6 us
  other arithmetic: 1.71 us -> 11.9 us
  waiting for transfers between devices: 47.7 us -> 56.3 us
  local copies, waits for them, and re-layouts: 13.6 us -> 8.05 us
    all_to_all x3 -> x0, blocking collectives: 60.5 us -> none  [the longest x1 32.3 us: exchange(): return lax.all_to_all(blocks, 'chain', 0, 0, tiled=True)]
    ppermute x0 -> x22, waiting for transfers between devices: none -> 56.3 us  [swap(): lax.ppermute(values, axis, [(i, i ^ s) for i in range(lax.axis_size(axis))])]
    ppermute x0 -> x22, starting transfers between devices: none -> 33.6 us  [swap(): lax.ppermute(values, axis, [(i, i ^ s) for i in range(lax.axis_size(axis))])]
    all_gather x1 -> x0, blocking collectives: 33.5 us -> none  [on_device(): grads = lax.all_gather(grads, 'chain', axis=0, tiled=True)]
    all_to_all x3 -> x0, waiting for transfers between devices: 30.9 us -> none  [exchange(): return lax.all_to_all(blocks, 'chain', 0, 0, tiled=True)]
    all_gather x1 -> x0, waiting for transfers between devices: 16.7 us -> none  [on_device(): grads = lax.all_gather(grads, 'lane', axis=0, tiled=True)]
    pallas_call x2, Pallas kernels: 20.8 us -> 31.6 us  [run_chunk(): pl.pallas_call(functools.partial(chunk_kernel, n, hops, last), name='chun...]
    all_to_all x3 -> x0, starting transfers between devices: 10.7 us -> none  [exchange(): return lax.all_to_all(blocks, 'chain', 0, 0, tiled=True)]
  transfers between devices with their start and end apart: 4 -> 22, of which waited for: 3 -> 11; matrix products, arithmetic and copies ran while one was open for 1% -> 8% of each run, Pallas kernels for 6% -> 22%
where the time goes in v2:
time: 143 us; the launch traced here: 142 us
  waiting for transfers between devices  56.3 us (39%)
  starting transfers between devices  33.6 us (23%)
  Pallas kernels  31.6 us (22%)
  other arithmetic  11.9 us (8%)
  local copies, waits for them, and re-layouts  8.05 us (6%)
    ppermute x22, waiting for transfers between devices, swap(): lax.ppermute(values, axis, [(i, i ^ s) for i in range(lax.axis_size(axis))])  56.3 us
    ppermute x22, starting transfers between devices, swap(): lax.ppermute(values, axis, [(i, i ^ s) for i in range(lax.axis_size(axis))])  33.6 us
    pallas_call x2, Pallas kernels, run_chunk(): pl.pallas_call(functools.partial(chunk_kernel, n, hops, last), name='chun...  31.6 us
    reshape x2, other arithmetic, block_of(): lax.dynamic_slice(both, start, (2, 1, 1, rows, width))  3.37 us
  transfers between devices with their start and end apart: 22, of which 11 were waited for; matrix products, arithmetic and copies ran while one was open for 8% of the time, Pallas kernels for 22%

profile of v2, /device:TPU:0, one launch (start us, length us, event | category | flops | bytes accessed | tf_op | source)
XLA Modules:
  0.0 142.4 jit_solution(18368569569570020512)
XLA Ops:
  0.7 2.6 %fusion.17 = (bf16[2,256,256]{2,1,0:T(8,128)(2,1)}, bf16[2,256,256]{2,1,0:T(8,128)(2,1)S(1)}, bf16[2,256,256]{2,1,0:T(8,128)(2,1)}, bf16[2,256,256]{2,1,0:T(8,12...) fusion(s32[]{:T(128)S(6)} %select_n.75, ...), kind=kLoop, calls=%fused_computation.55 | loop fusion | flops 917504 | bytes 3932176 | tf_op jit(solution)/shard_map/reshape | solution.py:230
  3.3 5.1 %collective-permute-start.2 = (bf16[2,256,256]{2,1,0:T(8,128)(2,1)S(1)}, bf16[2,256,256]{2,1,0:T(8,128)(2,1)S(1)}, u32[]{:S(2)}, u32[]{:S(2)}) collective-permute-start(bf16[2,256,256]{2,1,0:T(8,128)(2,1)S(1)} %get-tuple-element.82), channel_id=1, source_target_pairs={{0,12},{4,8},{8,4},{12,0},{1,13},{5,9},{9,5},{13,1},{2,14},{6,10},... | collective-permute-start | bytes 786440 | tf_op jit(solution)/shard_map/ppermute | solution.py:193
  8.5 0.6 collective-permute-start
  9.1 6.6 %collective-permute-done.2.refs_3_ = bf16[2,256,256]{2,1,0:T(8,128)(2,1)S(1)} collective-permute-done((bf16[2,256,256]{2,1,0:T(8,128)(2,1)S(1)}, bf16[2,256,256]{2,1,0:T(8,128)(2,1)S(1)}, u32[]{:S(2)}, u32[]{:S(2)}) %collective-permute-start.2) | collective-permute-done | bytes 262176 | tf_op jit(solution)/shard_map/ppermute | solution.py:193
  15.7 15.0 %collective-permute-done.1.refs_2_ = bf16[2,256,256]{2,1,0:T(8,128)(2,1)S(1)} collective-permute-done((bf16[2,256,256]{2,1,0:T(8,128)(2,1)S(1)}, bf16[2,256,256]{2,1,0:T(8,128)(2,1)S(1)}, u32[]{:S(2)}, u32[]{:S(2)}) %collective-permute-start.1) | collective-permute-done | bytes 262176 | tf_op jit(solution)/shard_map/ppermute | solution.py:193
  30.8 2.5 %collective-permute-start.5 = (bf16[2,256,256]{2,1,0:T(8,128)(2,1)}, bf16[2,256,256]{2,1,0:T(8,128)(2,1)}, u32[]{:S(2)}, u32[]{:S(2)}) collective-permute-start(bf16[2,256,256]{2,1,0:T(8,128)(2,1)} %get-tuple-element.50), channel_id=1, source_target_pairs={{0,12},{4,8},{8,4},{12,0},{1,13},{5,9},{9,5},{13,1},{2,14},{6,10},... | collective-permute-start | bytes 786440 | tf_op jit(solution)/shard_map/ppermute | solution.py:193
  33.3 1.9 %collective-permute-start.3 = (bf16[2,256,256]{2,1,0:T(8,128)(2,1)}, bf16[2,256,256]{2,1,0:T(8,128)(2,1)}, u32[]{:S(2)}, u32[]{:S(2)}) collective-permute-start(bf16[2,256,256]{2,1,0:T(8,128)(2,1)} %get-tuple-element.48), channel_id=1, source_target_pairs={{0,4},{4,0},{8,12},{12,8},{1,5},{5,1},{9,13},{13,9},{2,6},{6,2},{1... | collective-permute-start | bytes 786440 | tf_op jit(solution)/shard_map/ppermute | solution.py:193
  35.3 0.9 copy.18
  36.2 0.9 copy.20
  37.1 0.8 copy.19
  37.9 0.8 copy.21
  38.6 0.6 pad_add_fusion.me_ref
  39.3 0.8 fusion.16.refs_0_
  40.0 15.5 %chunk.2 = (bf16[2,256,256]{2,1,0:T(8,128)(2,1)}, bf16[2,256,256]{2,1,0:T(8,128)(2,1)}, bf16[2,256,256]{2,1,0:T(8,128)(2,1)}, bf16[2,256,256]{2,1,0:T(8,128)(2,1)}, f32[8,256,256]{2,1,0:T(8,128)}) custom-call(s32[2]{0:T(128)} %pad_add_fusion.me_ref, bf16[2,256,256]{2,1,0:T(8,128)(2,1)} %fusion.16.refs_0_, bf16[2,256,256]{2,1,0:T(8,128)(2,1)} %copy-done.13, ...), custom_call_target="tpu_custom_call" | custom-call | flops 1000 | bytes 1000 | tf_op jit(solution)/shard_map/chunk/pallas_call | solution.py:165
  55.5 2.5 %collective-permute-start.8 = (bf16[2,256,256]{2,1,0:T(8,128)(2,1)}, bf16[2,256,256]{2,1,0:T(8,128)(2,1)S(1)}, u32[]{:S(2)}, u32[]{:S(2)}) collective-permute-start(bf16[2,256,256]{2,1,0:T(8,128)(2,1)} %get-tuple-element.54), channel_id=1, source_target_pairs={{0,12},{4,8},{8,4},{12,0},{1,13},{5,9},{9,5},{13,1},{2,14},{6,10},... | collective-permute-start | bytes 786440 | tf_op jit(solution)/shard_map/ppermute | solution.py:193
  58.0 16.1 %chunk.3 = (bf16[2,256,256]{2,1,0:T(8,128)(2,1)}, bf16[2,256,256]{2,1,0:T(8,128)(2,1)}, bf16[2,256,256]{2,1,0:T(8,128)(2,1)}, bf16[2,256,256]{2,1,0:T(8,128)(2,1...) custom-call(s32[2]{0:T(128)} %pad_add_fusion.me_ref, bf16[2,256,256]{2,1,0:T(8,128)(2,1)} %get-tuple-element.55.refs_0_, ...), custom_call_target="tpu_custom_call" | custom-call | flops 1000 | bytes 1000 | tf_op jit(solution)/shard_map/chunk/pallas_call | solution.py:165
  74.3 2.1 %collective-permute-done.9 = bf16[4,256,256]{2,1,0:T(8,128)(2,1)S(1)} collective-permute-done((bf16[4,256,256]{2,1,0:T(8,128)(2,1)}, bf16[4,256,256]{2,1,0:T(8,128)(2,1)S(1)}, u32[]{:S(2)}, u32[]{:S(2)}) %collective-permute-start.9) | collective-permute-done | bytes 524320 | tf_op jit(solution)/shard_map/ppermute | solution.py:193
  76.4 1.3 convert_add_fusion
  77.8 1.6 %collective-permute-start.10 = (bf16[512,256]{1,0:T(8,128)(2,1)S(1)}, bf16[512,256]{1,0:T(8,128)(2,1)S(1)}, u32[]{:S(2)}, u32[]{:S(2)}) collective-permute-start(bf16[512,256]{1,0:T(8,128)(2,1)S(1)} %fusion.9), channel_id=1, source_target_pairs={{0,2},{2,0},{1,3},{3,1},{4,6},{6,4},{5,7},{7,5},{8,10},{10,8},{9,1... | collective-permute-start | bytes 786440 | tf_op jit(solution)/shard_map/ppermute | solution.py:193
  79.4 1.9 %collective-permute-start.7 = (bf16[2,256,256]{2,1,0:T(8,128)(2,1)S(1)}, bf16[2,256,256]{2,1,0:T(8,128)(2,1)S(1)}, u32[]{:S(2)}, u32[]{:S(2)}) collective-permute-start(bf16[2,256,256]{2,1,0:T(8,128)(2,1)S(1)} %copy-done.15), channel_id=1, source_target_pairs={{0,8},{4,12},{8,0},{12,4},{1,9},{5,13},{9,1},{13,5},{2,10},{6,14},... | collective-permute-start | bytes 786440 | tf_op jit(solution)/shard_map/ppermute | solution.py:193
  81.3 4.9 %collective-permute-done.10 = bf16[512,256]{1,0:T(8,128)(2,1)S(1)} collective-permute-done((bf16[512,256]{1,0:T(8,128)(2,1)S(1)}, bf16[512,256]{1,0:T(8,128)(2,1)S(1)}, u32[]{:S(2)}, u32[]{:S(2)}) %collective-permute-start.10) | collective-permute-done | bytes 262176 | tf_op jit(solution)/shard_map/ppermute | solution.py:193
  86.3 5.5 %collective-permute-done.6 = bf16[2,256,256]{2,1,0:T(8,128)(2,1)S(1)} collective-permute-done((bf16[2,256,256]{2,1,0:T(8,128)(2,1)S(1)}, bf16[2,256,256]{2,1,0:T(8,128)(2,1)S(1)}, u32[]{:S(2)}, u32[]{:S(2)}) %collective-permute-start.6) | collective-permute-done | bytes 262176 | tf_op jit(solution)/shard_map/ppermute | solution.py:193
  91.8 2.3 %collective-permute-done.7 = bf16[2,256,256]{2,1,0:T(8,128)(2,1)S(1)} collective-permute-done((bf16[2,256,256]{2,1,0:T(8,128)(2,1)S(1)}, bf16[2,256,256]{2,1,0:T(8,128)(2,1)S(1)}, u32[]{:S(2)}, u32[]{:S(2)}) %collective-permute-start.7) | collective-permute-done | bytes 262176 | tf_op jit(solution)/shard_map/ppermute | solution.py:193
  94.2 1.9 %collective-permute-start.15 = (bf16[128,256]{1,0:T(8,128)(2,1)S(1)}, bf16[128,256]{1,0:T(8,128)(2,1)S(1)}, u32[]{:S(2)}, u32[]{:S(2)}) collective-permute-start(bf16[128,256]{1,0:T(8,128)(2,1)S(1)} %get-tuple-element.88), channel_id=1, source_target_pairs={{0,8},{4,12},{8,0},{12,4},{1,9},{5,13},{9,1},{13,5},{2,10},{6,14},... | collective-permute-start | bytes 196616 | tf_op jit(solution)/shard_map/ppermute | solution.py:193
  96.2 2.4 %collective-permute-start.16 = (bf16[128,256]{1,0:T(8,128)(2,1)S(1)}, bf16[128,256]{1,0:T(8,128)(2,1)S(1)}, u32[]{:S(2)}, u32[]{:S(2)}) collective-permute-start(bf16[128,256]{1,0:T(8,128)(2,1)S(1)} %get-tuple-element.87), channel_id=1, source_target_pairs={{0,12},{4,8},{8,4},{12,0},{1,13},{5,9},{9,5},{13,1},{2,14},{6,10},... | collective-permute-start | bytes 196616 | tf_op jit(solution)/shard_map/ppermute | solution.py:193
  98.6 2.4 %collective-permute-done.15 = bf16[128,256]{1,0:T(8,128)(2,1)S(1)} collective-permute-done((bf16[128,256]{1,0:T(8,128)(2,1)S(1)}, bf16[128,256]{1,0:T(8,128)(2,1)S(1)}, u32[]{:S(2)}, u32[]{:S(2)}) %collective-permute-start.15) | collective-permute-done | bytes 65568 | tf_op jit(solution)/shard_map/ppermute | solution.py:193
  101.0 1.3 collective-permute-done.16
  102.4 0.7 collective-permute-start.17
  103.1 2.4 %collective-permute-start.18 = (bf16[128,256]{1,0:T(8,128)(2,1)S(1)}, bf16[128,256]{1,0:T(8,128)(2,1)S(1)}, u32[]{:S(2)}, u32[]{:S(2)}) collective-permute-start(bf16[128,256]{1,0:T(8,128)(2,1)S(1)} %fusion.21), channel_id=1, source_target_pairs={{0,8},{4,12},{8,0},{12,4},{1,9},{5,13},{9,1},{13,5},{2,10},{6,14},... | collective-permute-start | bytes 196616 | tf_op jit(solution)/shard_map/ppermute | solution.py:193
  105.6 1.3 collective-permute-start.19
  106.9 2.6 %collective-permute-start.13 = (bf16[2,256,256]{2,1,0:T(8,128)(2,1)S(1)}, bf16[2,256,256]{2,1,0:T(8,128)(2,1)S(1)}, u32[]{:S(2)}, u32[]{:S(2)}) collective-permute-start(bf16[2,256,256]{2,1,0:T(8,128)(2,1)S(1)} %copy-done.14), channel_id=1, source_target_pairs={{0,12},{4,8},{8,4},{12,0},{1,13},{5,9},{9,5},{13,1},{2,14},{6,10},... | collective-permute-start | bytes 786440 | tf_op jit(solution)/shard_map/ppermute | solution.py:193
  109.5 7.1 %collective-permute-done.18 = bf16[128,256]{1,0:T(8,128)(2,1)S(1)} collective-permute-done((bf16[128,256]{1,0:T(8,128)(2,1)S(1)}, bf16[128,256]{1,0:T(8,128)(2,1)S(1)}, u32[]{:S(2)}, u32[]{:S(2)}) %collective-permute-start.18) | collective-permute-done | bytes 65568 | tf_op jit(solution)/shard_map/ppermute | solution.py:193
  116.6 0.6 gather_fusion
  117.3 0.6 collective-permute-start.20
  117.8 4.1 %collective-permute-start.11 = (bf16[2,256,256]{2,1,0:T(8,128)(2,1)}, bf16[2,256,256]{2,1,0:T(8,128)(2,1)}, u32[]{:S(2)}, u32[]{:S(2)}) collective-permute-start(bf16[2,256,256]{2,1,0:T(8,128)(2,1)} %get-tuple-element.69), channel_id=1, source_target_pairs={{0,4},{4,0},{8,12},{12,8},{1,5},{5,1},{9,13},{13,9},{2,6},{6,2},{1... | collective-permute-start | bytes 786440 | tf_op jit(solution)/shard_map/ppermute | solution.py:193
  122.0 1.1 collective-permute-start.12
  123.0 1.1 pad_maximum_fusion.1
  124.1 0.6 gather_fusion.1
  124.8 0.9 reverse_select_fusion
  125.7 4.9 %collective-permute-done.11 = bf16[2,256,256]{2,1,0:T(8,128)(2,1)} collective-permute-done((bf16[2,256,256]{2,1,0:T(8,128)(2,1)}, bf16[2,256,256]{2,1,0:T(8,128)(2,1)}, u32[]{:S(2)}, u32[]{:S(2)}) %collective-permute-start.11) | collective-permute-done | bytes 262176 | tf_op jit(solution)/shard_map/ppermute | solution.py:193
  130.6 4.2 %collective-permute-done.12 = bf16[2,256,256]{2,1,0:T(8,128)(2,1)} collective-permute-done((bf16[2,256,256]{2,1,0:T(8,128)(2,1)}, bf16[2,256,256]{2,1,0:T(8,128)(2,1)}, u32[]{:S(2)}, u32[]{:S(2)}) %collective-permute-start.12) | collective-permute-done | bytes 262176 | tf_op jit(solution)/shard_map/ppermute | solution.py:193
  134.8 1.2 pad_maximum_fusion.2
  136.0 0.6 gather_fusion.2
  136.8 1.5 %pad_maximum_fusion = (bf16[2,4,1,256,256]{4,3,2,1,0:T(8,128)(2,1)}, bf16[2,4,1,256,256]{4,3,2,1,0:T(8,128)(2,1)}) fusion(bf16[1,4,2,256,256]{4,3,2,1,0:T(8,128)(2,1)S(1)} %get-tuple-element.89, bf16[1,4,2,256,256]{4,3,2,1,0:T(8,128)(2,1)S(1)} %get-tuple-element.90), kind=kLoop, calls=%fused_computation.22 | loop fusion | flops 1048576 | bytes 4194304 | tf_op jit(solution)/shard_map/stack | solution.py:280
  138.3 1.3 select_convert_fusion
  139.7 0.9 slice.32
  140.6 0.8 slice_bitcast_fusion
  141.4 0.9 slice.33
  (67 shorter events, 1.0 us)
Async XLA Ops:
  0.6 8.5 %copy-start.2 = (bf16[3,256,256]{2,1,0:T(8,128)(2,1)S(1)}, bf16[3,256,256]{2,1,0:T(8,128)(2,1)}, u32[]{:S(2)}) copy-start(bf16[3,256,256]{2,1,0:T(8,128)(2,1)} %param.14) | copy-start | bytes 1179652
  0.7 34.6 %copy-start.3 = (bf16[3,256,256]{2,1,0:T(8,128)(2,1)S(1)}, bf16[3,256,256]{2,1,0:T(8,128)(2,1)}, u32[]{:S(2)}) copy-start(bf16[3,256,256]{2,1,0:T(8,128)(2,1)} %param.15) | copy-start | bytes 1179652
  3.3 33.8 %copy-start.4 = (bf16[256,256]{1,0:T(8,128)(2,1)S(1)}, bf16[256,256]{1,0:T(8,128)(2,1)}, u32[]{:S(2)}) copy-start(bf16[256,256]{1,0:T(8,128)(2,1)} %refs_6_.3) | copy-start | bytes 393220
  3.3 34.6 %copy-start.5 = (bf16[256,256]{1,0:T(8,128)(2,1)S(1)}, bf16[256,256]{1,0:T(8,128)(2,1)}, u32[]{:S(2)}) copy-start(bf16[256,256]{1,0:T(8,128)(2,1)} %refs_10_.3) | copy-start | bytes 393220
  3.3 35.9 %copy-start = (bf16[1,2048,256]{2,1,0:T(8,128)(2,1)S(1)}, bf16[1,2048,256]{2,1,0:T(8,128)(2,1)}, u32[]{:S(2)}) copy-start(bf16[1,2048,256]{2,1,0:T(8,128)(2,1)} %param.13) | copy-start | bytes 3145732
  3.3 35.9 %copy-start.1 = (bf16[1,2048,256]{2,1,0:T(8,128)(2,1)S(1)}, bf16[1,2048,256]{2,1,0:T(8,128)(2,1)}, u32[]{:S(2)}) copy-start(bf16[1,2048,256]{2,1,0:T(8,128)(2,1)} %param.12) | copy-start | bytes 3145732
  3.3 12.4 %collective-permute-start.2 = (bf16[2,256,256]{2,1,0:T(8,128)(2,1)S(1)}, bf16[2,256,256]{2,1,0:T(8,128)(2,1)S(1)}, u32[]{:S(2)}, u32[]{:S(2)}) collective-permute-start(bf16[2,256,256]{2,1,0:T(8,128)(2,1)S(1)} %get-tuple-element.82), channel_id=1, source_target_pairs={{0,12},{4,8},{8,4},{12,0},{1,13},{5,9},{9,5},{13,1},{2,14},{6,10},... | collective-permute-start | bytes 786440 | tf_op jit(solution)/shard_map/ppermute | solution.py:193
  8.4 22.3 %collective-permute-start.1 = (bf16[2,256,256]{2,1,0:T(8,128)(2,1)S(1)}, bf16[2,256,256]{2,1,0:T(8,128)(2,1)S(1)}, u32[]{:S(2)}, u32[]{:S(2)}) collective-permute-start(bf16[2,256,256]{2,1,0:T(8,128)(2,1)S(1)} %get-tuple-element.80), channel_id=1, source_target_pairs={{0,8},{4,12},{8,0},{12,4},{1,9},{5,13},{9,1},{13,5},{2,10},{6,14},... | collective-permute-start | bytes 786440 | tf_op jit(solution)/shard_map/ppermute | solution.py:193
  8.5 22.3 %collective-permute-start = (bf16[2,256,256]{2,1,0:T(8,128)(2,1)S(1)}, bf16[2,256,256]{2,1,0:T(8,128)(2,1)S(1)}, u32[]{:S(2)}, u32[]{:S(2)}) collective-permute-start(bf16[2,256,256]{2,1,0:T(8,128)(2,1)S(1)} %get-tuple-element.78), channel_id=1, source_target_pairs={{0,4},{4,0},{8,12},{12,8},{1,5},{5,1},{9,13},{13,9},{2,6},{6,2},{1... | collective-permute-start | bytes 786440 | tf_op jit(solution)/shard_map/ppermute | solution.py:193
  15.7 24.3 %copy-start.11 = (bf16[2,256,256]{2,1,0:T(8,128)(2,1)}, bf16[2,256,256]{2,1,0:T(8,128)(2,1)S(1)}, u32[]{:S(2)}) copy-start(bf16[2,256,256]{2,1,0:T(8,128)(2,1)S(1)} %collective-permute-done.2.refs_3_) | copy-start | bytes 786436
  30.8 2.5 %copy-start.12 = (bf16[2,256,256]{2,1,0:T(8,128)(2,1)}, bf16[2,256,256]{2,1,0:T(8,128)(2,1)S(1)}, u32[]{:S(2)}) copy-start(bf16[2,256,256]{2,1,0:T(8,128)(2,1)S(1)} %collective-permute-done.1.refs_2_) | copy-start | bytes 786436
  30.8 4.5 %copy-start.13 = (bf16[2,256,256]{2,1,0:T(8,128)(2,1)}, bf16[2,256,256]{2,1,0:T(8,128)(2,1)S(1)}, u32[]{:S(2)}) copy-start(bf16[2,256,256]{2,1,0:T(8,128)(2,1)S(1)} %collective-permute-done.refs_1_) | copy-start | bytes 786436
  30.8 24.7 %collective-permute-start.5 = (bf16[2,256,256]{2,1,0:T(8,128)(2,1)}, bf16[2,256,256]{2,1,0:T(8,128)(2,1)}, u32[]{:S(2)}, u32[]{:S(2)}) collective-permute-start(bf16[2,256,256]{2,1,0:T(8,128)(2,1)} %get-tuple-element.50), channel_id=1, source_target_pairs={{0,12},{4,8},{8,4},{12,0},{1,13},{5,9},{9,5},{13,1},{2,14},{6,10},... | collective-permute-start | bytes 786440 | tf_op jit(solution)/shard_map/ppermute | solution.py:193
  33.3 22.2 %collective-permute-start.4 = (bf16[2,256,256]{2,1,0:T(8,128)(2,1)}, bf16[2,256,256]{2,1,0:T(8,128)(2,1)}, u32[]{:S(2)}, u32[]{:S(2)}) collective-permute-start(bf16[2,256,256]{2,1,0:T(8,128)(2,1)} %get-tuple-element.49), channel_id=1, source_target_pairs={{0,8},{4,12},{8,0},{12,4},{1,9},{5,13},{9,1},{13,5},{2,10},{6,14},... | collective-permute-start | bytes 786440 | tf_op jit(solution)/shard_map/ppermute | solution.py:193
  33.3 22.2 %collective-permute-start.3 = (bf16[2,256,256]{2,1,0:T(8,128)(2,1)}, bf16[2,256,256]{2,1,0:T(8,128)(2,1)}, u32[]{:S(2)}, u32[]{:S(2)}) collective-permute-start(bf16[2,256,256]{2,1,0:T(8,128)(2,1)} %get-tuple-element.48), channel_id=1, source_target_pairs={{0,4},{4,0},{8,12},{12,8},{1,5},{5,1},{9,13},{13,9},{2,6},{6,2},{1... | collective-permute-start | bytes 786440 | tf_op jit(solution)/shard_map/ppermute | solution.py:193
  55.5 18.7 %collective-permute-start.8 = (bf16[2,256,256]{2,1,0:T(8,128)(2,1)}, bf16[2,256,256]{2,1,0:T(8,128)(2,1)S(1)}, u32[]{:S(2)}, u32[]{:S(2)}) collective-permute-start(bf16[2,256,256]{2,1,0:T(8,128)(2,1)} %get-tuple-element.54), channel_id=1, source_target_pairs={{0,12},{4,8},{8,4},{12,0},{1,13},{5,9},{9,5},{13,1},{2,14},{6,10},... | collective-permute-start | bytes 786440 | tf_op jit(solution)/shard_map/ppermute | solution.py:193
  74.2 5.2 %copy-start.16 = (bf16[2,256,256]{2,1,0:T(8,128)(2,1)S(1)}, bf16[2,256,256]{2,1,0:T(8,128)(2,1)}, u32[]{:S(2)}) copy-start(bf16[2,256,256]{2,1,0:T(8,128)(2,1)} %get-tuple-element.52) | copy-start | bytes 786436
  74.2 5.2 %copy-start.15 = (bf16[2,256,256]{2,1,0:T(8,128)(2,1)S(1)}, bf16[2,256,256]{2,1,0:T(8,128)(2,1)}, u32[]{:S(2)}) copy-start(bf16[2,256,256]{2,1,0:T(8,128)(2,1)} %get-tuple-element.53) | copy-start | bytes 786436
  74.2 2.2 %collective-permute-start.9 = (bf16[4,256,256]{2,1,0:T(8,128)(2,1)}, bf16[4,256,256]{2,1,0:T(8,128)(2,1)S(1)}, u32[]{:S(2)}, u32[]{:S(2)}) collective-permute-start(bf16[4,256,256]{2,1,0:T(8,128)(2,1)} %get-tuple-element.63), channel_id=1, source_target_pairs={{0,1},{1,0},{2,3},{3,2},{4,5},{5,4},{6,7},{7,6},{8,9},{9,8},{10,11... | collective-permute-start | bytes 1572872 | tf_op jit(solution)/shard_map/ppermute | solution.py:193
  77.7 29.1 %copy-start.14 = (bf16[2,256,256]{2,1,0:T(8,128)(2,1)S(1)}, bf16[2,256,256]{2,1,0:T(8,128)(2,1)}, u32[]{:S(2)}) copy-start(bf16[2,256,256]{2,1,0:T(8,128)(2,1)} %get-tuple-element.71) | copy-start | bytes 786436
  77.8 8.4 %collective-permute-start.10 = (bf16[512,256]{1,0:T(8,128)(2,1)S(1)}, bf16[512,256]{1,0:T(8,128)(2,1)S(1)}, u32[]{:S(2)}, u32[]{:S(2)}) collective-permute-start(bf16[512,256]{1,0:T(8,128)(2,1)S(1)} %fusion.9), channel_id=1, source_target_pairs={{0,2},{2,0},{1,3},{3,1},{4,6},{6,4},{5,7},{7,5},{8,10},{10,8},{9,1... | collective-permute-start | bytes 786440 | tf_op jit(solution)/shard_map/ppermute | solution.py:193
  79.4 12.4 %collective-permute-start.6 = (bf16[2,256,256]{2,1,0:T(8,128)(2,1)S(1)}, bf16[2,256,256]{2,1,0:T(8,128)(2,1)S(1)}, u32[]{:S(2)}, u32[]{:S(2)}) collective-permute-start(bf16[2,256,256]{2,1,0:T(8,128)(2,1)S(1)} %copy-done.16), channel_id=1, source_target_pairs={{0,4},{4,0},{8,12},{12,8},{1,5},{5,1},{9,13},{13,9},{2,6},{6,2},{1... | collective-permute-start | bytes 786440 | tf_op jit(solution)/shard_map/ppermute | solution.py:193
  79.4 14.7 %collective-permute-start.7 = (bf16[2,256,256]{2,1,0:T(8,128)(2,1)S(1)}, bf16[2,256,256]{2,1,0:T(8,128)(2,1)S(1)}, u32[]{:S(2)}, u32[]{:S(2)}) collective-permute-start(bf16[2,256,256]{2,1,0:T(8,128)(2,1)S(1)} %copy-done.15), channel_id=1, source_target_pairs={{0,8},{4,12},{8,0},{12,4},{1,9},{5,13},{9,1},{13,5},{2,10},{6,14},... | collective-permute-start | bytes 786440 | tf_op jit(solution)/shard_map/ppermute | solution.py:193
  81.3 41.7 %copy-start.6 = (bf16[2,256,256]{2,1,0:T(8,128)(2,1)S(1)}, bf16[2,256,256]{2,1,0:T(8,128)(2,1)}, u32[]{:S(2)}) copy-start(bf16[2,256,256]{2,1,0:T(8,128)(2,1)} %get-tuple-element.64) | copy-start | bytes 786436
  94.1 28.9 %copy-start.8 = (bf16[2,256,256]{2,1,0:T(8,128)(2,1)}, bf16[2,256,256]{2,1,0:T(8,128)(2,1)S(1)}, u32[]{:S(2)}) copy-start(bf16[2,256,256]{2,1,0:T(8,128)(2,1)S(1)} %collective-permute-done.7) | copy-start | bytes 786436
  94.1 4.5 %collective-permute-start.14 = (bf16[128,256]{1,0:T(8,128)(2,1)S(1)}, bf16[128,256]{1,0:T(8,128)(2,1)S(1)}, u32[]{:S(2)}, u32[]{:S(2)}) collective-permute-start(bf16[128,256]{1,0:T(8,128)(2,1)S(1)} %get-tuple-element.86), channel_id=1, source_target_pairs={{0,4},{4,0},{8,12},{12,8},{1,5},{5,1},{9,13},{13,9},{2,6},{6,2},{1... | collective-permute-start | bytes 196616 | tf_op jit(solution)/shard_map/ppermute | solution.py:193
  94.2 6.8 %collective-permute-start.15 = (bf16[128,256]{1,0:T(8,128)(2,1)S(1)}, bf16[128,256]{1,0:T(8,128)(2,1)S(1)}, u32[]{:S(2)}, u32[]{:S(2)}) collective-permute-start(bf16[128,256]{1,0:T(8,128)(2,1)S(1)} %get-tuple-element.88), channel_id=1, source_target_pairs={{0,8},{4,12},{8,0},{12,4},{1,9},{5,13},{9,1},{13,5},{2,10},{6,14},... | collective-permute-start | bytes 196616 | tf_op jit(solution)/shard_map/ppermute | solution.py:193
  96.2 6.2 %collective-permute-start.16 = (bf16[128,256]{1,0:T(8,128)(2,1)S(1)}, bf16[128,256]{1,0:T(8,128)(2,1)S(1)}, u32[]{:S(2)}, u32[]{:S(2)}) collective-permute-start(bf16[128,256]{1,0:T(8,128)(2,1)S(1)} %get-tuple-element.87), channel_id=1, source_target_pairs={{0,12},{4,8},{8,4},{12,0},{1,13},{5,9},{9,5},{13,1},{2,14},{6,10},... | collective-permute-start | bytes 196616 | tf_op jit(solution)/shard_map/ppermute | solution.py:193
  102.4 7.1 %collective-permute-start.17 = (bf16[128,256]{1,0:T(8,128)(2,1)S(1)}, bf16[128,256]{1,0:T(8,128)(2,1)S(1)}, u32[]{:S(2)}, u32[]{:S(2)}) collective-permute-start(bf16[128,256]{1,0:T(8,128)(2,1)S(1)} %fusion.21), channel_id=1, source_target_pairs={{0,4},{4,0},{8,12},{12,8},{1,5},{5,1},{9,13},{13,9},{2,6},{6,2},{1... | collective-permute-start | bytes 196616 | tf_op jit(solution)/shard_map/ppermute | solution.py:193
  103.1 13.4 %collective-permute-start.18 = (bf16[128,256]{1,0:T(8,128)(2,1)S(1)}, bf16[128,256]{1,0:T(8,128)(2,1)S(1)}, u32[]{:S(2)}, u32[]{:S(2)}) collective-permute-start(bf16[128,256]{1,0:T(8,128)(2,1)S(1)} %fusion.21), channel_id=1, source_target_pairs={{0,8},{4,12},{8,0},{12,4},{1,9},{5,13},{9,1},{13,5},{2,10},{6,14},... | collective-permute-start | bytes 196616 | tf_op jit(solution)/shard_map/ppermute | solution.py:193
  105.6 11.0 %collective-permute-start.19 = (bf16[128,256]{1,0:T(8,128)(2,1)S(1)}, bf16[128,256]{1,0:T(8,128)(2,1)S(1)}, u32[]{:S(2)}, u32[]{:S(2)}) collective-permute-start(bf16[128,256]{1,0:T(8,128)(2,1)S(1)} %fusion.21), channel_id=1, source_target_pairs={{0,12},{4,8},{8,4},{12,0},{1,13},{5,9},{9,5},{13,1},{2,14},{6,10},... | collective-permute-start | bytes 196616 | tf_op jit(solution)/shard_map/ppermute | solution.py:193
  106.9 10.4 %collective-permute-start.13 = (bf16[2,256,256]{2,1,0:T(8,128)(2,1)S(1)}, bf16[2,256,256]{2,1,0:T(8,128)(2,1)S(1)}, u32[]{:S(2)}, u32[]{:S(2)}) collective-permute-start(bf16[2,256,256]{2,1,0:T(8,128)(2,1)S(1)} %copy-done.14), channel_id=1, source_target_pairs={{0,12},{4,8},{8,4},{12,0},{1,13},{5,9},{9,5},{13,1},{2,14},{6,10},... | collective-permute-start | bytes 786440 | tf_op jit(solution)/shard_map/ppermute | solution.py:193
  117.2 5.8 %copy-start.9 = (bf16[2,256,256]{2,1,0:T(8,128)(2,1)}, bf16[2,256,256]{2,1,0:T(8,128)(2,1)S(1)}, u32[]{:S(2)}) copy-start(bf16[2,256,256]{2,1,0:T(8,128)(2,1)S(1)} %collective-permute-done.13) | copy-start | bytes 786436
  117.3 7.5 %collective-permute-start.20 = (bf16[512,256]{1,0:T(8,128)(2,1)S(1)}, bf16[512,256]{1,0:T(8,128)(2,1)S(1)}, u32[]{:S(2)}, u32[]{:S(2)}) collective-permute-start(bf16[512,256]{1,0:T(8,128)(2,1)S(1)} %bitcast.108), channel_id=1, source_target_pairs={{0,2},{2,0},{1,3},{3,1},{4,6},{6,4},{5,7},{7,5},{8,10},{10,8},{9,1... | collective-permute-start | bytes 786440 | tf_op jit(solution)/shard_map/ppermute | solution.py:193
  117.8 12.7 %collective-permute-start.11 = (bf16[2,256,256]{2,1,0:T(8,128)(2,1)}, bf16[2,256,256]{2,1,0:T(8,128)(2,1)}, u32[]{:S(2)}, u32[]{:S(2)}) collective-permute-start(bf16[2,256,256]{2,1,0:T(8,128)(2,1)} %get-tuple-element.69), channel_id=1, source_target_pairs={{0,4},{4,0},{8,12},{12,8},{1,5},{5,1},{9,13},{13,9},{2,6},{6,2},{1... | collective-permute-start | bytes 786440 | tf_op jit(solution)/shard_map/ppermute | solution.py:193
  122.0 12.8 %collective-permute-start.12 = (bf16[2,256,256]{2,1,0:T(8,128)(2,1)}, bf16[2,256,256]{2,1,0:T(8,128)(2,1)}, u32[]{:S(2)}, u32[]{:S(2)}) collective-permute-start(bf16[2,256,256]{2,1,0:T(8,128)(2,1)} %get-tuple-element.70), channel_id=1, source_target_pairs={{0,8},{4,12},{8,0},{12,4},{1,9},{5,13},{9,1},{13,5},{2,10},{6,14},... | collective-permute-start | bytes 786440 | tf_op jit(solution)/shard_map/ppermute | solution.py:193
  124.1 10.7 %copy-start.7 = (bf16[2,256,256]{2,1,0:T(8,128)(2,1)S(1)}, bf16[2,256,256]{2,1,0:T(8,128)(2,1)}, u32[]{:S(2)}) copy-start(bf16[2,256,256]{2,1,0:T(8,128)(2,1)} %get-tuple-element.68) | copy-start | bytes 786436
  124.8 10.0 %copy-start.10 = (bf16[2,256,256]{2,1,0:T(8,128)(2,1)S(1)}, bf16[2,256,256]{2,1,0:T(8,128)(2,1)}, u32[]{:S(2)}) copy-start(bf16[2,256,256]{2,1,0:T(8,128)(2,1)} %copy-done.9) | copy-start | bytes 786436
  125.7 12.6 %collective-permute-start.21 = (bf16[4,256,256]{2,1,0:T(8,128)(2,1)}, bf16[4,256,256]{2,1,0:T(8,128)(2,1)}, u32[]{:S(2)}, u32[]{:S(2)}) collective-permute-start(bf16[4,256,256]{2,1,0:T(8,128)(2,1)} %bitcast.54), channel_id=1, source_target_pairs={{0,1},{1,0},{2,3},{3,2},{4,5},{5,4},{6,7},{7,6},{8,9},{9,8},{10,11... | collective-permute-start | bytes 1572872 | tf_op jit(solution)/shard_map/ppermute | solution.py:193

commit v3 on v2

v3 whole, which is shorter than its diff:
```python
import functools
import math

import jax
import jax.numpy as jnp
from jax import lax
from jax.experimental import pallas as pl
from jax.experimental.pallas import tpu as pltpu
from jax.sharding import Mesh
from jax.sharding import PartitionSpec as P

HOP1 = 4
HOP2 = 8

GELU_COEF = 0.7978845608028654
CUBIC = 0.044715
CHUNKS = 2
VMEM_LIMIT = 60 << 20
BF16 = jnp.bfloat16
F32 = jnp.float32


def gelu_parts(v):
    square = v * v
    th = jnp.tanh(v * (GELU_COEF + (GELU_COEF * CUBIC) * square))
    half = 0.5 + 0.5 * th
    value = v * half
    slope = half + value * (1.0 - th) * (GELU_COEF + (3.0 * CUBIC * GELU_COEF) * square)
    return value, slope


def inverse_rms(x):
    return lax.rsqrt(jnp.mean(x * x, axis=-1, keepdims=True) + 1e-06)


def dot(left, right):
    return jnp.dot(left, right, preferred_element_type=F32)


def row_dot(left, right):
    return lax.dot_general(left, right, (((0,), (0,)), ((), ())), preferred_element_type=F32)


def conv_at(parts, tile, taps, p, n, hop):
    width = parts.shape[-1]
    low = 0 if p - hop >= 0 else 1
    high = 3 if p + hop < n else 2
    left = jnp.concatenate(
        [parts[pl.ds((p + (k - 1) * hop) * tile, tile), :] for k in range(low, high)], axis=-1
    )
    return dot(left, taps[low * width : high * width, :])


def over_rows(total, body, step=64):
    for start in range(0, total, step):
        body(pl.ds(start, step))


def start_all(copies):
    for copy in copies:
        copy.start()
    return copies


def wait_all(copies):
    for copy in copies:
        copy.wait()


def stage(moves, held, sems):
    into, out = [], []
    for i, (source, target) in enumerate(moves):
        into.append(pltpu.make_async_copy(source, held.at[i], sems.at[0, i]))
        out.append(pltpu.make_async_copy(held.at[i], target, sems.at[1, i]))
    start_all(into)
    for arrival, departure in zip(into, out):
        arrival.wait()
        departure.start()
    wait_all(out)


def pick_kernel(n, chunk, inputs, cotangent, *refs):
    pieces, (held, sems) = refs[:-2], refs[-2:]
    me = lax.axis_index("chain")
    moves = [
        (source.at[chunk * n + (me ^ s)], pieces[s - 1].at[k])
        for s in reversed(range(1, n))
        for k, source in enumerate((inputs, cotangent))
    ]
    stage(moves, held, sems)


def pick(inputs, cotangent, n, chunk):
    _, rows, width = inputs.shape
    piece = jax.ShapeDtypeStruct((2, rows, width), BF16)
    return pl.pallas_call(
        functools.partial(pick_kernel, n, chunk),
        name="pick",
        in_specs=in_place(2),
        out_specs=in_place(n - 1),
        out_shape=[piece] * (n - 1),
        scratch_shapes=[
            pltpu.VMEM((2 * (n - 1), rows, width), BF16),
            pltpu.SemaphoreType.DMA((2, 2 * (n - 1))),
        ],
        cost_estimate=small_cost(),
    )(inputs, cotangent)


def put_kernel(n, chunk, fresh, *refs):
    pieces, refs = refs[:n], refs[n if fresh else n + 2 :]
    outs, (held, sems) = refs[:2], refs[2:]
    me = lax.axis_index("chain")
    moves = [
        (pieces[s].at[k], outs[k].at[chunk * n + (me ^ s)]) for s in range(n) for k in range(2)
    ]
    stage(moves, held, sems)


def put(pieces, chunk, into):
    n, (_, rows, width) = len(pieces), pieces[0].shape
    full = jax.ShapeDtypeStruct((CHUNKS * n, rows, width), BF16)
    return pl.pallas_call(
        functools.partial(put_kernel, n, chunk, into is None),
        name="put",
        in_specs=in_place(n if into is None else n + 2),
        out_specs=in_place(2),
        out_shape=[full, full],
        input_output_aliases={} if into is None else {n: 0, n + 1: 1},
        scratch_shapes=[
            pltpu.VMEM((2 * n, rows, width), BF16),
            pltpu.SemaphoreType.DMA((2, 2 * n)),
        ],
        cost_estimate=pl.CostEstimate(
            flops=0, bytes_accessed=16 * n * rows * width, transcendentals=0
        ),
    )(*pieces, *(into or ()))


def finish_kernel(own, by_pair, by_core, by_both, *refs):
    outs, held, sems = refs[:4], refs[4], refs[5]
    pair, core = lax.axis_index("pair"), lax.axis_index("core")
    places = ((core, pair), (core, 1 - pair), (1 - core, pair), (1 - core, 1 - pair))
    wait_all(
        start_all(
            [
                pltpu.make_async_copy(quarter, held.at[block, half], sems.at[i])
                for i, (quarter, (block, half)) in enumerate(
                    zip((own, by_pair, by_core, by_both), places)
                )
            ]
        )
    )
    for block in range(2):
        taps, project = outs[block], outs[2 + block]
        taps[0] = held[block, 0, 0].astype(F32)
        taps[1] = held[block, 0, 1].astype(F32)
        taps[2] = held[block, 1, 0].astype(F32)
        project[...] = held[block, 1, 1].astype(F32)


def finish(quarters, width):
    quarters = [quarter.reshape(2, width, width) for quarter in quarters]
    taps = jax.ShapeDtypeStruct((3, width, width), F32)
    project = jax.ShapeDtypeStruct((width, width), F32)
    return pl.pallas_call(
        finish_kernel,
        name="finish",
        in_specs=in_place(4),
        out_shape=[taps, taps, project, project],
        scratch_shapes=[
            pltpu.VMEM((2, 2, 2, width, width), BF16),
            pltpu.SemaphoreType.DMA((4,)),
        ],
        compiler_params=pltpu.CompilerParams(vmem_limit_bytes=VMEM_LIMIT),
        cost_estimate=small_cost(),
    )(*quarters)


def in_place(count):
    return [pl.BlockSpec(memory_space=pl.ANY)] * count


def small_cost():
    return pl.CostEstimate(flops=1000, bytes_accessed=1000, transcendentals=0)


def chunk_kernel(n, hops, chunk, last, *refs):
    inputs, cotangent, refs = refs[0], refs[1], refs[2:]
    pieces, weights, late, refs = refs[: n - 1], refs[n - 1 : n + 7], refs[n + 7 : n + 11], refs[n + 11 :]
    if last:
        before, refs = refs[0], refs[1:]
    piece_outs, refs = refs[:n], refs[n:]
    if last:
        keep_out, send_out, sums = refs[:3]
        refs = refs[3:]
    else:
        sums, refs = refs[0], refs[1:]
    sources, grad, wide, hidden_grad, acts, gelleds, norm_slopes, hidden_slopes = refs[:8]
    late_held, sems, late_sems = refs[8:12], refs[12], refs[13]
    me, core = lax.axis_index("chain"), lax.axis_index("core")
    _, rows_in, width = inputs.shape
    tile, total = rows_in, n * rows_in

    def place(s):
        return pl.ds(pl.multiple_of((me ^ s) * tile, tile), tile)

    def arriving(k, held, whole_array):
        copies = []
        for s in range(n):
            source = whole_array.at[chunk * n + me] if s == 0 else pieces[s - 1].at[k]
            copies.append(pltpu.make_async_copy(source, held.at[place(s), :], sems.at[k, s]))
        return start_all(copies)

    def leaving(k, held):
        copies = []
        for s in range(n):
            copies.append(
                pltpu.make_async_copy(
                    held.at[place(s), :], piece_outs[s].at[k], sems.at[2 + k, s]
                )
            )
        return start_all(copies)

    x_copies = arriving(0, sources.at[0], inputs)
    late_copies = start_all(
        [
            pltpu.make_async_copy(source, held, late_sems.at[i])
            for i, (source, held) in enumerate(zip(late, late_held))
        ]
    )
    y_copies = arriving(1, grad, cotangent)
    if last:
        late_copies += start_all([pltpu.make_async_copy(before, sums, late_sems.at[4])])
    wait_all(x_copies)

    for block in range(2):
        taps, bias, project, gain = weights[4 * block : 4 * block + 4]
        gain_row, bias_row = gain[...], bias[...]

        def before_conv(rows):
            x = sources[block, rows, :].astype(F32)
            value, slope = gelu_parts(x * inverse_rms(x) * gain_row)
            acts[block, rows, :] = value.astype(BF16)
            norm_slopes[block, rows, :] = slope * gain_row

        over_rows(total, before_conv)
        for p in range(n):
            wide[pl.ds(p * tile, tile), :] = conv_at(
                acts.at[block], tile, taps, p, n, hops[block]
            )

        def after_conv(rows):
            value, slope = gelu_parts(wide[rows, :] + bias_row)
            gelleds[block, rows, :] = value.astype(BF16)
            hidden_slopes[block, rows, :] = slope

        over_rows(total, after_conv)
        sources[block + 1] = (
            sources[block].astype(F32) + dot(gelleds[block], project[...])
        ).astype(BF16)

    out_copies = leaving(0, sources.at[2])
    wait_all(y_copies + late_copies)

    def add(k, value):
        sums[k] = sums[k] + value if last else value

    for block in (1, 0):
        taps_t, project_t = late_held[2 * block : 2 * block + 2]
        hop = hops[block]
        cut = hop * tile
        add(4 * block + 3, row_dot(gelleds[block], grad[...]))
        wide[...] = dot(grad[...], project_t[...])

        def hidden_rows(rows):
            hidden_grad[rows, :] = (wide[rows, :] * hidden_slopes[block, rows, :]).astype(BF16)

        over_rows(total, hidden_rows)
        add(4 * block, row_dot(acts[block, : total - cut, :], hidden_grad[cut:, :]))
        add(4 * block + 1, row_dot(acts[block], hidden_grad[...]))
        add(4 * block + 2, row_dot(acts[block, cut:, :], hidden_grad[: total - cut, :]))
        for p in range(n):
            wide[pl.ds(p * tile, tile), :] = conv_at(hidden_grad, tile, taps_t, p, n, hop)

        def source_rows(rows):
            weighted = wide[rows, :] * norm_slopes[block, rows, :]
            x = sources[block, rows, :].astype(F32)
            inv = inverse_rms(x)
            unit = x * inv
            mean = jnp.mean(unit * weighted, axis=-1, keepdims=True)
            grad[rows, :] = (
                grad[rows, :].astype(F32) + inv * (weighted - unit * mean)
            ).astype(BF16)

        over_rows(total, source_rows)

    out_copies += leaving(1, grad)
    if last:
        keep_out[...] = sums[pl.ds(4 * core, 4)]
        send_out[...] = sums[pl.ds(4 * (1 - core), 4)].astype(BF16)
    wait_all(out_copies)


def run_chunk(inputs, cotangent, pieces, weights, late, before, hops, chunk):
    n, (_, rows, width) = len(pieces) + 1, pieces[0].shape
    last = before is not None
    total = n * rows
    full = jax.ShapeDtypeStruct((8, width, width), F32)
    half = (4, width, width)
    sums = [jax.ShapeDtypeStruct(half, F32), jax.ShapeDtypeStruct(half, BF16)] if last else [full]
    operands = [inputs, cotangent, *pieces, *weights, *late] + ([before] if last else [])
    scratch = [pltpu.VMEM(full.shape, F32)] if last else []
    outs = pl.pallas_call(
        functools.partial(chunk_kernel, n, hops, chunk, last),
        name="chunk",
        in_specs=in_place(n + 1)
        + [pl.BlockSpec(weight.shape, None) for weight in weights]
        + in_place(5 if last else 4),
        out_specs=in_place(n) + [pl.BlockSpec(kind.shape, None) for kind in sums],
        out_shape=[jax.ShapeDtypeStruct(pieces[0].shape, BF16)] * n + sums,
        scratch_shapes=scratch
        + [
            pltpu.VMEM((3, total, width), BF16),
            pltpu.VMEM((total, width), BF16),
            pltpu.VMEM((total, width), F32),
            pltpu.VMEM((total, width), BF16),
            pltpu.VMEM((2, total, width), BF16),
            pltpu.VMEM((2, total, width), BF16),
            pltpu.VMEM((2, total, width), F32),
            pltpu.VMEM((2, total, width), F32),
        ]
        + [pltpu.VMEM(weight.shape, BF16) for weight in late]
        + [pltpu.SemaphoreType.DMA((4, n)), pltpu.SemaphoreType.DMA((5,))],
        compiler_params=pltpu.CompilerParams(vmem_limit_bytes=VMEM_LIMIT),
        cost_estimate=small_cost(),
    )(*operands)
    return list(outs[:n]), list(outs[n:])


def take(array, index):
    return lax.dynamic_index_in_dim(array, index, 0, keepdims=False)


def swap(values, axis, s=1):
    return lax.ppermute(values, axis, [(i, i ^ s) for i in range(lax.axis_size(axis))])


def spread(array, me):
    n = array.shape[0]
    return [swap(take(array, me ^ s), "chain", s) for s in range(1, n)]


def assemble(pieces, me):
    out = jnp.stack(pieces)
    return jnp.take(out, me ^ jnp.arange(len(pieces)), axis=0)


def on_device(
    inputs,
    cotangent,
    taps_first,
    taps_second,
    bias_first,
    bias_second,
    proj_first,
    proj_second,
    gain_first,
    gain_second,
):
    n = lax.axis_size("chain")
    place, pair = lax.axis_index("chain"), lax.axis_index("pair")
    hops = (1, HOP2 // HOP1)
    shape = inputs.shape
    width = shape[-1]
    weight_scale = 1.0 / math.sqrt(shape[0] * shape[1] * n * HOP1)
    rows = shape[0] * shape[1] // (CHUNKS * n)
    inputs = inputs.reshape(CHUNKS * n, rows, width)
    cotangent = cotangent.reshape(CHUNKS * n, rows, width)
    flat = (3 * width, width)
    weights = (
        taps_first.reshape(flat), bias_first[None], proj_first, gain_first[None],
        taps_second.reshape(flat), bias_second[None], proj_second, gain_second[None],
    )
    late = (
        taps_first[::-1].transpose(0, 2, 1).reshape(flat), proj_first.T,
        taps_second[::-1].transpose(0, 2, 1).reshape(flat), proj_second.T,
    )

    third = max(1, (n - 1) // 3)
    far, middle, near = (
        range(n - third, n), range(n - 2 * third, n - third), range(1, n - 2 * third)
    )
    order = [s for part in (far, middle, near) for s in reversed(part)]

    picked = [pick(inputs, cotangent, n, chunk) for chunk in range(CHUNKS)]
    first = {s: swap(picked[0][s - 1], "chain", s) for s in order}
    second = {}
    for s in order:
        block = picked[1][s - 1]
        if s in middle:
            partner = s + third
            first[partner], block = lax.optimization_barrier((first[partner], block))
        second[s] = swap(block, "chain", s)
    first = [first[s] for s in range(1, n)]
    second = [second[s] for s in range(1, n)]

    def tie(pieces, part, value):
        held = [pieces[s] for s in part]
        held, value = lax.optimization_barrier((held, value))
        for s, piece in zip(part, held):
            pieces[s] = piece
        return value

    def send_back(pieces):
        return pieces[:1] + [swap(pieces[s], "chain", s) for s in range(1, n)]

    pieces, before = run_chunk(inputs, cotangent, first, weights, late, None, hops, 0)
    pieces, second = lax.optimization_barrier((pieces, second))
    results_a = send_back(pieces)
    pieces, (keep, send) = run_chunk(
        inputs, cotangent, second, weights, late, before[0], hops, 1
    )
    results_b = send_back(pieces)

    send = tie(results_a, far, send)
    got = jnp.concatenate([swap(part, "core") for part in jnp.split(send.reshape(4 * width, width), 1)])
    got = got.reshape(keep.shape)
    half = (keep + got).reshape(2, 2 * width, width)
    parts = jnp.split(take(half, 1 - pair).astype(BF16), 4)
    got = jnp.concatenate([swap(part, "pair") for part in parts])
    quarter = (take(half, pair) + got).reshape(n, 2 * width // n, width)
    quarter = tie(results_a, middle, quarter)
    got = spread(quarter.astype(BF16), place)
    total = take(quarter, place)
    for part in got:
        total = total + part
    total = (total * weight_scale).astype(BF16)
    total = tie(results_b, far, total)
    total = tie(results_a, near, total)
    own = assemble([total] + [swap(total, "chain", s) for s in range(1, n)], place)
    own = own.reshape(2 * width, width)
    by_pair, by_core = swap(own, "pair"), swap(own, "core")
    partial = put(results_a, 0, None)
    partial, by_pair = lax.optimization_barrier((partial, by_pair))
    by_pair = tie(results_b, middle, by_pair)
    by_pair = tie(results_b, near, by_pair)
    by_both = swap(by_pair, "core")
    sums = finish((own, by_pair, by_core, by_both), width)
    outputs, input_grad = put(results_b, 1, partial)
    return (outputs.reshape(shape), input_grad.reshape(shape), *sums)


def solution(mesh):
    groups, seq = mesh.shape["groups"], mesh.shape["seq"]
    own = Mesh(
        mesh.devices.reshape(groups, seq // HOP1, HOP1 // 2, 2),
        ("groups", "chain", "pair", "core"),
    )
    split = P("groups", ("chain", "pair", "core"), None)
    return jax.shard_map(
        on_device,
        mesh=own,
        in_specs=(split, split) + (P(),) * 8,
        out_specs=(
            split,
            split,
            P("groups", None, None),
            P("groups", None, None),
            P("groups", None),
            P("groups", None),
        ),
        check_vma=False,
    )
```

time: 143 us -> 129 us (0.902)
  other arithmetic: 11.9 us -> 2.58 us
  waiting for transfers between devices: 56.3 us -> 49.7 us
  starting transfers between devices: 33.6 us -> 37.8 us
  local copies, waits for them, and re-layouts: 8.05 us -> 5.83 us
    ppermute x22 -> x26, waiting for transfers between devices: 56.3 us -> 49.7 us  [swap(): lax.ppermute(values, axis, [(i, i ^ s) for i in range(lax.axis_size(axis))])]
    ppermute x22 -> x26, starting transfers between devices: 33.6 us -> 37.8 us  [swap(): lax.ppermute(values, axis, [(i, i ^ s) for i in range(lax.axis_size(axis))])]
    reshape x2 -> x0, other arithmetic: 3.37 us -> none  [block_of(): lax.dynamic_slice(both, start, (2, 1, 1, rows, width))]
    another operation x4 -> x0, other arithmetic: 2.42 us -> none  [the longest x2 1.76 us: on_device(): outputs = jnp.stack([assemble(pieces, place) for pieces in results])]
    another operation x3 -> x1, other arithmetic: 2.28 us -> 0.04 us  [assemble(): out = jnp.stack(pieces)]
    slice x2 -> x0, local copies, waits for them, and re-layouts: 1.86 us -> none  [the longest x1 0.93 us: on_device(): first[:3]]
    unnamed x36 -> x52, local copies, waits for them, and re-layouts: 1.62 us -> 3.18 us
    pallas_call x2 -> x7, Pallas kernels: 31.6 us -> 31.7 us  [the longest x2 21 us: run_chunk(): pl.pallas_call(functools.partial(chunk_kernel, n, hops, chunk, last), nam...]
  transfers between devices with their start and end apart: 22 -> 26, of which waited for: 11 -> 15; matrix products, arithmetic and copies ran while one was open for 8% -> 5% of each run, Pallas kernels for 22% -> 21%
where the time goes in v3:
time: 129 us
  waiting for transfers between devices  49.7 us (39%)
  starting transfers between devices  37.8 us (29%)
  Pallas kernels  31.7 us (25%)
  local copies, waits for them, and re-layouts  5.83 us (5%)
  other arithmetic  2.58 us (2%)
    ppermute x26, waiting for transfers between devices, swap(): lax.ppermute(values, axis, [(i, i ^ s) for i in range(lax.axis_size(axis))])  49.7 us
    ppermute x26, starting transfers between devices, swap(): lax.ppermute(values, axis, [(i, i ^ s) for i in range(lax.axis_size(axis))])  37.8 us
    pallas_call x2, Pallas kernels, run_chunk(): pl.pallas_call(functools.partial(chunk_kernel, n, hops, chunk, last), nam...  21 us
    pallas_call x2, Pallas kernels, put(): pl.pallas_call(functools.partial(put_kernel, n, chunk, into is None), nam...  4.18 us
    pallas_call x2, Pallas kernels, pick(): pl.pallas_call(functools.partial(pick_kernel, n, chunk), name='pick', in_...  3.98 us
    unnamed x52, local copies, waits for them, and re-layouts  3.18 us
  transfers between devices with their start and end apart: 26, of which 15 were waited for; matrix products, arithmetic and copies ran while one was open for 5% of the time, Pallas kernels for 21%

profile of v3, /device:TPU:0, one launch (start us, length us, event | category | flops | bytes accessed | tf_op | source)
XLA Modules:
  0.0 128.8 jit_solution(7140259355348315602)
XLA Ops:
  0.6 2.0 %pick.2 = (bf16[2,256,256]{2,1,0:T(8,128)(2,1)}, bf16[2,256,256]{2,1,0:T(8,128)(2,1)}, bf16[2,256,256]{2,1,0:T(8,128)(2,1)}) custom-call(bf16[8,256,256]{2,1,0:T(8,128)(2,1)} %bitcast.70, bf16[8,256,256]{2,1,0:T(8,128)(2,1)} %bitcast.74), custom_call_target="tpu_custom_call" | custom-call | flops 1000 | bytes 1000 | tf_op jit(solution)/shard_map/pick/pallas_call | solution.py:96
  2.7 5.1 %collective-permute-start.2 = (bf16[2,256,256]{2,1,0:T(8,128)(2,1)}, bf16[2,256,256]{2,1,0:T(8,128)(2,1)S(1)}, u32[]{:S(2)}, u32[]{:S(2)}) collective-permute-start(bf16[2,256,256]{2,1,0:T(8,128)(2,1)} %get-tuple-element.57), channel_id=1, source_target_pairs={{0,12},{4,8},{8,4},{12,0},{1,13},{5,9},{9,5},{13,1},{2,14},{6,10},... | collective-permute-start | bytes 786440 | tf_op jit(solution)/shard_map/ppermute | solution.py:346
  7.8 0.6 collective-permute-start.1
  8.4 2.0 %pick.3 = (bf16[2,256,256]{2,1,0:T(8,128)(2,1)}, bf16[2,256,256]{2,1,0:T(8,128)(2,1)}, bf16[2,256,256]{2,1,0:T(8,128)(2,1)}) custom-call(bf16[8,256,256]{2,1,0:T(8,128)(2,1)} %bitcast.71, bf16[8,256,256]{2,1,0:T(8,128)(2,1)} %bitcast.75), custom_call_target="tpu_custom_call" | custom-call | flops 1000 | bytes 1000 | tf_op jit(solution)/shard_map/pick/pallas_call | solution.py:96
  10.4 1.5 %collective-permute-start.3 = (bf16[2,256,256]{2,1,0:T(8,128)(2,1)}, bf16[2,256,256]{2,1,0:T(8,128)(2,1)S(1)}, u32[]{:S(2)}, u32[]{:S(2)}) collective-permute-start(bf16[2,256,256]{2,1,0:T(8,128)(2,1)} %get-tuple-element.64), channel_id=1, source_target_pairs={{0,4},{4,0},{8,12},{12,8},{1,5},{5,1},{9,13},{13,9},{2,6},{6,2},{1... | collective-permute-start | bytes 786440 | tf_op jit(solution)/shard_map/ppermute | solution.py:346
  11.9 2.4 %collective-permute-start.5 = (bf16[2,256,256]{2,1,0:T(8,128)(2,1)}, bf16[2,256,256]{2,1,0:T(8,128)(2,1)S(1)}, u32[]{:S(2)}, u32[]{:S(2)}) collective-permute-start(bf16[2,256,256]{2,1,0:T(8,128)(2,1)} %get-tuple-element.66), channel_id=1, source_target_pairs={{0,12},{4,8},{8,4},{12,0},{1,13},{5,9},{9,5},{13,1},{2,14},{6,10},... | collective-permute-start | bytes 786440 | tf_op jit(solution)/shard_map/ppermute | solution.py:346
  14.3 0.9 collective-permute-done.2.refs_4_
  15.2 6.9 %collective-permute-start.4 = (bf16[2,256,256]{2,1,0:T(8,128)(2,1)}, bf16[2,256,256]{2,1,0:T(8,128)(2,1)S(1)}, u32[]{:S(2)}, u32[]{:S(2)}) collective-permute-start(bf16[2,256,256]{2,1,0:T(8,128)(2,1)} %get-tuple-element.65), channel_id=1, source_target_pairs={{0,8},{4,12},{8,0},{12,4},{1,9},{5,13},{9,1},{13,5},{2,10},{6,14},... | collective-permute-start | bytes 786440 | tf_op jit(solution)/shard_map/ppermute | solution.py:346
  22.1 0.9 copy.20
  23.1 0.9 copy.18
  24.0 0.8 copy.19
  24.8 0.8 copy.21
  25.5 6.6 %collective-permute-done.1.refs_3_ = bf16[2,256,256]{2,1,0:T(8,128)(2,1)S(1)} collective-permute-done((bf16[2,256,256]{2,1,0:T(8,128)(2,1)}, bf16[2,256,256]{2,1,0:T(8,128)(2,1)S(1)}, u32[]{:S(2)}, u32[]{:S(2)}) %collective-permute-start.1) | collective-permute-done | bytes 262176 | tf_op jit(solution)/shard_map/ppermute | solution.py:346
  32.2 0.7 copy-done.11
  32.9 10.2 %chunk.2 = (bf16[2,256,256]{2,1,0:T(8,128)(2,1)}, bf16[2,256,256]{2,1,0:T(8,128)(2,1)}, bf16[2,256,256]{2,1,0:T(8,128)(2,1)}, bf16[2,256,256]{2,1,0:T(8,128)(2,1)}, f32[8,256,256]{2,1,0:T(8,128)}) custom-call(bf16[8,256,256]{2,1,0:T(8,128)(2,1)} %bitcast.72, bf16[8,256,256]{2,1,0:T(8,128)(2,1)} %bitcast.76, bf16[2,256,256]{2,1,0:T(8,128)(2,1)} %copy-done.9, ...), custom_call_target="tpu_custom_call" | custom-call | flops 1000 | bytes 1000 | tf_op jit(solution)/shard_map/chunk/pallas_call | solution.py:314
  43.1 9.7 %collective-permute-done.4.refs_3_ = bf16[2,256,256]{2,1,0:T(8,128)(2,1)S(1)} collective-permute-done((bf16[2,256,256]{2,1,0:T(8,128)(2,1)}, bf16[2,256,256]{2,1,0:T(8,128)(2,1)S(1)}, u32[]{:S(2)}, u32[]{:S(2)}) %collective-permute-start.4) | collective-permute-done | bytes 262176 | tf_op jit(solution)/shard_map/ppermute | solution.py:346
  52.8 2.5 %collective-permute-start.11 = (bf16[2,256,256]{2,1,0:T(8,128)(2,1)}, bf16[2,256,256]{2,1,0:T(8,128)(2,1)S(1)}, u32[]{:S(2)}, u32[]{:S(2)}) collective-permute-start(bf16[2,256,256]{2,1,0:T(8,128)(2,1)} %get-tuple-element.79), channel_id=1, source_target_pairs={{0,12},{4,8},{8,4},{12,0},{1,13},{5,9},{9,5},{13,1},{2,14},{6,10},... | collective-permute-start | bytes 786440 | tf_op jit(solution)/shard_map/ppermute | solution.py:346
  55.3 10.8 %chunk.3 = (bf16[2,256,256]{2,1,0:T(8,128)(2,1)}, bf16[2,256,256]{2,1,0:T(8,128)(2,1)}, bf16[2,256,256]{2,1,0:T(8,128)(2,1)}, bf16[2,256,256]{2,1,0:T(8,128)(2,1...) custom-call(bf16[8,256,256]{2,1,0:T(8,128)(2,1)} %bitcast.73, bf16[8,256,256]{2,1,0:T(8,128)(2,1)} %bitcast.77, ...), custom_call_target="tpu_custom_call" | custom-call | flops 1000 | bytes 1000 | tf_op jit(solution)/shard_map/chunk/pallas_call | solution.py:314
  66.3 2.0 %collective-permute-done.12 = bf16[1024,256]{1,0:T(8,128)(2,1)S(1)} collective-permute-done((bf16[1024,256]{1,0:T(8,128)(2,1)}, bf16[1024,256]{1,0:T(8,128)(2,1)S(1)}, u32[]{:S(2)}, u32[]{:S(2)}) %collective-permute-start.12) | collective-permute-done | bytes 524320 | tf_op jit(solution)/shard_map/ppermute | solution.py:346
  68.3 1.4 %convert_add_fusion = f32[4,256,256]{2,1,0:T(8,128)S(1)} fusion(f32[4,256,256]{2,1,0:T(8,128)} %get-tuple-element.78, bf16[4,256,256]{2,1,0:T(8,128)(2,1)S(1)} %bitcast.97), kind=kLoop, calls=%fused_computation.1 | loop fusion | flops 524288 | bytes 2621440 | tf_op jit(solution)/shard_map/add | solution.py:429
  69.8 1.6 %collective-permute-start.13 = (bf16[128,256]{1,0:T(8,128)(2,1)S(1)}, bf16[128,256]{1,0:T(8,128)(2,1)S(1)}, u32[]{:S(2)}, u32[]{:S(2)}) collective-permute-start(bf16[128,256]{1,0:T(8,128)(2,1)S(1)} %get-tuple-element.107), channel_id=1, source_target_pairs={{0,2},{2,0},{1,3},{3,1},{4,6},{6,4},{5,7},{7,5},{8,10},{10,8},{9,1... | collective-permute-start | bytes 196616 | tf_op jit(solution)/shard_map/ppermute | solution.py:346
  71.4 0.5 collective-permute-start.14
  71.9 1.5 %collective-permute-start.15 = (bf16[128,256]{1,0:T(8,128)(2,1)S(1)}, bf16[128,256]{1,0:T(8,128)(2,1)S(1)}, u32[]{:S(2)}, u32[]{:S(2)}) collective-permute-start(bf16[128,256]{1,0:T(8,128)(2,1)S(1)} %get-tuple-element.109), channel_id=1, source_target_pairs={{0,2},{2,0},{1,3},{3,1},{4,6},{6,4},{5,7},{7,5},{8,10},{10,8},{9,1... | collective-permute-start | bytes 196616 | tf_op jit(solution)/shard_map/ppermute | solution.py:346
  73.4 0.5 collective-permute-start.16
  74.0 0.5 collective-permute-done.13
  74.5 1.3 %collective-permute-start.9 = (bf16[2,256,256]{2,1,0:T(8,128)(2,1)S(1)}, bf16[2,256,256]{2,1,0:T(8,128)(2,1)S(1)}, u32[]{:S(2)}, u32[]{:S(2)}) collective-permute-start(bf16[2,256,256]{2,1,0:T(8,128)(2,1)S(1)} %copy-done.22), channel_id=1, source_target_pairs={{0,12},{4,8},{8,4},{12,0},{1,13},{5,9},{9,5},{13,1},{2,14},{6,10},... | collective-permute-start | bytes 786440 | tf_op jit(solution)/shard_map/ppermute | solution.py:346
  75.8 0.5 collective-permute-done.14
  76.4 1.2 collective-permute-done.15
  77.6 0.7 collective-permute-done.16
  78.4 7.7 %collective-permute-done.10.refs_2_ = bf16[2,256,256]{2,1,0:T(8,128)(2,1)S(1)} collective-permute-done((bf16[2,256,256]{2,1,0:T(8,128)(2,1)S(1)}, bf16[2,256,256]{2,1,0:T(8,128)(2,1)S(1)}, u32[]{:S(2)}, u32[]{:S(2)}) %collective-permute-start.10) | collective-permute-done | bytes 262176 | tf_op jit(solution)/shard_map/ppermute | solution.py:346
  86.2 2.9 %collective-permute-start.18 = (bf16[128,256]{1,0:T(8,128)(2,1)S(1)}, bf16[128,256]{1,0:T(8,128)(2,1)S(1)}, u32[]{:S(2)}, u32[]{:S(2)}) collective-permute-start(bf16[128,256]{1,0:T(8,128)(2,1)S(1)} %get-tuple-element.106), channel_id=1, source_target_pairs={{0,8},{4,12},{8,0},{12,4},{1,9},{5,13},{9,1},{13,5},{2,10},{6,14},... | collective-permute-start | bytes 196616 | tf_op jit(solution)/shard_map/ppermute | solution.py:346
  89.1 1.5 %collective-permute-start.19 = (bf16[128,256]{1,0:T(8,128)(2,1)S(1)}, bf16[128,256]{1,0:T(8,128)(2,1)S(1)}, u32[]{:S(2)}, u32[]{:S(2)}) collective-permute-start(bf16[128,256]{1,0:T(8,128)(2,1)S(1)} %get-tuple-element.105), channel_id=1, source_target_pairs={{0,12},{4,8},{8,4},{12,0},{1,13},{5,9},{9,5},{13,1},{2,14},{6,10},... | collective-permute-start | bytes 196616 | tf_op jit(solution)/shard_map/ppermute | solution.py:346
  90.6 2.4 %collective-permute-done.17 = bf16[128,256]{1,0:T(8,128)(2,1)S(1)} collective-permute-done((bf16[128,256]{1,0:T(8,128)(2,1)S(1)}, bf16[128,256]{1,0:T(8,128)(2,1)S(1)}, u32[]{:S(2)}, u32[]{:S(2)}) %collective-permute-start.17) | collective-permute-done | bytes 65568 | tf_op jit(solution)/shard_map/ppermute | solution.py:346
  93.0 2.9 %collective-permute-done.18 = bf16[128,256]{1,0:T(8,128)(2,1)S(1)} collective-permute-done((bf16[128,256]{1,0:T(8,128)(2,1)S(1)}, bf16[128,256]{1,0:T(8,128)(2,1)S(1)}, u32[]{:S(2)}, u32[]{:S(2)}) %collective-permute-start.18) | collective-permute-done | bytes 65568 | tf_op jit(solution)/shard_map/ppermute | solution.py:346
  96.0 2.0 %collective-permute-start.20 = (bf16[128,256]{1,0:T(8,128)(2,1)S(1)}, bf16[128,256]{1,0:T(8,128)(2,1)S(1)}, u32[]{:S(2)}, u32[]{:S(2)}) collective-permute-start(bf16[128,256]{1,0:T(8,128)(2,1)S(1)} %fusion.3), channel_id=1, source_target_pairs={{0,4},{4,0},{8,12},{12,8},{1,5},{5,1},{9,13},{13,9},{2,6},{6,2},{1... | collective-permute-start | bytes 196616 | tf_op jit(solution)/shard_map/ppermute | solution.py:346
  98.0 1.0 collective-permute-start.21
  98.9 1.5 %collective-permute-start.22 = (bf16[128,256]{1,0:T(8,128)(2,1)S(1)}, bf16[128,256]{1,0:T(8,128)(2,1)S(1)}, u32[]{:S(2)}, u32[]{:S(2)}) collective-permute-start(bf16[128,256]{1,0:T(8,128)(2,1)S(1)} %fusion.3), channel_id=1, source_target_pairs={{0,12},{4,8},{8,4},{12,0},{1,13},{5,9},{9,5},{13,1},{2,14},{6,10},... | collective-permute-start | bytes 196616 | tf_op jit(solution)/shard_map/ppermute | solution.py:346
  100.5 5.7 %collective-permute-done.21 = bf16[128,256]{1,0:T(8,128)(2,1)S(1)} collective-permute-done((bf16[128,256]{1,0:T(8,128)(2,1)S(1)}, bf16[128,256]{1,0:T(8,128)(2,1)S(1)}, u32[]{:S(2)}, u32[]{:S(2)}) %collective-permute-start.21) | collective-permute-done | bytes 65568 | tf_op jit(solution)/shard_map/ppermute | solution.py:346
  106.2 0.6 gather_fusion
  106.9 1.6 %collective-permute-start.23 = (bf16[512,256]{1,0:T(8,128)(2,1)S(1)}, bf16[512,256]{1,0:T(8,128)(2,1)S(1)}, u32[]{:S(2)}, u32[]{:S(2)}) collective-permute-start(bf16[512,256]{1,0:T(8,128)(2,1)S(1)} %bitcast_select_fusion.1), channel_id=1, source_target_pairs={{0,2},{2,0},{1,3},{3,1},{4,6},{6,4},{5,7},{7,5},{8,10},{10,8},{9,1... | collective-permute-start | bytes 786440 | tf_op jit(solution)/shard_map/ppermute | solution.py:346
  108.5 2.0 %collective-permute-start.7 = (bf16[2,256,256]{2,1,0:T(8,128)(2,1)S(1)}, bf16[2,256,256]{2,1,0:T(8,128)(2,1)S(1)}, u32[]{:S(2)}, u32[]{:S(2)}) collective-permute-start(bf16[2,256,256]{2,1,0:T(8,128)(2,1)S(1)} %copy-done.20), channel_id=1, source_target_pairs={{0,8},{4,12},{8,0},{12,4},{1,9},{5,13},{9,1},{13,5},{2,10},{6,14},... | collective-permute-start | bytes 786440 | tf_op jit(solution)/shard_map/ppermute | solution.py:346
  110.5 0.7 collective-permute-start.6
  111.3 2.1 %put.2 = (bf16[8,256,256]{2,1,0:T(8,128)(2,1)}, bf16[8,256,256]{2,1,0:T(8,128)(2,1)}) custom-call(bf16[2,256,256]{2,1,0:T(8,128)(2,1)} %get-tuple-element.74.refs_0_, bf16[2,256,256]{2,1,0:T(8,128)(2,1)} %copy-done.15, bf16[2,256,256]{2,1,0:T(8,128)(2,1)} %copy-done.14, bf16[2,256,256]{2,1,0:T(8,128)(2,1)} %copy-done.13), custom_call_target="tpu_custom_call" | custom-call | bytes 4194304 | tf_op jit(solution)/shard_map/put/pallas_call | solution.py:123
  113.7 8.3 %collective-permute-done.7.refs_2_ = bf16[2,256,256]{2,1,0:T(8,128)(2,1)S(1)} collective-permute-done((bf16[2,256,256]{2,1,0:T(8,128)(2,1)S(1)}, bf16[2,256,256]{2,1,0:T(8,128)(2,1)S(1)}, u32[]{:S(2)}, u32[]{:S(2)}) %collective-permute-start.7) | collective-permute-done | bytes 262176 | tf_op jit(solution)/shard_map/ppermute | solution.py:346
  122.3 0.8 bitcast_select_fusion.own
  123.2 2.1 %put.3 = (bf16[8,256,256]{2,1,0:T(8,128)(2,1)}, bf16[8,256,256]{2,1,0:T(8,128)(2,1)}) custom-call(bf16[2,256,256]{2,1,0:T(8,128)(2,1)} %get-tuple-element.71.refs_0_, bf16[2,256,256]{2,1,0:T(8,128)(2,1)} %copy-done.12, bf16[2,256,256]{2,1,0:T(8,128)(2,1)} %copy-done.10, ...), custom_call_target="tpu_custom_call", output_to_operand_aliasing={{0}: (4, {}), {1}: (5, {})} | custom-call | bytes 4194304 | tf_op jit(solution)/shard_map/put/pallas_call | solution.py:123
  125.3 0.7 copy-done.17
  126.1 2.6 %finish.1 = (f32[3,256,256]{2,1,0:T(8,128)}, f32[3,256,256]{2,1,0:T(8,128)}, f32[256,256]{1,0:T(8,128)}, f32[256,256]{1,0:T(8,128)}) custom-call(bf16[2,256,256]{2,1,0:T(8,128)(2,1)} %bitcast_select_fusion.own, bf16[2,256,256]{2,1,0:T(8,128)(2,1)} %bitcast.98, bf16[2,256,256]{2,1,0:T(8,128)(2,1)} %bitcast.99, bf16[2,256,256]{2,1,0:T(8,128)(2,1)} %bitcast.100), custom_call_target="tpu_custom_call" | custom-call | flops 1000 | bytes 1000 | tf_op jit(solution)/shard_map/finish/pallas_call | solution.py:166
  (85 shorter events, 1.7 us)
Async XLA Ops:
  0.6 21.5 %copy-start.1 = (bf16[3,256,256]{2,1,0:T(8,128)(2,1)S(1)}, bf16[3,256,256]{2,1,0:T(8,128)(2,1)}, u32[]{:S(2)}) copy-start(bf16[3,256,256]{2,1,0:T(8,128)(2,1)} %param.13) | copy-start | bytes 1179652
  2.7 20.4 %copy-start = (bf16[3,256,256]{2,1,0:T(8,128)(2,1)S(1)}, bf16[3,256,256]{2,1,0:T(8,128)(2,1)}, u32[]{:S(2)}) copy-start(bf16[3,256,256]{2,1,0:T(8,128)(2,1)} %param.12) | copy-start | bytes 1179652
  2.7 12.5 %collective-permute-start.2 = (bf16[2,256,256]{2,1,0:T(8,128)(2,1)}, bf16[2,256,256]{2,1,0:T(8,128)(2,1)S(1)}, u32[]{:S(2)}, u32[]{:S(2)}) collective-permute-start(bf16[2,256,256]{2,1,0:T(8,128)(2,1)} %get-tuple-element.57), channel_id=1, source_target_pairs={{0,12},{4,8},{8,4},{12,0},{1,13},{5,9},{9,5},{13,1},{2,14},{6,10},... | collective-permute-start | bytes 786440 | tf_op jit(solution)/shard_map/ppermute | solution.py:346
  7.8 17.7 %collective-permute-start = (bf16[2,256,256]{2,1,0:T(8,128)(2,1)}, bf16[2,256,256]{2,1,0:T(8,128)(2,1)S(1)}, u32[]{:S(2)}, u32[]{:S(2)}) collective-permute-start(bf16[2,256,256]{2,1,0:T(8,128)(2,1)} %get-tuple-element.55), channel_id=1, source_target_pairs={{0,4},{4,0},{8,12},{12,8},{1,5},{5,1},{9,13},{13,9},{2,6},{6,2},{1... | collective-permute-start | bytes 786440 | tf_op jit(solution)/shard_map/ppermute | solution.py:346
  7.8 24.4 %collective-permute-start.1 = (bf16[2,256,256]{2,1,0:T(8,128)(2,1)}, bf16[2,256,256]{2,1,0:T(8,128)(2,1)S(1)}, u32[]{:S(2)}, u32[]{:S(2)}) collective-permute-start(bf16[2,256,256]{2,1,0:T(8,128)(2,1)} %get-tuple-element.56), channel_id=1, source_target_pairs={{0,8},{4,12},{8,0},{12,4},{1,9},{5,13},{9,1},{13,5},{2,10},{6,14},... | collective-permute-start | bytes 786440 | tf_op jit(solution)/shard_map/ppermute | solution.py:346
  10.4 13.6 %copy-start.2 = (bf16[256,256]{1,0:T(8,128)(2,1)S(1)}, bf16[256,256]{1,0:T(8,128)(2,1)}, u32[]{:S(2)}) copy-start(bf16[256,256]{1,0:T(8,128)(2,1)} %refs_7_.3) | copy-start | bytes 393220
  10.4 14.3 %copy-start.3 = (bf16[256,256]{1,0:T(8,128)(2,1)S(1)}, bf16[256,256]{1,0:T(8,128)(2,1)}, u32[]{:S(2)}) copy-start(bf16[256,256]{1,0:T(8,128)(2,1)} %refs_11_.3) | copy-start | bytes 393220
  10.4 32.7 %collective-permute-start.3 = (bf16[2,256,256]{2,1,0:T(8,128)(2,1)}, bf16[2,256,256]{2,1,0:T(8,128)(2,1)S(1)}, u32[]{:S(2)}, u32[]{:S(2)}) collective-permute-start(bf16[2,256,256]{2,1,0:T(8,128)(2,1)} %get-tuple-element.64), channel_id=1, source_target_pairs={{0,4},{4,0},{8,12},{12,8},{1,5},{5,1},{9,13},{13,9},{2,6},{6,2},{1... | collective-permute-start | bytes 786440 | tf_op jit(solution)/shard_map/ppermute | solution.py:346
  11.9 31.2 %collective-permute-start.5 = (bf16[2,256,256]{2,1,0:T(8,128)(2,1)}, bf16[2,256,256]{2,1,0:T(8,128)(2,1)S(1)}, u32[]{:S(2)}, u32[]{:S(2)}) collective-permute-start(bf16[2,256,256]{2,1,0:T(8,128)(2,1)} %get-tuple-element.66), channel_id=1, source_target_pairs={{0,12},{4,8},{8,4},{12,0},{1,13},{5,9},{9,5},{13,1},{2,14},{6,10},... | collective-permute-start | bytes 786440 | tf_op jit(solution)/shard_map/ppermute | solution.py:346
  15.2 16.9 %copy-start.7 = (bf16[2,256,256]{2,1,0:T(8,128)(2,1)}, bf16[2,256,256]{2,1,0:T(8,128)(2,1)S(1)}, u32[]{:S(2)}) copy-start(bf16[2,256,256]{2,1,0:T(8,128)(2,1)S(1)} %collective-permute-done.2.refs_4_) | copy-start | bytes 786436
  15.2 37.6 %collective-permute-start.4 = (bf16[2,256,256]{2,1,0:T(8,128)(2,1)}, bf16[2,256,256]{2,1,0:T(8,128)(2,1)S(1)}, u32[]{:S(2)}, u32[]{:S(2)}) collective-permute-start(bf16[2,256,256]{2,1,0:T(8,128)(2,1)} %get-tuple-element.65), channel_id=1, source_target_pairs={{0,8},{4,12},{8,0},{12,4},{1,9},{5,13},{9,1},{13,5},{2,10},{6,14},... | collective-permute-start | bytes 786440 | tf_op jit(solution)/shard_map/ppermute | solution.py:346
  25.5 6.6 %copy-start.9 = (bf16[2,256,256]{2,1,0:T(8,128)(2,1)}, bf16[2,256,256]{2,1,0:T(8,128)(2,1)S(1)}, u32[]{:S(2)}) copy-start(bf16[2,256,256]{2,1,0:T(8,128)(2,1)S(1)} %collective-permute-done.refs_2_) | copy-start | bytes 786436
  43.1 12.2 %copy-start.5 = (bf16[2,256,256]{2,1,0:T(8,128)(2,1)}, bf16[2,256,256]{2,1,0:T(8,128)(2,1)S(1)}, u32[]{:S(2)}) copy-start(bf16[2,256,256]{2,1,0:T(8,128)(2,1)S(1)} %collective-permute-done.3.refs_2_) | copy-start | bytes 786436
  43.1 12.2 %copy-start.6 = (bf16[2,256,256]{2,1,0:T(8,128)(2,1)}, bf16[2,256,256]{2,1,0:T(8,128)(2,1)S(1)}, u32[]{:S(2)}) copy-start(bf16[2,256,256]{2,1,0:T(8,128)(2,1)S(1)} %collective-permute-done.5.refs_4_) | copy-start | bytes 786436
  52.8 2.5 %copy-start.8 = (bf16[2,256,256]{2,1,0:T(8,128)(2,1)}, bf16[2,256,256]{2,1,0:T(8,128)(2,1)S(1)}, u32[]{:S(2)}) copy-start(bf16[2,256,256]{2,1,0:T(8,128)(2,1)S(1)} %collective-permute-done.4.refs_3_) | copy-start | bytes 786436
  52.8 13.3 %collective-permute-start.11 = (bf16[2,256,256]{2,1,0:T(8,128)(2,1)}, bf16[2,256,256]{2,1,0:T(8,128)(2,1)S(1)}, u32[]{:S(2)}, u32[]{:S(2)}) collective-permute-start(bf16[2,256,256]{2,1,0:T(8,128)(2,1)} %get-tuple-element.79), channel_id=1, source_target_pairs={{0,12},{4,8},{8,4},{12,0},{1,13},{5,9},{9,5},{13,1},{2,14},{6,10},... | collective-permute-start | bytes 786440 | tf_op jit(solution)/shard_map/ppermute | solution.py:346
  55.3 11.0 %copy-start.23 = (bf16[2,256,256]{2,1,0:T(8,128)(2,1)S(1)}, bf16[2,256,256]{2,1,0:T(8,128)(2,1)}, u32[]{:S(2)}) copy-start(bf16[2,256,256]{2,1,0:T(8,128)(2,1)} %get-tuple-element.77) | copy-start | bytes 786436
  66.1 7.8 %copy-start.13 = (bf16[2,256,256]{2,1,0:T(8,128)(2,1)}, bf16[2,256,256]{2,1,0:T(8,128)(2,1)S(1)}, u32[]{:S(2)}) copy-start(bf16[2,256,256]{2,1,0:T(8,128)(2,1)S(1)} %collective-permute-done.11.refs_3_) | copy-start | bytes 786436
  66.1 2.2 %collective-permute-start.12 = (bf16[1024,256]{1,0:T(8,128)(2,1)}, bf16[1024,256]{1,0:T(8,128)(2,1)S(1)}, u32[]{:S(2)}, u32[]{:S(2)}) collective-permute-start(bf16[1024,256]{1,0:T(8,128)(2,1)} %bitcast.114), channel_id=1, source_target_pairs={{0,1},{1,0},{2,3},{3,2},{4,5},{5,4},{6,7},{7,6},{8,9},{9,8},{10,11... | collective-permute-start | bytes 1572872 | tf_op jit(solution)/shard_map/ppermute | solution.py:346
  66.3 19.8 %collective-permute-start.10 = (bf16[2,256,256]{2,1,0:T(8,128)(2,1)S(1)}, bf16[2,256,256]{2,1,0:T(8,128)(2,1)S(1)}, u32[]{:S(2)}, u32[]{:S(2)}) collective-permute-start(bf16[2,256,256]{2,1,0:T(8,128)(2,1)S(1)} %copy-done.23), channel_id=1, source_target_pairs={{0,8},{4,12},{8,0},{12,4},{1,9},{5,13},{9,1},{13,5},{2,10},{6,14},... | collective-permute-start | bytes 786440 | tf_op jit(solution)/shard_map/ppermute | solution.py:346
  68.3 6.2 %copy-start.22 = (bf16[2,256,256]{2,1,0:T(8,128)(2,1)S(1)}, bf16[2,256,256]{2,1,0:T(8,128)(2,1)}, u32[]{:S(2)}) copy-start(bf16[2,256,256]{2,1,0:T(8,128)(2,1)} %get-tuple-element.76) | copy-start | bytes 786436
  68.3 8.1 %copy-start.21 = (bf16[2,256,256]{2,1,0:T(8,128)(2,1)S(1)}, bf16[2,256,256]{2,1,0:T(8,128)(2,1)}, u32[]{:S(2)}) copy-start(bf16[2,256,256]{2,1,0:T(8,128)(2,1)} %get-tuple-element.75) | copy-start | bytes 786436
  69.8 4.7 %collective-permute-start.13 = (bf16[128,256]{1,0:T(8,128)(2,1)S(1)}, bf16[128,256]{1,0:T(8,128)(2,1)S(1)}, u32[]{:S(2)}, u32[]{:S(2)}) collective-permute-start(bf16[128,256]{1,0:T(8,128)(2,1)S(1)} %get-tuple-element.107), channel_id=1, source_target_pairs={{0,2},{2,0},{1,3},{3,1},{4,6},{6,4},{5,7},{7,5},{8,10},{10,8},{9,1... | collective-permute-start | bytes 196616 | tf_op jit(solution)/shard_map/ppermute | solution.py:346
  71.4 5.0 %collective-permute-start.14 = (bf16[128,256]{1,0:T(8,128)(2,1)S(1)}, bf16[128,256]{1,0:T(8,128)(2,1)S(1)}, u32[]{:S(2)}, u32[]{:S(2)}) collective-permute-start(bf16[128,256]{1,0:T(8,128)(2,1)S(1)} %get-tuple-element.110), channel_id=1, source_target_pairs={{0,2},{2,0},{1,3},{3,1},{4,6},{6,4},{5,7},{7,5},{8,10},{10,8},{9,1... | collective-permute-start | bytes 196616 | tf_op jit(solution)/shard_map/ppermute | solution.py:346
  71.9 5.8 %collective-permute-start.15 = (bf16[128,256]{1,0:T(8,128)(2,1)S(1)}, bf16[128,256]{1,0:T(8,128)(2,1)S(1)}, u32[]{:S(2)}, u32[]{:S(2)}) collective-permute-start(bf16[128,256]{1,0:T(8,128)(2,1)S(1)} %get-tuple-element.109), channel_id=1, source_target_pairs={{0,2},{2,0},{1,3},{3,1},{4,6},{6,4},{5,7},{7,5},{8,10},{10,8},{9,1... | collective-permute-start | bytes 196616 | tf_op jit(solution)/shard_map/ppermute | solution.py:346
  73.4 4.9 %collective-permute-start.16 = (bf16[128,256]{1,0:T(8,128)(2,1)S(1)}, bf16[128,256]{1,0:T(8,128)(2,1)S(1)}, u32[]{:S(2)}, u32[]{:S(2)}) collective-permute-start(bf16[128,256]{1,0:T(8,128)(2,1)S(1)} %get-tuple-element.108), channel_id=1, source_target_pairs={{0,2},{2,0},{1,3},{3,1},{4,6},{6,4},{5,7},{7,5},{8,10},{10,8},{9,1... | collective-permute-start | bytes 196616 | tf_op jit(solution)/shard_map/ppermute | solution.py:346
  74.5 21.5 %collective-permute-start.9 = (bf16[2,256,256]{2,1,0:T(8,128)(2,1)S(1)}, bf16[2,256,256]{2,1,0:T(8,128)(2,1)S(1)}, u32[]{:S(2)}, u32[]{:S(2)}) collective-permute-start(bf16[2,256,256]{2,1,0:T(8,128)(2,1)S(1)} %copy-done.22), channel_id=1, source_target_pairs={{0,12},{4,8},{8,4},{12,0},{1,13},{5,9},{9,5},{13,1},{2,14},{6,10},... | collective-permute-start | bytes 786440 | tf_op jit(solution)/shard_map/ppermute | solution.py:346
  76.4 19.6 %collective-permute-start.8 = (bf16[2,256,256]{2,1,0:T(8,128)(2,1)S(1)}, bf16[2,256,256]{2,1,0:T(8,128)(2,1)S(1)}, u32[]{:S(2)}, u32[]{:S(2)}) collective-permute-start(bf16[2,256,256]{2,1,0:T(8,128)(2,1)S(1)} %copy-done.21), channel_id=1, source_target_pairs={{0,4},{4,0},{8,12},{12,8},{1,5},{5,1},{9,13},{13,9},{2,6},{6,2},{1... | collective-permute-start | bytes 786440 | tf_op jit(solution)/shard_map/ppermute | solution.py:346
  78.4 30.2 %copy-start.20 = (bf16[2,256,256]{2,1,0:T(8,128)(2,1)S(1)}, bf16[2,256,256]{2,1,0:T(8,128)(2,1)}, u32[]{:S(2)}) copy-start(bf16[2,256,256]{2,1,0:T(8,128)(2,1)} %get-tuple-element.73) | copy-start | bytes 786436
  78.4 32.2 %copy-start.19 = (bf16[2,256,256]{2,1,0:T(8,128)(2,1)S(1)}, bf16[2,256,256]{2,1,0:T(8,128)(2,1)}, u32[]{:S(2)}) copy-start(bf16[2,256,256]{2,1,0:T(8,128)(2,1)} %get-tuple-element.72) | copy-start | bytes 786436
  86.1 25.2 %copy-start.14 = (bf16[2,256,256]{2,1,0:T(8,128)(2,1)}, bf16[2,256,256]{2,1,0:T(8,128)(2,1)S(1)}, u32[]{:S(2)}) copy-start(bf16[2,256,256]{2,1,0:T(8,128)(2,1)S(1)} %collective-permute-done.10.refs_2_) | copy-start | bytes 786436
  86.2 6.9 %collective-permute-start.17 = (bf16[128,256]{1,0:T(8,128)(2,1)S(1)}, bf16[128,256]{1,0:T(8,128)(2,1)S(1)}, u32[]{:S(2)}, u32[]{:S(2)}) collective-permute-start(bf16[128,256]{1,0:T(8,128)(2,1)S(1)} %get-tuple-element.104), channel_id=1, source_target_pairs={{0,4},{4,0},{8,12},{12,8},{1,5},{5,1},{9,13},{13,9},{2,6},{6,2},{1... | collective-permute-start | bytes 196616 | tf_op jit(solution)/shard_map/ppermute | solution.py:346
  86.2 9.7 %collective-permute-start.18 = (bf16[128,256]{1,0:T(8,128)(2,1)S(1)}, bf16[128,256]{1,0:T(8,128)(2,1)S(1)}, u32[]{:S(2)}, u32[]{:S(2)}) collective-permute-start(bf16[128,256]{1,0:T(8,128)(2,1)S(1)} %get-tuple-element.106), channel_id=1, source_target_pairs={{0,8},{4,12},{8,0},{12,4},{1,9},{5,13},{9,1},{13,5},{2,10},{6,14},... | collective-permute-start | bytes 196616 | tf_op jit(solution)/shard_map/ppermute | solution.py:346
  89.1 6.8 %collective-permute-start.19 = (bf16[128,256]{1,0:T(8,128)(2,1)S(1)}, bf16[128,256]{1,0:T(8,128)(2,1)S(1)}, u32[]{:S(2)}, u32[]{:S(2)}) collective-permute-start(bf16[128,256]{1,0:T(8,128)(2,1)S(1)} %get-tuple-element.105), channel_id=1, source_target_pairs={{0,12},{4,8},{8,4},{12,0},{1,13},{5,9},{9,5},{13,1},{2,14},{6,10},... | collective-permute-start | bytes 196616 | tf_op jit(solution)/shard_map/ppermute | solution.py:346
  96.0 27.2 %copy-start.4 = (bf16[2,256,256]{2,1,0:T(8,128)(2,1)}, bf16[2,256,256]{2,1,0:T(8,128)(2,1)S(1)}, u32[]{:S(2)}) copy-start(bf16[2,256,256]{2,1,0:T(8,128)(2,1)S(1)} %collective-permute-done.9.refs_3_) | copy-start | bytes 786436
  96.0 15.3 %copy-start.15 = (bf16[2,256,256]{2,1,0:T(8,128)(2,1)}, bf16[2,256,256]{2,1,0:T(8,128)(2,1)S(1)}, u32[]{:S(2)}) copy-start(bf16[2,256,256]{2,1,0:T(8,128)(2,1)S(1)} %collective-permute-done.8.refs_1_) | copy-start | bytes 786436
  96.0 4.5 %collective-permute-start.20 = (bf16[128,256]{1,0:T(8,128)(2,1)S(1)}, bf16[128,256]{1,0:T(8,128)(2,1)S(1)}, u32[]{:S(2)}, u32[]{:S(2)}) collective-permute-start(bf16[128,256]{1,0:T(8,128)(2,1)S(1)} %fusion.3), channel_id=1, source_target_pairs={{0,4},{4,0},{8,12},{12,8},{1,5},{5,1},{9,13},{13,9},{2,6},{6,2},{1... | collective-permute-start | bytes 196616 | tf_op jit(solution)/shard_map/ppermute | solution.py:346
  98.0 8.2 %collective-permute-start.21 = (bf16[128,256]{1,0:T(8,128)(2,1)S(1)}, bf16[128,256]{1,0:T(8,128)(2,1)S(1)}, u32[]{:S(2)}, u32[]{:S(2)}) collective-permute-start(bf16[128,256]{1,0:T(8,128)(2,1)S(1)} %fusion.3), channel_id=1, source_target_pairs={{0,8},{4,12},{8,0},{12,4},{1,9},{5,13},{9,1},{13,5},{2,10},{6,14},... | collective-permute-start | bytes 196616 | tf_op jit(solution)/shard_map/ppermute | solution.py:346
  98.9 7.2 %collective-permute-start.22 = (bf16[128,256]{1,0:T(8,128)(2,1)S(1)}, bf16[128,256]{1,0:T(8,128)(2,1)S(1)}, u32[]{:S(2)}, u32[]{:S(2)}) collective-permute-start(bf16[128,256]{1,0:T(8,128)(2,1)S(1)} %fusion.3), channel_id=1, source_target_pairs={{0,12},{4,8},{8,4},{12,0},{1,13},{5,9},{9,5},{13,1},{2,14},{6,10},... | collective-permute-start | bytes 196616 | tf_op jit(solution)/shard_map/ppermute | solution.py:346
  106.9 6.7 %collective-permute-start.23 = (bf16[512,256]{1,0:T(8,128)(2,1)S(1)}, bf16[512,256]{1,0:T(8,128)(2,1)S(1)}, u32[]{:S(2)}, u32[]{:S(2)}) collective-permute-start(bf16[512,256]{1,0:T(8,128)(2,1)S(1)} %bitcast_select_fusion.1), channel_id=1, source_target_pairs={{0,2},{2,0},{1,3},{3,1},{4,6},{6,4},{5,7},{7,5},{8,10},{10,8},{9,1... | collective-permute-start | bytes 786440 | tf_op jit(solution)/shard_map/ppermute | solution.py:346
  108.5 13.4 %collective-permute-start.7 = (bf16[2,256,256]{2,1,0:T(8,128)(2,1)S(1)}, bf16[2,256,256]{2,1,0:T(8,128)(2,1)S(1)}, u32[]{:S(2)}, u32[]{:S(2)}) collective-permute-start(bf16[2,256,256]{2,1,0:T(8,128)(2,1)S(1)} %copy-done.20), channel_id=1, source_target_pairs={{0,8},{4,12},{8,0},{12,4},{1,9},{5,13},{9,1},{13,5},{2,10},{6,14},... | collective-permute-start | bytes 786440 | tf_op jit(solution)/shard_map/ppermute | solution.py:346
  110.5 11.7 %collective-permute-start.6 = (bf16[2,256,256]{2,1,0:T(8,128)(2,1)S(1)}, bf16[2,256,256]{2,1,0:T(8,128)(2,1)S(1)}, u32[]{:S(2)}, u32[]{:S(2)}) collective-permute-start(bf16[2,256,256]{2,1,0:T(8,128)(2,1)S(1)} %copy-done.19), channel_id=1, source_target_pairs={{0,4},{4,0},{8,12},{12,8},{1,5},{5,1},{9,13},{13,9},{2,6},{6,2},{1... | collective-permute-start | bytes 786440 | tf_op jit(solution)/shard_map/ppermute | solution.py:346
  113.4 11.9 %collective-permute-start.24 = (bf16[512,256]{1,0:T(8,128)(2,1)S(1)}, bf16[512,256]{1,0:T(8,128)(2,1)S(1)}, u32[]{:S(2)}, u32[]{:S(2)}) collective-permute-start(bf16[512,256]{1,0:T(8,128)(2,1)S(1)} %bitcast_select_fusion.1), channel_id=1, source_target_pairs={{0,1},{1,0},{2,3},{3,2},{4,5},{5,4},{6,7},{7,6},{8,9},{9,8},{10,11... | collective-permute-start | bytes 786440 | tf_op jit(solution)/shard_map/ppermute | solution.py:346
  113.7 11.6 %copy-start.16 = (bf16[512,256]{1,0:T(8,128)(2,1)}, bf16[512,256]{1,0:T(8,128)(2,1)S(1)}, u32[]{:S(2)}) copy-start(bf16[512,256]{1,0:T(8,128)(2,1)S(1)} %collective-permute-done.23) | copy-start | bytes 786436
  121.9 1.2 copy-start.10
  122.2 0.9 copy-start.12
  122.2 3.1 %collective-permute-start.25 = (bf16[512,256]{1,0:T(8,128)(2,1)S(1)}, bf16[512,256]{1,0:T(8,128)(2,1)S(1)}, u32[]{:S(2)}, u32[]{:S(2)}) collective-permute-start(bf16[512,256]{1,0:T(8,128)(2,1)S(1)} %collective-permute-done.23), channel_id=1, source_target_pairs={{0,1},{1,0},{2,3},{3,2},{4,5},{5,4},{6,7},{7,6},{8,9},{9,8},{10,11... | collective-permute-start | bytes 786440 | tf_op jit(solution)/shard_map/ppermute | solution.py:346
  125.3 0.8 copy-start.18
  (2 other events, 1.4 us)

commit v4 on v3

--- a/solution.py
+++ b/solution.py
@@ -442,11 +442,9 @@
     own = own.reshape(2 * width, width)
     by_pair, by_core = swap(own, "pair"), swap(own, "core")
     partial = put(results_a, 0, None)
-    partial, by_pair = lax.optimization_barrier((partial, by_pair))
-    by_pair = tie(results_b, middle, by_pair)
-    by_pair = tie(results_b, near, by_pair)
-    by_both = swap(by_pair, "core")
+    by_both = lax.ppermute(own, ("pair", "core"), [(i, i ^ 3) for i in range(4)])
     sums = finish((own, by_pair, by_core, by_both), width)
+    sums, partial = lax.optimization_barrier((sums, partial))
     outputs, input_grad = put(results_b, 1, partial)
     return (outputs.reshape(shape), input_grad.reshape(shape), *sums)
 

time: 129 us -> 126 us (0.977)
  waiting for transfers between devices: 49.7 us -> 44.3 us
    ppermute x26 -> x25, waiting for transfers between devices: 49.7 us -> 41.8 us  [swap(): lax.ppermute(values, axis, [(i, i ^ s) for i in range(lax.axis_size(axis))])]
    ppermute x0 -> x1, waiting for transfers between devices: none -> 2.49 us  [on_device(): lax.ppermute(own, ('pair', 'core'), [(i, i ^ 3) for i in range(4)])]
    unnamed x52 -> x50, local copies, waits for them, and re-layouts: 3.18 us -> 3.9 us
    ppermute x26 -> x25, starting transfers between devices: 37.8 us -> 38 us  [swap(): lax.ppermute(values, axis, [(i, i ^ s) for i in range(lax.axis_size(axis))])]
  transfers between devices with their start and end apart: 26 -> 26, of which waited for: 15 -> 14; matrix products, arithmetic and copies ran while one was open for 5% -> 5% of each run, Pallas kernels for 21% -> 22%
where the time goes in v4:
time: 126 us; the launch traced here: 125 us
  waiting for transfers between devices  44.3 us (35%)
  starting transfers between devices  38.6 us (31%)
  Pallas kernels  31.7 us (25%)
  local copies, waits for them, and re-layouts  6.54 us (5%)
  other arithmetic  2.59 us (2%)
    ppermute x25, waiting for transfers between devices, swap(): lax.ppermute(values, axis, [(i, i ^ s) for i in range(lax.axis_size(axis))])  41.8 us
    ppermute x25, starting transfers between devices, swap(): lax.ppermute(values, axis, [(i, i ^ s) for i in range(lax.axis_size(axis))])  38 us
    pallas_call x2, Pallas kernels, run_chunk(): pl.pallas_call(functools.partial(chunk_kernel, n, hops, chunk, last), nam...  21 us
    pallas_call x2, Pallas kernels, put(): pl.pallas_call(functools.partial(put_kernel, n, chunk, into is None), nam...  4.17 us
    pallas_call x2, Pallas kernels, pick(): pl.pallas_call(functools.partial(pick_kernel, n, chunk), name='pick', in_...  3.98 us
    unnamed x50, local copies, waits for them, and re-layouts  3.9 us
    pallas_call x1, Pallas kernels, finish(): pl.pallas_call(finish_kernel, name='finish', in_specs=in_place(4), out_sh...  2.58 us
  transfers between devices with their start and end apart: 26, of which 14 were waited for; matrix products, arithmetic and copies ran while one was open for 5% of the time, Pallas kernels for 22%

profile of v4, /device:TPU:0, one launch (start us, length us, event | category | flops | bytes accessed | tf_op | source)
XLA Modules:
  0.0 124.9 jit_solution(16686631304788583919)
XLA Ops:
  0.6 2.0 %pick.2 = (bf16[2,256,256]{2,1,0:T(8,128)(2,1)}, bf16[2,256,256]{2,1,0:T(8,128)(2,1)}, bf16[2,256,256]{2,1,0:T(8,128)(2,1)}) custom-call(bf16[8,256,256]{2,1,0:T(8,128)(2,1)} %bitcast.70, bf16[8,256,256]{2,1,0:T(8,128)(2,1)} %bitcast.74), custom_call_target="tpu_custom_call" | custom-call | flops 1000 | bytes 1000 | tf_op jit(solution)/shard_map/pick/pallas_call | solution.py:96
  2.7 5.1 %collective-permute-start.2 = (bf16[2,256,256]{2,1,0:T(8,128)(2,1)}, bf16[2,256,256]{2,1,0:T(8,128)(2,1)S(1)}, u32[]{:S(2)}, u32[]{:S(2)}) collective-permute-start(bf16[2,256,256]{2,1,0:T(8,128)(2,1)} %get-tuple-element.56), channel_id=1, source_target_pairs={{0,12},{4,8},{8,4},{12,0},{1,13},{5,9},{9,5},{13,1},{2,14},{6,10},... | collective-permute-start | bytes 786440 | tf_op jit(solution)/shard_map/ppermute | solution.py:346
  7.8 0.6 collective-permute-start.1
  8.4 2.0 %pick.3 = (bf16[2,256,256]{2,1,0:T(8,128)(2,1)}, bf16[2,256,256]{2,1,0:T(8,128)(2,1)}, bf16[2,256,256]{2,1,0:T(8,128)(2,1)}) custom-call(bf16[8,256,256]{2,1,0:T(8,128)(2,1)} %bitcast.71, bf16[8,256,256]{2,1,0:T(8,128)(2,1)} %bitcast.75), custom_call_target="tpu_custom_call" | custom-call | flops 1000 | bytes 1000 | tf_op jit(solution)/shard_map/pick/pallas_call | solution.py:96
  10.4 1.5 %collective-permute-start.3 = (bf16[2,256,256]{2,1,0:T(8,128)(2,1)}, bf16[2,256,256]{2,1,0:T(8,128)(2,1)S(1)}, u32[]{:S(2)}, u32[]{:S(2)}) collective-permute-start(bf16[2,256,256]{2,1,0:T(8,128)(2,1)} %get-tuple-element.63), channel_id=1, source_target_pairs={{0,4},{4,0},{8,12},{12,8},{1,5},{5,1},{9,13},{13,9},{2,6},{6,2},{1... | collective-permute-start | bytes 786440 | tf_op jit(solution)/shard_map/ppermute | solution.py:346
  11.9 2.4 %collective-permute-start.5 = (bf16[2,256,256]{2,1,0:T(8,128)(2,1)}, bf16[2,256,256]{2,1,0:T(8,128)(2,1)S(1)}, u32[]{:S(2)}, u32[]{:S(2)}) collective-permute-start(bf16[2,256,256]{2,1,0:T(8,128)(2,1)} %get-tuple-element.65), channel_id=1, source_target_pairs={{0,12},{4,8},{8,4},{12,0},{1,13},{5,9},{9,5},{13,1},{2,14},{6,10},... | collective-permute-start | bytes 786440 | tf_op jit(solution)/shard_map/ppermute | solution.py:346
  14.3 0.9 collective-permute-done.2.refs_4_
  15.2 6.9 %collective-permute-start.4 = (bf16[2,256,256]{2,1,0:T(8,128)(2,1)}, bf16[2,256,256]{2,1,0:T(8,128)(2,1)S(1)}, u32[]{:S(2)}, u32[]{:S(2)}) collective-permute-start(bf16[2,256,256]{2,1,0:T(8,128)(2,1)} %get-tuple-element.64), channel_id=1, source_target_pairs={{0,8},{4,12},{8,0},{12,4},{1,9},{5,13},{9,1},{13,5},{2,10},{6,14},... | collective-permute-start | bytes 786440 | tf_op jit(solution)/shard_map/ppermute | solution.py:346
  22.1 0.9 copy.20
  23.1 0.9 copy.18
  24.0 0.8 copy.19
  24.8 0.8 copy.21
  25.5 6.6 %collective-permute-done.1.refs_3_ = bf16[2,256,256]{2,1,0:T(8,128)(2,1)S(1)} collective-permute-done((bf16[2,256,256]{2,1,0:T(8,128)(2,1)}, bf16[2,256,256]{2,1,0:T(8,128)(2,1)S(1)}, u32[]{:S(2)}, u32[]{:S(2)}) %collective-permute-start.1) | collective-permute-done | bytes 262176 | tf_op jit(solution)/shard_map/ppermute | solution.py:346
  32.2 0.7 copy-done.12
  32.9 10.3 %chunk.2 = (bf16[2,256,256]{2,1,0:T(8,128)(2,1)}, bf16[2,256,256]{2,1,0:T(8,128)(2,1)}, bf16[2,256,256]{2,1,0:T(8,128)(2,1)}, bf16[2,256,256]{2,1,0:T(8,128)(2,1)}, f32[8,256,256]{2,1,0:T(8,128)}) custom-call(bf16[8,256,256]{2,1,0:T(8,128)(2,1)} %bitcast.72, bf16[8,256,256]{2,1,0:T(8,128)(2,1)} %bitcast.76, bf16[2,256,256]{2,1,0:T(8,128)(2,1)} %copy-done.11, ...), custom_call_target="tpu_custom_call" | custom-call | flops 1000 | bytes 1000 | tf_op jit(solution)/shard_map/chunk/pallas_call | solution.py:314
  43.2 9.7 %collective-permute-done.4.refs_3_ = bf16[2,256,256]{2,1,0:T(8,128)(2,1)S(1)} collective-permute-done((bf16[2,256,256]{2,1,0:T(8,128)(2,1)}, bf16[2,256,256]{2,1,0:T(8,128)(2,1)S(1)}, u32[]{:S(2)}, u32[]{:S(2)}) %collective-permute-start.4) | collective-permute-done | bytes 262176 | tf_op jit(solution)/shard_map/ppermute | solution.py:346
  52.8 2.5 %collective-permute-start.10 = (bf16[2,256,256]{2,1,0:T(8,128)(2,1)}, bf16[2,256,256]{2,1,0:T(8,128)(2,1)S(1)}, u32[]{:S(2)}, u32[]{:S(2)}) collective-permute-start(bf16[2,256,256]{2,1,0:T(8,128)(2,1)} %get-tuple-element.76), channel_id=1, source_target_pairs={{0,12},{4,8},{8,4},{12,0},{1,13},{5,9},{9,5},{13,1},{2,14},{6,10},... | collective-permute-start | bytes 786440 | tf_op jit(solution)/shard_map/ppermute | solution.py:346
  55.3 10.7 %chunk.3 = (bf16[2,256,256]{2,1,0:T(8,128)(2,1)}, bf16[2,256,256]{2,1,0:T(8,128)(2,1)}, bf16[2,256,256]{2,1,0:T(8,128)(2,1)}, bf16[2,256,256]{2,1,0:T(8,128)(2,1...) custom-call(bf16[8,256,256]{2,1,0:T(8,128)(2,1)} %bitcast.73, bf16[8,256,256]{2,1,0:T(8,128)(2,1)} %bitcast.77, ...), custom_call_target="tpu_custom_call" | custom-call | flops 1000 | bytes 1000 | tf_op jit(solution)/shard_map/chunk/pallas_call | solution.py:314
  66.3 2.0 %collective-permute-done.11 = bf16[1024,256]{1,0:T(8,128)(2,1)S(1)} collective-permute-done((bf16[1024,256]{1,0:T(8,128)(2,1)}, bf16[1024,256]{1,0:T(8,128)(2,1)S(1)}, u32[]{:S(2)}, u32[]{:S(2)}) %collective-permute-start.11) | collective-permute-done | bytes 524320 | tf_op jit(solution)/shard_map/ppermute | solution.py:346
  68.3 1.4 %convert_add_fusion = f32[4,256,256]{2,1,0:T(8,128)S(1)} fusion(f32[4,256,256]{2,1,0:T(8,128)} %get-tuple-element.75, bf16[4,256,256]{2,1,0:T(8,128)(2,1)S(1)} %bitcast.97), kind=kLoop, calls=%fused_computation.1 | loop fusion | flops 524288 | bytes 2621440 | tf_op jit(solution)/shard_map/add | solution.py:429
  69.8 1.6 %collective-permute-start.12 = (bf16[128,256]{1,0:T(8,128)(2,1)S(1)}, bf16[128,256]{1,0:T(8,128)(2,1)S(1)}, u32[]{:S(2)}, u32[]{:S(2)}) collective-permute-start(bf16[128,256]{1,0:T(8,128)(2,1)S(1)} %get-tuple-element.105), channel_id=1, source_target_pairs={{0,2},{2,0},{1,3},{3,1},{4,6},{6,4},{5,7},{7,5},{8,10},{10,8},{9,1... | collective-permute-start | bytes 196616 | tf_op jit(solution)/shard_map/ppermute | solution.py:346
  71.9 1.5 %collective-permute-start.14 = (bf16[128,256]{1,0:T(8,128)(2,1)S(1)}, bf16[128,256]{1,0:T(8,128)(2,1)S(1)}, u32[]{:S(2)}, u32[]{:S(2)}) collective-permute-start(bf16[128,256]{1,0:T(8,128)(2,1)S(1)} %get-tuple-element.107), channel_id=1, source_target_pairs={{0,2},{2,0},{1,3},{3,1},{4,6},{6,4},{5,7},{7,5},{8,10},{10,8},{9,1... | collective-permute-start | bytes 196616 | tf_op jit(solution)/shard_map/ppermute | solution.py:346
  73.9 0.5 collective-permute-done.12
  74.5 1.3 %collective-permute-start.8 = (bf16[2,256,256]{2,1,0:T(8,128)(2,1)S(1)}, bf16[2,256,256]{2,1,0:T(8,128)(2,1)S(1)}, u32[]{:S(2)}, u32[]{:S(2)}) collective-permute-start(bf16[2,256,256]{2,1,0:T(8,128)(2,1)S(1)} %copy-done.22), channel_id=1, source_target_pairs={{0,12},{4,8},{8,4},{12,0},{1,13},{5,9},{9,5},{13,1},{2,14},{6,10},... | collective-permute-start | bytes 786440 | tf_op jit(solution)/shard_map/ppermute | solution.py:346
  76.3 1.3 %collective-permute-done.14 = bf16[128,256]{1,0:T(8,128)(2,1)S(1)} collective-permute-done((bf16[128,256]{1,0:T(8,128)(2,1)S(1)}, bf16[128,256]{1,0:T(8,128)(2,1)S(1)}, u32[]{:S(2)}, u32[]{:S(2)}) %collective-permute-start.14) | collective-permute-done | bytes 65568 | tf_op jit(solution)/shard_map/ppermute | solution.py:346
  77.6 0.7 collective-permute-done.15
  78.4 7.9 %collective-permute-done.9.refs_2_ = bf16[2,256,256]{2,1,0:T(8,128)(2,1)S(1)} collective-permute-done((bf16[2,256,256]{2,1,0:T(8,128)(2,1)}, bf16[2,256,256]{2,1,0:T(8,128)(2,1)S(1)}, u32[]{:S(2)}, u32[]{:S(2)}) %collective-permute-start.9) | collective-permute-done | bytes 262176 | tf_op jit(solution)/shard_map/ppermute | solution.py:346
  86.4 2.9 %collective-permute-start.17 = (bf16[128,256]{1,0:T(8,128)(2,1)S(1)}, bf16[128,256]{1,0:T(8,128)(2,1)S(1)}, u32[]{:S(2)}, u32[]{:S(2)}) collective-permute-start(bf16[128,256]{1,0:T(8,128)(2,1)S(1)} %get-tuple-element.104), channel_id=1, source_target_pairs={{0,8},{4,12},{8,0},{12,4},{1,9},{5,13},{9,1},{13,5},{2,10},{6,14},... | collective-permute-start | bytes 196616 | tf_op jit(solution)/shard_map/ppermute | solution.py:346
  89.3 1.5 %collective-permute-start.18 = (bf16[128,256]{1,0:T(8,128)(2,1)S(1)}, bf16[128,256]{1,0:T(8,128)(2,1)S(1)}, u32[]{:S(2)}, u32[]{:S(2)}) collective-permute-start(bf16[128,256]{1,0:T(8,128)(2,1)S(1)} %get-tuple-element.103), channel_id=1, source_target_pairs={{0,12},{4,8},{8,4},{12,0},{1,13},{5,9},{9,5},{13,1},{2,14},{6,10},... | collective-permute-start | bytes 196616 | tf_op jit(solution)/shard_map/ppermute | solution.py:346
  90.8 2.4 %collective-permute-done.16 = bf16[128,256]{1,0:T(8,128)(2,1)S(1)} collective-permute-done((bf16[128,256]{1,0:T(8,128)(2,1)S(1)}, bf16[128,256]{1,0:T(8,128)(2,1)S(1)}, u32[]{:S(2)}, u32[]{:S(2)}) %collective-permute-start.16) | collective-permute-done | bytes 65568 | tf_op jit(solution)/shard_map/ppermute | solution.py:346
  93.2 2.9 %collective-permute-done.17 = bf16[128,256]{1,0:T(8,128)(2,1)S(1)} collective-permute-done((bf16[128,256]{1,0:T(8,128)(2,1)S(1)}, bf16[128,256]{1,0:T(8,128)(2,1)S(1)}, u32[]{:S(2)}, u32[]{:S(2)}) %collective-permute-start.17) | collective-permute-done | bytes 65568 | tf_op jit(solution)/shard_map/ppermute | solution.py:346
  96.2 2.0 %collective-permute-start.20 = (bf16[128,256]{1,0:T(8,128)(2,1)S(1)}, bf16[128,256]{1,0:T(8,128)(2,1)S(1)}, u32[]{:S(2)}, u32[]{:S(2)}) collective-permute-start(bf16[128,256]{1,0:T(8,128)(2,1)S(1)} %fusion.3), channel_id=1, source_target_pairs={{0,4},{4,0},{8,12},{12,8},{1,5},{5,1},{9,13},{13,9},{2,6},{6,2},{1... | collective-permute-start | bytes 196616 | tf_op jit(solution)/shard_map/ppermute | solution.py:346
  98.2 0.9 collective-permute-start.21
  99.1 1.5 %collective-permute-start.22 = (bf16[128,256]{1,0:T(8,128)(2,1)S(1)}, bf16[128,256]{1,0:T(8,128)(2,1)S(1)}, u32[]{:S(2)}, u32[]{:S(2)}) collective-permute-start(bf16[128,256]{1,0:T(8,128)(2,1)S(1)} %fusion.3), channel_id=1, source_target_pairs={{0,12},{4,8},{8,4},{12,0},{1,13},{5,9},{9,5},{13,1},{2,14},{6,10},... | collective-permute-start | bytes 196616 | tf_op jit(solution)/shard_map/ppermute | solution.py:346
  100.7 1.1 collective-permute-start.6
  101.8 1.8 %collective-permute-start.7 = (bf16[2,256,256]{2,1,0:T(8,128)(2,1)S(1)}, bf16[2,256,256]{2,1,0:T(8,128)(2,1)S(1)}, u32[]{:S(2)}, u32[]{:S(2)}) collective-permute-start(bf16[2,256,256]{2,1,0:T(8,128)(2,1)S(1)} %copy-done.19), channel_id=1, source_target_pairs={{0,8},{4,12},{8,0},{12,4},{1,9},{5,13},{9,1},{13,5},{2,10},{6,14},... | collective-permute-start | bytes 786440 | tf_op jit(solution)/shard_map/ppermute | solution.py:346
  103.6 2.8 %collective-permute-done.21 = bf16[128,256]{1,0:T(8,128)(2,1)S(1)} collective-permute-done((bf16[128,256]{1,0:T(8,128)(2,1)S(1)}, bf16[128,256]{1,0:T(8,128)(2,1)S(1)}, u32[]{:S(2)}, u32[]{:S(2)}) %collective-permute-start.21) | collective-permute-done | bytes 65568 | tf_op jit(solution)/shard_map/ppermute | solution.py:346
  106.4 0.6 gather_fusion
  107.1 1.6 %collective-permute-start.23 = (bf16[512,256]{1,0:T(8,128)(2,1)S(1)}, bf16[512,256]{1,0:T(8,128)(2,1)S(1)}, u32[]{:S(2)}, u32[]{:S(2)}) collective-permute-start(bf16[512,256]{1,0:T(8,128)(2,1)S(1)} %bitcast_select_fusion), channel_id=1, source_target_pairs={{0,2},{2,0},{1,3},{3,1},{4,6},{6,4},{5,7},{7,5},{8,10},{10,8},{9,1... | collective-permute-start | bytes 786440 | tf_op jit(solution)/shard_map/ppermute | solution.py:346
  108.7 0.6 collective-permute-start.25
  109.4 2.1 %put.2 = (bf16[8,256,256]{2,1,0:T(8,128)(2,1)}, bf16[8,256,256]{2,1,0:T(8,128)(2,1)}) custom-call(bf16[2,256,256]{2,1,0:T(8,128)(2,1)} %get-tuple-element.88.refs_0_, bf16[2,256,256]{2,1,0:T(8,128)(2,1)} %copy-done.15, bf16[2,256,256]{2,1,0:T(8,128)(2,1)} %copy-done.14, bf16[2,256,256]{2,1,0:T(8,128)(2,1)} %copy-done.13), custom_call_target="tpu_custom_call" | custom-call | bytes 4194304 | tf_op jit(solution)/shard_map/put/pallas_call | solution.py:123
  111.5 0.8 bitcast_select_fusion.1.own
  112.4 3.6 %collective-permute-done.23 = bf16[512,256]{1,0:T(8,128)(2,1)S(1)} collective-permute-done((bf16[512,256]{1,0:T(8,128)(2,1)S(1)}, bf16[512,256]{1,0:T(8,128)(2,1)S(1)}, u32[]{:S(2)}, u32[]{:S(2)}) %collective-permute-start.23) | collective-permute-done | bytes 262176 | tf_op jit(solution)/shard_map/ppermute | solution.py:346
  116.0 2.5 %collective-permute-done.25 = bf16[512,256]{1,0:T(8,128)(2,1)S(1)} collective-permute-done((bf16[512,256]{1,0:T(8,128)(2,1)S(1)}, bf16[512,256]{1,0:T(8,128)(2,1)S(1)}, u32[]{:S(2)}, u32[]{:S(2)}) %collective-permute-start.25) | collective-permute-done | bytes 262176 | tf_op jit(solution)/shard_map/ppermute | solution.py:445
  118.5 0.7 copy-done.18
  119.2 2.6 %finish.1 = (f32[3,256,256]{2,1,0:T(8,128)}, f32[3,256,256]{2,1,0:T(8,128)}, f32[256,256]{1,0:T(8,128)}, f32[256,256]{1,0:T(8,128)}) custom-call(bf16[2,256,256]{2,1,0:T(8,128)(2,1)} %bitcast_select_fusion.1.own, bf16[2,256,256]{2,1,0:T(8,128)(2,1)} %bitcast.98, bf16[2,256,256]{2,1,0:T(8,128)(2,1)} %bitcast.99, bf16[2,256,256]{2,1,0:T(8,128)(2,1)} %bitcast.100), custom_call_target="tpu_custom_call" | custom-call | flops 1000 | bytes 1000 | tf_op jit(solution)/shard_map/finish/pallas_call | solution.py:166
  121.9 0.7 copy-done.5
  122.7 2.1 %put.3 = (bf16[8,256,256]{2,1,0:T(8,128)(2,1)}, bf16[8,256,256]{2,1,0:T(8,128)(2,1)}) custom-call(bf16[2,256,256]{2,1,0:T(8,128)(2,1)} %get-tuple-element.70.refs_0_, bf16[2,256,256]{2,1,0:T(8,128)(2,1)} %copy-done.5, bf16[2,256,256]{2,1,0:T(8,128)(2,1)} %copy-done.6, bf16[2,256,256]{2,1,0:T(8,128)(2,1)} %copy-done.4, ...), custom_call_target="tpu_custom_call", output_to_operand_aliasing={{0}: (4, {}), {1}: (5, {})} | custom-call | bytes 4194304 | tf_op jit(solution)/shard_map/put/pallas_call | solution.py:123
  (83 shorter events, 2.6 us)
Async XLA Ops:
  0.6 21.5 %copy-start.1 = (bf16[3,256,256]{2,1,0:T(8,128)(2,1)S(1)}, bf16[3,256,256]{2,1,0:T(8,128)(2,1)}, u32[]{:S(2)}) copy-start(bf16[3,256,256]{2,1,0:T(8,128)(2,1)} %param.13) | copy-start | bytes 1179652
  2.7 20.4 %copy-start = (bf16[3,256,256]{2,1,0:T(8,128)(2,1)S(1)}, bf16[3,256,256]{2,1,0:T(8,128)(2,1)}, u32[]{:S(2)}) copy-start(bf16[3,256,256]{2,1,0:T(8,128)(2,1)} %param.12) | copy-start | bytes 1179652
  2.7 12.5 %collective-permute-start.2 = (bf16[2,256,256]{2,1,0:T(8,128)(2,1)}, bf16[2,256,256]{2,1,0:T(8,128)(2,1)S(1)}, u32[]{:S(2)}, u32[]{:S(2)}) collective-permute-start(bf16[2,256,256]{2,1,0:T(8,128)(2,1)} %get-tuple-element.56), channel_id=1, source_target_pairs={{0,12},{4,8},{8,4},{12,0},{1,13},{5,9},{9,5},{13,1},{2,14},{6,10},... | collective-permute-start | bytes 786440 | tf_op jit(solution)/shard_map/ppermute | solution.py:346
  7.8 17.8 %collective-permute-start = (bf16[2,256,256]{2,1,0:T(8,128)(2,1)}, bf16[2,256,256]{2,1,0:T(8,128)(2,1)S(1)}, u32[]{:S(2)}, u32[]{:S(2)}) collective-permute-start(bf16[2,256,256]{2,1,0:T(8,128)(2,1)} %get-tuple-element.54), channel_id=1, source_target_pairs={{0,4},{4,0},{8,12},{12,8},{1,5},{5,1},{9,13},{13,9},{2,6},{6,2},{1... | collective-permute-start | bytes 786440 | tf_op jit(solution)/shard_map/ppermute | solution.py:346
  7.8 24.4 %collective-permute-start.1 = (bf16[2,256,256]{2,1,0:T(8,128)(2,1)}, bf16[2,256,256]{2,1,0:T(8,128)(2,1)S(1)}, u32[]{:S(2)}, u32[]{:S(2)}) collective-permute-start(bf16[2,256,256]{2,1,0:T(8,128)(2,1)} %get-tuple-element.55), channel_id=1, source_target_pairs={{0,8},{4,12},{8,0},{12,4},{1,9},{5,13},{9,1},{13,5},{2,10},{6,14},... | collective-permute-start | bytes 786440 | tf_op jit(solution)/shard_map/ppermute | solution.py:346
  10.4 13.6 %copy-start.2 = (bf16[256,256]{1,0:T(8,128)(2,1)S(1)}, bf16[256,256]{1,0:T(8,128)(2,1)}, u32[]{:S(2)}) copy-start(bf16[256,256]{1,0:T(8,128)(2,1)} %refs_7_.3) | copy-start | bytes 393220
  10.4 14.3 %copy-start.3 = (bf16[256,256]{1,0:T(8,128)(2,1)S(1)}, bf16[256,256]{1,0:T(8,128)(2,1)}, u32[]{:S(2)}) copy-start(bf16[256,256]{1,0:T(8,128)(2,1)} %refs_11_.3) | copy-start | bytes 393220
  10.4 32.7 %collective-permute-start.3 = (bf16[2,256,256]{2,1,0:T(8,128)(2,1)}, bf16[2,256,256]{2,1,0:T(8,128)(2,1)S(1)}, u32[]{:S(2)}, u32[]{:S(2)}) collective-permute-start(bf16[2,256,256]{2,1,0:T(8,128)(2,1)} %get-tuple-element.63), channel_id=1, source_target_pairs={{0,4},{4,0},{8,12},{12,8},{1,5},{5,1},{9,13},{13,9},{2,6},{6,2},{1... | collective-permute-start | bytes 786440 | tf_op jit(solution)/shard_map/ppermute | solution.py:346
  11.9 31.3 %collective-permute-start.5 = (bf16[2,256,256]{2,1,0:T(8,128)(2,1)}, bf16[2,256,256]{2,1,0:T(8,128)(2,1)S(1)}, u32[]{:S(2)}, u32[]{:S(2)}) collective-permute-start(bf16[2,256,256]{2,1,0:T(8,128)(2,1)} %get-tuple-element.65), channel_id=1, source_target_pairs={{0,12},{4,8},{8,4},{12,0},{1,13},{5,9},{9,5},{13,1},{2,14},{6,10},... | collective-permute-start | bytes 786440 | tf_op jit(solution)/shard_map/ppermute | solution.py:346
  15.2 16.9 %copy-start.9 = (bf16[2,256,256]{2,1,0:T(8,128)(2,1)}, bf16[2,256,256]{2,1,0:T(8,128)(2,1)S(1)}, u32[]{:S(2)}) copy-start(bf16[2,256,256]{2,1,0:T(8,128)(2,1)S(1)} %collective-permute-done.2.refs_4_) | copy-start | bytes 786436
  15.2 37.6 %collective-permute-start.4 = (bf16[2,256,256]{2,1,0:T(8,128)(2,1)}, bf16[2,256,256]{2,1,0:T(8,128)(2,1)S(1)}, u32[]{:S(2)}, u32[]{:S(2)}) collective-permute-start(bf16[2,256,256]{2,1,0:T(8,128)(2,1)} %get-tuple-element.64), channel_id=1, source_target_pairs={{0,8},{4,12},{8,0},{12,4},{1,9},{5,13},{9,1},{13,5},{2,10},{6,14},... | collective-permute-start | bytes 786440 | tf_op jit(solution)/shard_map/ppermute | solution.py:346
  25.5 6.6 %copy-start.11 = (bf16[2,256,256]{2,1,0:T(8,128)(2,1)}, bf16[2,256,256]{2,1,0:T(8,128)(2,1)S(1)}, u32[]{:S(2)}) copy-start(bf16[2,256,256]{2,1,0:T(8,128)(2,1)S(1)} %collective-permute-done.refs_2_) | copy-start | bytes 786436
  43.1 12.2 %copy-start.7 = (bf16[2,256,256]{2,1,0:T(8,128)(2,1)}, bf16[2,256,256]{2,1,0:T(8,128)(2,1)S(1)}, u32[]{:S(2)}) copy-start(bf16[2,256,256]{2,1,0:T(8,128)(2,1)S(1)} %collective-permute-done.3.refs_2_) | copy-start | bytes 786436
  43.1 12.2 %copy-start.8 = (bf16[2,256,256]{2,1,0:T(8,128)(2,1)}, bf16[2,256,256]{2,1,0:T(8,128)(2,1)S(1)}, u32[]{:S(2)}) copy-start(bf16[2,256,256]{2,1,0:T(8,128)(2,1)S(1)} %collective-permute-done.5.refs_4_) | copy-start | bytes 786436
  52.8 2.5 %copy-start.10 = (bf16[2,256,256]{2,1,0:T(8,128)(2,1)}, bf16[2,256,256]{2,1,0:T(8,128)(2,1)S(1)}, u32[]{:S(2)}) copy-start(bf16[2,256,256]{2,1,0:T(8,128)(2,1)S(1)} %collective-permute-done.4.refs_3_) | copy-start | bytes 786436
  52.8 13.2 %collective-permute-start.10 = (bf16[2,256,256]{2,1,0:T(8,128)(2,1)}, bf16[2,256,256]{2,1,0:T(8,128)(2,1)S(1)}, u32[]{:S(2)}, u32[]{:S(2)}) collective-permute-start(bf16[2,256,256]{2,1,0:T(8,128)(2,1)} %get-tuple-element.76), channel_id=1, source_target_pairs={{0,12},{4,8},{8,4},{12,0},{1,13},{5,9},{9,5},{13,1},{2,14},{6,10},... | collective-permute-start | bytes 786440 | tf_op jit(solution)/shard_map/ppermute | solution.py:346
  66.1 7.8 %copy-start.13 = (bf16[2,256,256]{2,1,0:T(8,128)(2,1)}, bf16[2,256,256]{2,1,0:T(8,128)(2,1)S(1)}, u32[]{:S(2)}) copy-start(bf16[2,256,256]{2,1,0:T(8,128)(2,1)S(1)} %collective-permute-done.10.refs_3_) | copy-start | bytes 786436
  66.1 2.2 %collective-permute-start.11 = (bf16[1024,256]{1,0:T(8,128)(2,1)}, bf16[1024,256]{1,0:T(8,128)(2,1)S(1)}, u32[]{:S(2)}, u32[]{:S(2)}) collective-permute-start(bf16[1024,256]{1,0:T(8,128)(2,1)} %bitcast.114), channel_id=1, source_target_pairs={{0,1},{1,0},{2,3},{3,2},{4,5},{5,4},{6,7},{7,6},{8,9},{9,8},{10,11... | collective-permute-start | bytes 1572872 | tf_op jit(solution)/shard_map/ppermute | solution.py:346
  66.3 20.0 %collective-permute-start.9 = (bf16[2,256,256]{2,1,0:T(8,128)(2,1)}, bf16[2,256,256]{2,1,0:T(8,128)(2,1)S(1)}, u32[]{:S(2)}, u32[]{:S(2)}) collective-permute-start(bf16[2,256,256]{2,1,0:T(8,128)(2,1)} %get-tuple-element.74), channel_id=1, source_target_pairs={{0,8},{4,12},{8,0},{12,4},{1,9},{5,13},{9,1},{13,5},{2,10},{6,14},... | collective-permute-start | bytes 786440 | tf_op jit(solution)/shard_map/ppermute | solution.py:346
  68.3 6.2 %copy-start.22 = (bf16[2,256,256]{2,1,0:T(8,128)(2,1)S(1)}, bf16[2,256,256]{2,1,0:T(8,128)(2,1)}, u32[]{:S(2)}) copy-start(bf16[2,256,256]{2,1,0:T(8,128)(2,1)} %get-tuple-element.73) | copy-start | bytes 786436
  68.3 8.1 %copy-start.21 = (bf16[2,256,256]{2,1,0:T(8,128)(2,1)S(1)}, bf16[2,256,256]{2,1,0:T(8,128)(2,1)}, u32[]{:S(2)}) copy-start(bf16[2,256,256]{2,1,0:T(8,128)(2,1)} %get-tuple-element.81) | copy-start | bytes 786436
  69.8 4.7 %collective-permute-start.12 = (bf16[128,256]{1,0:T(8,128)(2,1)S(1)}, bf16[128,256]{1,0:T(8,128)(2,1)S(1)}, u32[]{:S(2)}, u32[]{:S(2)}) collective-permute-start(bf16[128,256]{1,0:T(8,128)(2,1)S(1)} %get-tuple-element.105), channel_id=1, source_target_pairs={{0,2},{2,0},{1,3},{3,1},{4,6},{6,4},{5,7},{7,5},{8,10},{10,8},{9,1... | collective-permute-start | bytes 196616 | tf_op jit(solution)/shard_map/ppermute | solution.py:346
  71.4 5.0 %collective-permute-start.13 = (bf16[128,256]{1,0:T(8,128)(2,1)S(1)}, bf16[128,256]{1,0:T(8,128)(2,1)S(1)}, u32[]{:S(2)}, u32[]{:S(2)}) collective-permute-start(bf16[128,256]{1,0:T(8,128)(2,1)S(1)} %get-tuple-element.108), channel_id=1, source_target_pairs={{0,2},{2,0},{1,3},{3,1},{4,6},{6,4},{5,7},{7,5},{8,10},{10,8},{9,1... | collective-permute-start | bytes 196616 | tf_op jit(solution)/shard_map/ppermute | solution.py:346
  71.9 5.8 %collective-permute-start.14 = (bf16[128,256]{1,0:T(8,128)(2,1)S(1)}, bf16[128,256]{1,0:T(8,128)(2,1)S(1)}, u32[]{:S(2)}, u32[]{:S(2)}) collective-permute-start(bf16[128,256]{1,0:T(8,128)(2,1)S(1)} %get-tuple-element.107), channel_id=1, source_target_pairs={{0,2},{2,0},{1,3},{3,1},{4,6},{6,4},{5,7},{7,5},{8,10},{10,8},{9,1... | collective-permute-start | bytes 196616 | tf_op jit(solution)/shard_map/ppermute | solution.py:346
  73.4 27.3 %copy-start.20 = (bf16[2,256,256]{2,1,0:T(8,128)(2,1)S(1)}, bf16[2,256,256]{2,1,0:T(8,128)(2,1)}, u32[]{:S(2)}) copy-start(bf16[2,256,256]{2,1,0:T(8,128)(2,1)} %get-tuple-element.71) | copy-start | bytes 786436
  73.4 28.4 %copy-start.19 = (bf16[2,256,256]{2,1,0:T(8,128)(2,1)S(1)}, bf16[2,256,256]{2,1,0:T(8,128)(2,1)}, u32[]{:S(2)}) copy-start(bf16[2,256,256]{2,1,0:T(8,128)(2,1)} %get-tuple-element.72) | copy-start | bytes 786436
  73.4 4.9 %collective-permute-start.15 = (bf16[128,256]{1,0:T(8,128)(2,1)S(1)}, bf16[128,256]{1,0:T(8,128)(2,1)S(1)}, u32[]{:S(2)}, u32[]{:S(2)}) collective-permute-start(bf16[128,256]{1,0:T(8,128)(2,1)S(1)} %get-tuple-element.106), channel_id=1, source_target_pairs={{0,2},{2,0},{1,3},{3,1},{4,6},{6,4},{5,7},{7,5},{8,10},{10,8},{9,1... | collective-permute-start | bytes 196616 | tf_op jit(solution)/shard_map/ppermute | solution.py:346
  74.5 21.7 %collective-permute-start.8 = (bf16[2,256,256]{2,1,0:T(8,128)(2,1)S(1)}, bf16[2,256,256]{2,1,0:T(8,128)(2,1)S(1)}, u32[]{:S(2)}, u32[]{:S(2)}) collective-permute-start(bf16[2,256,256]{2,1,0:T(8,128)(2,1)S(1)} %copy-done.22), channel_id=1, source_target_pairs={{0,12},{4,8},{8,4},{12,0},{1,13},{5,9},{9,5},{13,1},{2,14},{6,10},... | collective-permute-start | bytes 786440 | tf_op jit(solution)/shard_map/ppermute | solution.py:346
  76.3 19.8 %collective-permute-start.19 = (bf16[2,256,256]{2,1,0:T(8,128)(2,1)S(1)}, bf16[2,256,256]{2,1,0:T(8,128)(2,1)S(1)}, u32[]{:S(2)}, u32[]{:S(2)}) collective-permute-start(bf16[2,256,256]{2,1,0:T(8,128)(2,1)S(1)} %copy-done.21), channel_id=1, source_target_pairs={{0,4},{4,0},{8,12},{12,8},{1,5},{5,1},{9,13},{13,9},{2,6},{6,2},{1... | collective-permute-start | bytes 786440 | tf_op jit(solution)/shard_map/ppermute | solution.py:346
  86.3 23.1 %copy-start.14 = (bf16[2,256,256]{2,1,0:T(8,128)(2,1)}, bf16[2,256,256]{2,1,0:T(8,128)(2,1)S(1)}, u32[]{:S(2)}) copy-start(bf16[2,256,256]{2,1,0:T(8,128)(2,1)S(1)} %collective-permute-done.9.refs_2_) | copy-start | bytes 786436
  86.4 6.9 %collective-permute-start.16 = (bf16[128,256]{1,0:T(8,128)(2,1)S(1)}, bf16[128,256]{1,0:T(8,128)(2,1)S(1)}, u32[]{:S(2)}, u32[]{:S(2)}) collective-permute-start(bf16[128,256]{1,0:T(8,128)(2,1)S(1)} %get-tuple-element.102), channel_id=1, source_target_pairs={{0,4},{4,0},{8,12},{12,8},{1,5},{5,1},{9,13},{13,9},{2,6},{6,2},{1... | collective-permute-start | bytes 196616 | tf_op jit(solution)/shard_map/ppermute | solution.py:346
  86.4 9.7 %collective-permute-start.17 = (bf16[128,256]{1,0:T(8,128)(2,1)S(1)}, bf16[128,256]{1,0:T(8,128)(2,1)S(1)}, u32[]{:S(2)}, u32[]{:S(2)}) collective-permute-start(bf16[128,256]{1,0:T(8,128)(2,1)S(1)} %get-tuple-element.104), channel_id=1, source_target_pairs={{0,8},{4,12},{8,0},{12,4},{1,9},{5,13},{9,1},{13,5},{2,10},{6,14},... | collective-permute-start | bytes 196616 | tf_op jit(solution)/shard_map/ppermute | solution.py:346
  89.3 6.8 %collective-permute-start.18 = (bf16[128,256]{1,0:T(8,128)(2,1)S(1)}, bf16[128,256]{1,0:T(8,128)(2,1)S(1)}, u32[]{:S(2)}, u32[]{:S(2)}) collective-permute-start(bf16[128,256]{1,0:T(8,128)(2,1)S(1)} %get-tuple-element.103), channel_id=1, source_target_pairs={{0,12},{4,8},{8,4},{12,0},{1,13},{5,9},{9,5},{13,1},{2,14},{6,10},... | collective-permute-start | bytes 196616 | tf_op jit(solution)/shard_map/ppermute | solution.py:346
  96.2 25.6 %copy-start.4 = (bf16[2,256,256]{2,1,0:T(8,128)(2,1)}, bf16[2,256,256]{2,1,0:T(8,128)(2,1)S(1)}, u32[]{:S(2)}) copy-start(bf16[2,256,256]{2,1,0:T(8,128)(2,1)S(1)} %collective-permute-done.8.refs_3_) | copy-start | bytes 786436
  96.2 13.2 %copy-start.15 = (bf16[2,256,256]{2,1,0:T(8,128)(2,1)}, bf16[2,256,256]{2,1,0:T(8,128)(2,1)S(1)}, u32[]{:S(2)}) copy-start(bf16[2,256,256]{2,1,0:T(8,128)(2,1)S(1)} %collective-permute-done.19.refs_1_) | copy-start | bytes 786436
  96.2 7.4 %collective-permute-start.20 = (bf16[128,256]{1,0:T(8,128)(2,1)S(1)}, bf16[128,256]{1,0:T(8,128)(2,1)S(1)}, u32[]{:S(2)}, u32[]{:S(2)}) collective-permute-start(bf16[128,256]{1,0:T(8,128)(2,1)S(1)} %fusion.3), channel_id=1, source_target_pairs={{0,4},{4,0},{8,12},{12,8},{1,5},{5,1},{9,13},{13,9},{2,6},{6,2},{1... | collective-permute-start | bytes 196616 | tf_op jit(solution)/shard_map/ppermute | solution.py:346
  98.2 8.2 %collective-permute-start.21 = (bf16[128,256]{1,0:T(8,128)(2,1)S(1)}, bf16[128,256]{1,0:T(8,128)(2,1)S(1)}, u32[]{:S(2)}, u32[]{:S(2)}) collective-permute-start(bf16[128,256]{1,0:T(8,128)(2,1)S(1)} %fusion.3), channel_id=1, source_target_pairs={{0,8},{4,12},{8,0},{12,4},{1,9},{5,13},{9,1},{13,5},{2,10},{6,14},... | collective-permute-start | bytes 196616 | tf_op jit(solution)/shard_map/ppermute | solution.py:346
  99.1 7.2 %collective-permute-start.22 = (bf16[128,256]{1,0:T(8,128)(2,1)S(1)}, bf16[128,256]{1,0:T(8,128)(2,1)S(1)}, u32[]{:S(2)}, u32[]{:S(2)}) collective-permute-start(bf16[128,256]{1,0:T(8,128)(2,1)S(1)} %fusion.3), channel_id=1, source_target_pairs={{0,12},{4,8},{8,4},{12,0},{1,13},{5,9},{9,5},{13,1},{2,14},{6,10},... | collective-permute-start | bytes 196616 | tf_op jit(solution)/shard_map/ppermute | solution.py:346
  100.7 21.1 %collective-permute-start.6 = (bf16[2,256,256]{2,1,0:T(8,128)(2,1)S(1)}, bf16[2,256,256]{2,1,0:T(8,128)(2,1)S(1)}, u32[]{:S(2)}, u32[]{:S(2)}) collective-permute-start(bf16[2,256,256]{2,1,0:T(8,128)(2,1)S(1)} %copy-done.20), channel_id=1, source_target_pairs={{0,4},{4,0},{8,12},{12,8},{1,5},{5,1},{9,13},{13,9},{2,6},{6,2},{1... | collective-permute-start | bytes 786440 | tf_op jit(solution)/shard_map/ppermute | solution.py:346
  101.8 20.1 %collective-permute-start.7 = (bf16[2,256,256]{2,1,0:T(8,128)(2,1)S(1)}, bf16[2,256,256]{2,1,0:T(8,128)(2,1)S(1)}, u32[]{:S(2)}, u32[]{:S(2)}) collective-permute-start(bf16[2,256,256]{2,1,0:T(8,128)(2,1)S(1)} %copy-done.19), channel_id=1, source_target_pairs={{0,8},{4,12},{8,0},{12,4},{1,9},{5,13},{9,1},{13,5},{2,10},{6,14},... | collective-permute-start | bytes 786440 | tf_op jit(solution)/shard_map/ppermute | solution.py:346
  107.1 8.9 %collective-permute-start.23 = (bf16[512,256]{1,0:T(8,128)(2,1)S(1)}, bf16[512,256]{1,0:T(8,128)(2,1)S(1)}, u32[]{:S(2)}, u32[]{:S(2)}) collective-permute-start(bf16[512,256]{1,0:T(8,128)(2,1)S(1)} %bitcast_select_fusion), channel_id=1, source_target_pairs={{0,2},{2,0},{1,3},{3,1},{4,6},{6,4},{5,7},{7,5},{8,10},{10,8},{9,1... | collective-permute-start | bytes 786440 | tf_op jit(solution)/shard_map/ppermute | solution.py:346
  108.7 7.3 %collective-permute-start.24 = (bf16[512,256]{1,0:T(8,128)(2,1)S(1)}, bf16[512,256]{1,0:T(8,128)(2,1)S(1)}, u32[]{:S(2)}, u32[]{:S(2)}) collective-permute-start(bf16[512,256]{1,0:T(8,128)(2,1)S(1)} %bitcast_select_fusion), channel_id=1, source_target_pairs={{0,1},{1,0},{2,3},{3,2},{4,5},{5,4},{6,7},{7,6},{8,9},{9,8},{10,11... | collective-permute-start | bytes 786440 | tf_op jit(solution)/shard_map/ppermute | solution.py:346
  108.7 9.8 %collective-permute-start.25 = (bf16[512,256]{1,0:T(8,128)(2,1)S(1)}, bf16[512,256]{1,0:T(8,128)(2,1)S(1)}, u32[]{:S(2)}, u32[]{:S(2)}) collective-permute-start(bf16[512,256]{1,0:T(8,128)(2,1)S(1)} %bitcast_select_fusion), channel_id=1, source_target_pairs={{0,3},{1,2},{2,1},{3,0},{4,7},{5,6},{6,5},{7,4},{8,11},{9,10},{10,... | collective-permute-start | bytes 786440 | tf_op jit(solution)/shard_map/ppermute | solution.py:445
  116.0 2.5 %copy-start.16 = (bf16[512,256]{1,0:T(8,128)(2,1)}, bf16[512,256]{1,0:T(8,128)(2,1)S(1)}, u32[]{:S(2)}) copy-start(bf16[512,256]{1,0:T(8,128)(2,1)S(1)} %collective-permute-done.23) | copy-start | bytes 786436
  116.0 2.5 %copy-start.17 = (bf16[512,256]{1,0:T(8,128)(2,1)}, bf16[512,256]{1,0:T(8,128)(2,1)S(1)}, u32[]{:S(2)}) copy-start(bf16[512,256]{1,0:T(8,128)(2,1)S(1)} %collective-permute-done.24) | copy-start | bytes 786436
  118.5 0.7 copy-start.18
  121.8 0.7 copy-start.5
  121.9 0.8 copy-start.6
  (1 other events, 0.7 us)

commit v5 on v4

--- a/solution.py
+++ b/solution.py
@@ -131,6 +131,7 @@
             pltpu.VMEM((2 * n, rows, width), BF16),
             pltpu.SemaphoreType.DMA((2, 2 * n)),
         ],
+        compiler_params=pltpu.CompilerParams(vmem_limit_bytes=8 << 20),
         cost_estimate=pl.CostEstimate(
             flops=0, bytes_accessed=16 * n * rows * width, transcendentals=0
         ),
@@ -172,7 +173,7 @@
             pltpu.VMEM((2, 2, 2, width, width), BF16),
             pltpu.SemaphoreType.DMA((4,)),
         ],
-        compiler_params=pltpu.CompilerParams(vmem_limit_bytes=VMEM_LIMIT),
+        compiler_params=pltpu.CompilerParams(vmem_limit_bytes=8 << 20),
         cost_estimate=small_cost(),
     )(*quarters)
 

time: 126 us -> 123 us (0.976)
  local copies, waits for them, and re-layouts: 6.54 us -> 4.98 us
    unnamed x50 -> x36, local copies, waits for them, and re-layouts: 3.9 us -> 2.34 us
where the time goes in v5:
time: 123 us
  waiting for transfers between devices  44.7 us (36%)
  starting transfers between devices  38.6 us (31%)
  Pallas kernels  31.3 us (25%)
  local copies, waits for them, and re-layouts  4.98 us (4%)
  other arithmetic  1.88 us (2%)
    ppermute x25, waiting for transfers between devices, swap(): lax.ppermute(values, axis, [(i, i ^ s) for i in range(lax.axis_size(axis))])  42.2 us
    ppermute x25, starting transfers between devices, swap(): lax.ppermute(values, axis, [(i, i ^ s) for i in range(lax.axis_size(axis))])  37.9 us
    pallas_call x2, Pallas kernels, run_chunk(): pl.pallas_call(functools.partial(chunk_kernel, n, hops, chunk, last), nam...  21 us
    pallas_call x2, Pallas kernels, put(): pl.pallas_call(functools.partial(put_kernel, n, chunk, into is None), nam...  4.92 us
    pallas_call x2, Pallas kernels, pick(): pl.pallas_call(functools.partial(pick_kernel, n, chunk), name='pick', in_...  3.98 us
    ppermute x1, waiting for transfers between devices, on_device(): lax.ppermute(own, ('pair', 'core'), [(i, i ^ 3) for i in range(4)])  2.51 us
  transfers between devices with their start and end apart: 26, of which 14 were waited for; matrix products, arithmetic and copies ran while one was open for 5% of the time, Pallas kernels for 22%

profile of v5, /device:TPU:0, one launch (start us, length us, event | category | flops | bytes accessed | tf_op | source)
XLA Modules:
  0.0 122.6 jit_solution(17178267101002197075)
XLA Ops:
  0.6 2.0 %pick.2 = (bf16[2,256,256]{2,1,0:T(8,128)(2,1)}, bf16[2,256,256]{2,1,0:T(8,128)(2,1)}, bf16[2,256,256]{2,1,0:T(8,128)(2,1)}) custom-call(bf16[8,256,256]{2,1,0:T(8,128)(2,1)} %bitcast.73, bf16[8,256,256]{2,1,0:T(8,128)(2,1)} %bitcast.77), custom_call_target="tpu_custom_call" | custom-call | flops 1000 | bytes 1000 | tf_op jit(solution)/shard_map/pick/pallas_call | solution.py:96
  2.7 5.1 %collective-permute-start.2 = (bf16[2,256,256]{2,1,0:T(8,128)(2,1)}, bf16[2,256,256]{2,1,0:T(8,128)(2,1)S(1)}, u32[]{:S(2)}, u32[]{:S(2)}) collective-permute-start(bf16[2,256,256]{2,1,0:T(8,128)(2,1)} %get-tuple-element.56), channel_id=1, source_target_pairs={{0,12},{4,8},{8,4},{12,0},{1,13},{5,9},{9,5},{13,1},{2,14},{6,10},... | collective-permute-start | bytes 786440 | tf_op jit(solution)/shard_map/ppermute | solution.py:347
  7.8 0.6 collective-permute-start.1
  8.4 2.0 %pick.3 = (bf16[2,256,256]{2,1,0:T(8,128)(2,1)}, bf16[2,256,256]{2,1,0:T(8,128)(2,1)}, bf16[2,256,256]{2,1,0:T(8,128)(2,1)}) custom-call(bf16[8,256,256]{2,1,0:T(8,128)(2,1)} %bitcast.74, bf16[8,256,256]{2,1,0:T(8,128)(2,1)} %bitcast.78), custom_call_target="tpu_custom_call" | custom-call | flops 1000 | bytes 1000 | tf_op jit(solution)/shard_map/pick/pallas_call | solution.py:96
  10.4 1.5 %collective-permute-start.3 = (bf16[2,256,256]{2,1,0:T(8,128)(2,1)}, bf16[2,256,256]{2,1,0:T(8,128)(2,1)S(1)}, u32[]{:S(2)}, u32[]{:S(2)}) collective-permute-start(bf16[2,256,256]{2,1,0:T(8,128)(2,1)} %get-tuple-element.63), channel_id=1, source_target_pairs={{0,4},{4,0},{8,12},{12,8},{1,5},{5,1},{9,13},{13,9},{2,6},{6,2},{1... | collective-permute-start | bytes 786440 | tf_op jit(solution)/shard_map/ppermute | solution.py:347
  11.9 2.4 %collective-permute-start.5 = (bf16[2,256,256]{2,1,0:T(8,128)(2,1)}, bf16[2,256,256]{2,1,0:T(8,128)(2,1)S(1)}, u32[]{:S(2)}, u32[]{:S(2)}) collective-permute-start(bf16[2,256,256]{2,1,0:T(8,128)(2,1)} %get-tuple-element.65), channel_id=1, source_target_pairs={{0,12},{4,8},{8,4},{12,0},{1,13},{5,9},{9,5},{13,1},{2,14},{6,10},... | collective-permute-start | bytes 786440 | tf_op jit(solution)/shard_map/ppermute | solution.py:347
  14.3 0.9 collective-permute-done.2.refs_4_
  15.2 6.9 %collective-permute-start.4 = (bf16[2,256,256]{2,1,0:T(8,128)(2,1)}, bf16[2,256,256]{2,1,0:T(8,128)(2,1)S(1)}, u32[]{:S(2)}, u32[]{:S(2)}) collective-permute-start(bf16[2,256,256]{2,1,0:T(8,128)(2,1)} %get-tuple-element.64), channel_id=1, source_target_pairs={{0,8},{4,12},{8,0},{12,4},{1,9},{5,13},{9,1},{13,5},{2,10},{6,14},... | collective-permute-start | bytes 786440 | tf_op jit(solution)/shard_map/ppermute | solution.py:347
  22.1 0.9 copy.20
  23.1 0.9 copy.18
  24.0 0.8 copy.19
  24.8 0.8 copy.21
  25.5 6.6 %collective-permute-done.1.refs_3_ = bf16[2,256,256]{2,1,0:T(8,128)(2,1)S(1)} collective-permute-done((bf16[2,256,256]{2,1,0:T(8,128)(2,1)}, bf16[2,256,256]{2,1,0:T(8,128)(2,1)S(1)}, u32[]{:S(2)}, u32[]{:S(2)}) %collective-permute-start.1) | collective-permute-done | bytes 262176 | tf_op jit(solution)/shard_map/ppermute | solution.py:347
  32.2 0.7 copy-done.11
  32.8 10.2 %chunk.2 = (bf16[2,256,256]{2,1,0:T(8,128)(2,1)}, bf16[2,256,256]{2,1,0:T(8,128)(2,1)}, bf16[2,256,256]{2,1,0:T(8,128)(2,1)}, bf16[2,256,256]{2,1,0:T(8,128)(2,1)}, f32[8,256,256]{2,1,0:T(8,128)}) custom-call(bf16[8,256,256]{2,1,0:T(8,128)(2,1)} %bitcast.75, bf16[8,256,256]{2,1,0:T(8,128)(2,1)} %bitcast.79, bf16[2,256,256]{2,1,0:T(8,128)(2,1)} %copy-done.10, ...), custom_call_target="tpu_custom_call" | custom-call | flops 1000 | bytes 1000 | tf_op jit(solution)/shard_map/chunk/pallas_call | solution.py:315
  43.1 9.7 %collective-permute-done.4.refs_3_ = bf16[2,256,256]{2,1,0:T(8,128)(2,1)S(1)} collective-permute-done((bf16[2,256,256]{2,1,0:T(8,128)(2,1)}, bf16[2,256,256]{2,1,0:T(8,128)(2,1)S(1)}, u32[]{:S(2)}, u32[]{:S(2)}) %collective-permute-start.4) | collective-permute-done | bytes 262176 | tf_op jit(solution)/shard_map/ppermute | solution.py:347
  52.8 2.5 %collective-permute-start.10 = (bf16[2,256,256]{2,1,0:T(8,128)(2,1)}, bf16[2,256,256]{2,1,0:T(8,128)(2,1)S(1)}, u32[]{:S(2)}, u32[]{:S(2)}) collective-permute-start(bf16[2,256,256]{2,1,0:T(8,128)(2,1)} %get-tuple-element.76), channel_id=1, source_target_pairs={{0,12},{4,8},{8,4},{12,0},{1,13},{5,9},{9,5},{13,1},{2,14},{6,10},... | collective-permute-start | bytes 786440 | tf_op jit(solution)/shard_map/ppermute | solution.py:347
  55.3 10.7 %chunk.3 = (bf16[2,256,256]{2,1,0:T(8,128)(2,1)}, bf16[2,256,256]{2,1,0:T(8,128)(2,1)}, bf16[2,256,256]{2,1,0:T(8,128)(2,1)}, bf16[2,256,256]{2,1,0:T(8,128)(2,1...) custom-call(bf16[8,256,256]{2,1,0:T(8,128)(2,1)} %bitcast.76, bf16[8,256,256]{2,1,0:T(8,128)(2,1)} %bitcast.80, ...), custom_call_target="tpu_custom_call" | custom-call | flops 1000 | bytes 1000 | tf_op jit(solution)/shard_map/chunk/pallas_call | solution.py:315
  66.3 2.0 %collective-permute-done.11 = bf16[1024,256]{1,0:T(8,128)(2,1)S(1)} collective-permute-done((bf16[1024,256]{1,0:T(8,128)(2,1)}, bf16[1024,256]{1,0:T(8,128)(2,1)S(1)}, u32[]{:S(2)}, u32[]{:S(2)}) %collective-permute-start.11) | collective-permute-done | bytes 524320 | tf_op jit(solution)/shard_map/ppermute | solution.py:347
  68.3 1.4 %convert_add_fusion = f32[4,256,256]{2,1,0:T(8,128)S(1)} fusion(f32[4,256,256]{2,1,0:T(8,128)} %get-tuple-element.75, bf16[4,256,256]{2,1,0:T(8,128)(2,1)S(1)} %bitcast.100), kind=kLoop, calls=%fused_computation.1 | loop fusion | flops 524288 | bytes 2621440 | tf_op jit(solution)/shard_map/add | solution.py:430
  69.7 1.6 %collective-permute-start.12 = (bf16[128,256]{1,0:T(8,128)(2,1)S(1)}, bf16[128,256]{1,0:T(8,128)(2,1)S(1)}, u32[]{:S(2)}, u32[]{:S(2)}) collective-permute-start(bf16[128,256]{1,0:T(8,128)(2,1)S(1)} %get-tuple-element.105), channel_id=1, source_target_pairs={{0,2},{2,0},{1,3},{3,1},{4,6},{6,4},{5,7},{7,5},{8,10},{10,8},{9,1... | collective-permute-start | bytes 196616 | tf_op jit(solution)/shard_map/ppermute | solution.py:347
  71.3 0.5 collective-permute-start.13
  71.8 1.5 %collective-permute-start.14 = (bf16[128,256]{1,0:T(8,128)(2,1)S(1)}, bf16[128,256]{1,0:T(8,128)(2,1)S(1)}, u32[]{:S(2)}, u32[]{:S(2)}) collective-permute-start(bf16[128,256]{1,0:T(8,128)(2,1)S(1)} %get-tuple-element.107), channel_id=1, source_target_pairs={{0,2},{2,0},{1,3},{3,1},{4,6},{6,4},{5,7},{7,5},{8,10},{10,8},{9,1... | collective-permute-start | bytes 196616 | tf_op jit(solution)/shard_map/ppermute | solution.py:347
  73.4 0.5 collective-permute-start.15
  73.9 0.6 collective-permute-done.12
  74.5 1.3 %collective-permute-start.8 = (bf16[2,256,256]{2,1,0:T(8,128)(2,1)S(1)}, bf16[2,256,256]{2,1,0:T(8,128)(2,1)S(1)}, u32[]{:S(2)}, u32[]{:S(2)}) collective-permute-start(bf16[2,256,256]{2,1,0:T(8,128)(2,1)S(1)} %copy-done.15), channel_id=1, source_target_pairs={{0,12},{4,8},{8,4},{12,0},{1,13},{5,9},{9,5},{13,1},{2,14},{6,10},... | collective-permute-start | bytes 786440 | tf_op jit(solution)/shard_map/ppermute | solution.py:347
  75.8 0.5 collective-permute-done.13
  76.3 1.3 %collective-permute-done.14 = bf16[128,256]{1,0:T(8,128)(2,1)S(1)} collective-permute-done((bf16[128,256]{1,0:T(8,128)(2,1)S(1)}, bf16[128,256]{1,0:T(8,128)(2,1)S(1)}, u32[]{:S(2)}, u32[]{:S(2)}) %collective-permute-start.14) | collective-permute-done | bytes 65568 | tf_op jit(solution)/shard_map/ppermute | solution.py:347
  77.6 0.7 collective-permute-done.15
  78.4 7.9 %collective-permute-done.9.refs_2_ = bf16[2,256,256]{2,1,0:T(8,128)(2,1)S(1)} collective-permute-done((bf16[2,256,256]{2,1,0:T(8,128)(2,1)}, bf16[2,256,256]{2,1,0:T(8,128)(2,1)S(1)}, u32[]{:S(2)}, u32[]{:S(2)}) %collective-permute-start.9) | collective-permute-done | bytes 262176 | tf_op jit(solution)/shard_map/ppermute | solution.py:347
  86.4 2.8 %collective-permute-start.17 = (bf16[128,256]{1,0:T(8,128)(2,1)S(1)}, bf16[128,256]{1,0:T(8,128)(2,1)S(1)}, u32[]{:S(2)}, u32[]{:S(2)}) collective-permute-start(bf16[128,256]{1,0:T(8,128)(2,1)S(1)} %get-tuple-element.104), channel_id=1, source_target_pairs={{0,8},{4,12},{8,0},{12,4},{1,9},{5,13},{9,1},{13,5},{2,10},{6,14},... | collective-permute-start | bytes 196616 | tf_op jit(solution)/shard_map/ppermute | solution.py:347
  89.3 1.5 %collective-permute-start.18 = (bf16[128,256]{1,0:T(8,128)(2,1)S(1)}, bf16[128,256]{1,0:T(8,128)(2,1)S(1)}, u32[]{:S(2)}, u32[]{:S(2)}) collective-permute-start(bf16[128,256]{1,0:T(8,128)(2,1)S(1)} %get-tuple-element.103), channel_id=1, source_target_pairs={{0,12},{4,8},{8,4},{12,0},{1,13},{5,9},{9,5},{13,1},{2,14},{6,10},... | collective-permute-start | bytes 196616 | tf_op jit(solution)/shard_map/ppermute | solution.py:347
  90.8 2.4 %collective-permute-done.16 = bf16[128,256]{1,0:T(8,128)(2,1)S(1)} collective-permute-done((bf16[128,256]{1,0:T(8,128)(2,1)S(1)}, bf16[128,256]{1,0:T(8,128)(2,1)S(1)}, u32[]{:S(2)}, u32[]{:S(2)}) %collective-permute-start.16) | collective-permute-done | bytes 65568 | tf_op jit(solution)/shard_map/ppermute | solution.py:347
  93.2 2.9 %collective-permute-done.17 = bf16[128,256]{1,0:T(8,128)(2,1)S(1)} collective-permute-done((bf16[128,256]{1,0:T(8,128)(2,1)S(1)}, bf16[128,256]{1,0:T(8,128)(2,1)S(1)}, u32[]{:S(2)}, u32[]{:S(2)}) %collective-permute-start.17) | collective-permute-done | bytes 65568 | tf_op jit(solution)/shard_map/ppermute | solution.py:347
  96.2 2.0 %collective-permute-start.20 = (bf16[128,256]{1,0:T(8,128)(2,1)S(1)}, bf16[128,256]{1,0:T(8,128)(2,1)S(1)}, u32[]{:S(2)}, u32[]{:S(2)}) collective-permute-start(bf16[128,256]{1,0:T(8,128)(2,1)S(1)} %fusion.3), channel_id=1, source_target_pairs={{0,4},{4,0},{8,12},{12,8},{1,5},{5,1},{9,13},{13,9},{2,6},{6,2},{1... | collective-permute-start | bytes 196616 | tf_op jit(solution)/shard_map/ppermute | solution.py:347
  98.2 0.9 collective-permute-start.21
  99.1 1.5 %collective-permute-start.22 = (bf16[128,256]{1,0:T(8,128)(2,1)S(1)}, bf16[128,256]{1,0:T(8,128)(2,1)S(1)}, u32[]{:S(2)}, u32[]{:S(2)}) collective-permute-start(bf16[128,256]{1,0:T(8,128)(2,1)S(1)} %fusion.3), channel_id=1, source_target_pairs={{0,12},{4,8},{8,4},{12,0},{1,13},{5,9},{9,5},{13,1},{2,14},{6,10},... | collective-permute-start | bytes 196616 | tf_op jit(solution)/shard_map/ppermute | solution.py:347
  100.7 1.1 collective-permute-start.6
  101.7 1.8 %collective-permute-start.7 = (bf16[2,256,256]{2,1,0:T(8,128)(2,1)S(1)}, bf16[2,256,256]{2,1,0:T(8,128)(2,1)S(1)}, u32[]{:S(2)}, u32[]{:S(2)}) collective-permute-start(bf16[2,256,256]{2,1,0:T(8,128)(2,1)S(1)} %copy-done.12), channel_id=1, source_target_pairs={{0,8},{4,12},{8,0},{12,4},{1,9},{5,13},{9,1},{13,5},{2,10},{6,14},... | collective-permute-start | bytes 786440 | tf_op jit(solution)/shard_map/ppermute | solution.py:347
  103.6 2.8 %collective-permute-done.21 = bf16[128,256]{1,0:T(8,128)(2,1)S(1)} collective-permute-done((bf16[128,256]{1,0:T(8,128)(2,1)S(1)}, bf16[128,256]{1,0:T(8,128)(2,1)S(1)}, u32[]{:S(2)}, u32[]{:S(2)}) %collective-permute-start.21) | collective-permute-done | bytes 65568 | tf_op jit(solution)/shard_map/ppermute | solution.py:347
  106.4 0.6 gather_fusion
  107.1 1.6 %collective-permute-start.23 = (bf16[512,256]{1,0:T(8,128)(2,1)S(1)}, bf16[512,256]{1,0:T(8,128)(2,1)S(1)}, u32[]{:S(2)}, u32[]{:S(2)}) collective-permute-start(bf16[512,256]{1,0:T(8,128)(2,1)S(1)} %bitcast_select_fusion), channel_id=1, source_target_pairs={{0,2},{2,0},{1,3},{3,1},{4,6},{6,4},{5,7},{7,5},{8,10},{10,8},{9,1... | collective-permute-start | bytes 786440 | tf_op jit(solution)/shard_map/ppermute | solution.py:347
  108.7 0.6 collective-permute-start.25
  109.4 2.5 %put.2 = (bf16[8,256,256]{2,1,0:T(8,128)(2,1)}, bf16[8,256,256]{2,1,0:T(8,128)(2,1)}) custom-call(bf16[2,256,256]{2,1,0:T(8,128)(2,1)S(1)} %copy-done.1, bf16[2,256,256]{2,1,0:T(8,128)(2,1)S(1)} %collective-permute-done.19.refs_1_, bf16[2,256,256]{2,1,0:T(8,128)(2,1)S(1)} %collective-permute-done.9.refs_2_, ...), custom_call_target="tpu_custom_call" | custom-call | bytes 4194304 | tf_op jit(solution)/shard_map/put/pallas_call | solution.py:123
  112.0 4.0 %collective-permute-done.23 = bf16[512,256]{1,0:T(8,128)(2,1)S(1)} collective-permute-done((bf16[512,256]{1,0:T(8,128)(2,1)S(1)}, bf16[512,256]{1,0:T(8,128)(2,1)S(1)}, u32[]{:S(2)}, u32[]{:S(2)}) %collective-permute-start.23) | collective-permute-done | bytes 262176 | tf_op jit(solution)/shard_map/ppermute | solution.py:347
  116.0 2.5 %collective-permute-done.25 = bf16[512,256]{1,0:T(8,128)(2,1)S(1)} collective-permute-done((bf16[512,256]{1,0:T(8,128)(2,1)S(1)}, bf16[512,256]{1,0:T(8,128)(2,1)S(1)}, u32[]{:S(2)}, u32[]{:S(2)}) %collective-permute-start.25) | collective-permute-done | bytes 262176 | tf_op jit(solution)/shard_map/ppermute | solution.py:446
  118.5 1.5 %finish.1 = (f32[3,256,256]{2,1,0:T(8,128)}, f32[3,256,256]{2,1,0:T(8,128)}, f32[256,256]{1,0:T(8,128)}, f32[256,256]{1,0:T(8,128)}) custom-call(bf16[2,256,256]{2,1,0:T(8,128)(2,1)S(1)} %bitcast_select_fusion.1.own, bf16[2,256,256]{2,1,0:T(8,128)(2,1)S(1)} %bitcast.70, bf16[2,256,256]{2,1,0:T(8,128)(2,1)S(1)} %bitcast.71, bf16[2,256,256]{2,1,0:T(8,128)(2,1)S(1)} %bitcast.72), custom_call_target="tpu_custom_call" | custom-call | flops 1000 | bytes 1000 | tf_op jit(solution)/shard_map/finish/pallas_call | solution.py:167
  120.0 2.5 %put.3 = (bf16[8,256,256]{2,1,0:T(8,128)(2,1)}, bf16[8,256,256]{2,1,0:T(8,128)(2,1)}) custom-call(bf16[2,256,256]{2,1,0:T(8,128)(2,1)S(1)} %copy-done, bf16[2,256,256]{2,1,0:T(8,128)(2,1)S(1)} %collective-permute-done.6.refs_1_, bf16[2,256,256]{2,1,0:T(8,128)(2,1)S(1)} %collective-permute-done.7.refs_2_, ...), custom_call_target="tpu_custom_call", output_to_operand_aliasing={{0}: (4, {}), {1}: (5, {})} | custom-call | bytes 4194304 | tf_op jit(solution)/shard_map/put/pallas_call | solution.py:123
  (69 shorter events, 1.1 us)
Async XLA Ops:
  0.6 21.5 %copy-start.3 = (bf16[3,256,256]{2,1,0:T(8,128)(2,1)S(1)}, bf16[3,256,256]{2,1,0:T(8,128)(2,1)}, u32[]{:S(2)}) copy-start(bf16[3,256,256]{2,1,0:T(8,128)(2,1)} %param.13) | copy-start | bytes 1179652
  2.7 20.4 %copy-start.2 = (bf16[3,256,256]{2,1,0:T(8,128)(2,1)S(1)}, bf16[3,256,256]{2,1,0:T(8,128)(2,1)}, u32[]{:S(2)}) copy-start(bf16[3,256,256]{2,1,0:T(8,128)(2,1)} %param.12) | copy-start | bytes 1179652
  2.7 12.5 %collective-permute-start.2 = (bf16[2,256,256]{2,1,0:T(8,128)(2,1)}, bf16[2,256,256]{2,1,0:T(8,128)(2,1)S(1)}, u32[]{:S(2)}, u32[]{:S(2)}) collective-permute-start(bf16[2,256,256]{2,1,0:T(8,128)(2,1)} %get-tuple-element.56), channel_id=1, source_target_pairs={{0,12},{4,8},{8,4},{12,0},{1,13},{5,9},{9,5},{13,1},{2,14},{6,10},... | collective-permute-start | bytes 786440 | tf_op jit(solution)/shard_map/ppermute | solution.py:347
  7.8 17.7 %collective-permute-start = (bf16[2,256,256]{2,1,0:T(8,128)(2,1)}, bf16[2,256,256]{2,1,0:T(8,128)(2,1)S(1)}, u32[]{:S(2)}, u32[]{:S(2)}) collective-permute-start(bf16[2,256,256]{2,1,0:T(8,128)(2,1)} %get-tuple-element.54), channel_id=1, source_target_pairs={{0,4},{4,0},{8,12},{12,8},{1,5},{5,1},{9,13},{13,9},{2,6},{6,2},{1... | collective-permute-start | bytes 786440 | tf_op jit(solution)/shard_map/ppermute | solution.py:347
  7.8 24.4 %collective-permute-start.1 = (bf16[2,256,256]{2,1,0:T(8,128)(2,1)}, bf16[2,256,256]{2,1,0:T(8,128)(2,1)S(1)}, u32[]{:S(2)}, u32[]{:S(2)}) collective-permute-start(bf16[2,256,256]{2,1,0:T(8,128)(2,1)} %get-tuple-element.55), channel_id=1, source_target_pairs={{0,8},{4,12},{8,0},{12,4},{1,9},{5,13},{9,1},{13,5},{2,10},{6,14},... | collective-permute-start | bytes 786440 | tf_op jit(solution)/shard_map/ppermute | solution.py:347
  10.4 13.6 %copy-start.4 = (bf16[256,256]{1,0:T(8,128)(2,1)S(1)}, bf16[256,256]{1,0:T(8,128)(2,1)}, u32[]{:S(2)}) copy-start(bf16[256,256]{1,0:T(8,128)(2,1)} %refs_7_.3) | copy-start | bytes 393220
  10.4 14.3 %copy-start.5 = (bf16[256,256]{1,0:T(8,128)(2,1)S(1)}, bf16[256,256]{1,0:T(8,128)(2,1)}, u32[]{:S(2)}) copy-start(bf16[256,256]{1,0:T(8,128)(2,1)} %refs_11_.3) | copy-start | bytes 393220
  10.4 32.7 %collective-permute-start.3 = (bf16[2,256,256]{2,1,0:T(8,128)(2,1)}, bf16[2,256,256]{2,1,0:T(8,128)(2,1)S(1)}, u32[]{:S(2)}, u32[]{:S(2)}) collective-permute-start(bf16[2,256,256]{2,1,0:T(8,128)(2,1)} %get-tuple-element.63), channel_id=1, source_target_pairs={{0,4},{4,0},{8,12},{12,8},{1,5},{5,1},{9,13},{13,9},{2,6},{6,2},{1... | collective-permute-start | bytes 786440 | tf_op jit(solution)/shard_map/ppermute | solution.py:347
  11.9 31.2 %collective-permute-start.5 = (bf16[2,256,256]{2,1,0:T(8,128)(2,1)}, bf16[2,256,256]{2,1,0:T(8,128)(2,1)S(1)}, u32[]{:S(2)}, u32[]{:S(2)}) collective-permute-start(bf16[2,256,256]{2,1,0:T(8,128)(2,1)} %get-tuple-element.65), channel_id=1, source_target_pairs={{0,12},{4,8},{8,4},{12,0},{1,13},{5,9},{9,5},{13,1},{2,14},{6,10},... | collective-permute-start | bytes 786440 | tf_op jit(solution)/shard_map/ppermute | solution.py:347
  15.2 16.9 %copy-start.8 = (bf16[2,256,256]{2,1,0:T(8,128)(2,1)}, bf16[2,256,256]{2,1,0:T(8,128)(2,1)S(1)}, u32[]{:S(2)}) copy-start(bf16[2,256,256]{2,1,0:T(8,128)(2,1)S(1)} %collective-permute-done.2.refs_4_) | copy-start | bytes 786436
  15.2 37.6 %collective-permute-start.4 = (bf16[2,256,256]{2,1,0:T(8,128)(2,1)}, bf16[2,256,256]{2,1,0:T(8,128)(2,1)S(1)}, u32[]{:S(2)}, u32[]{:S(2)}) collective-permute-start(bf16[2,256,256]{2,1,0:T(8,128)(2,1)} %get-tuple-element.64), channel_id=1, source_target_pairs={{0,8},{4,12},{8,0},{12,4},{1,9},{5,13},{9,1},{13,5},{2,10},{6,14},... | collective-permute-start | bytes 786440 | tf_op jit(solution)/shard_map/ppermute | solution.py:347
  25.5 6.6 %copy-start.10 = (bf16[2,256,256]{2,1,0:T(8,128)(2,1)}, bf16[2,256,256]{2,1,0:T(8,128)(2,1)S(1)}, u32[]{:S(2)}) copy-start(bf16[2,256,256]{2,1,0:T(8,128)(2,1)S(1)} %collective-permute-done.refs_2_) | copy-start | bytes 786436
  32.2 0.7 copy-start.11
  43.1 12.2 %copy-start.6 = (bf16[2,256,256]{2,1,0:T(8,128)(2,1)}, bf16[2,256,256]{2,1,0:T(8,128)(2,1)S(1)}, u32[]{:S(2)}) copy-start(bf16[2,256,256]{2,1,0:T(8,128)(2,1)S(1)} %collective-permute-done.3.refs_2_) | copy-start | bytes 786436
  43.1 12.2 %copy-start.7 = (bf16[2,256,256]{2,1,0:T(8,128)(2,1)}, bf16[2,256,256]{2,1,0:T(8,128)(2,1)S(1)}, u32[]{:S(2)}) copy-start(bf16[2,256,256]{2,1,0:T(8,128)(2,1)S(1)} %collective-permute-done.5.refs_4_) | copy-start | bytes 786436
  52.8 2.5 %copy-start.9 = (bf16[2,256,256]{2,1,0:T(8,128)(2,1)}, bf16[2,256,256]{2,1,0:T(8,128)(2,1)S(1)}, u32[]{:S(2)}) copy-start(bf16[2,256,256]{2,1,0:T(8,128)(2,1)S(1)} %collective-permute-done.4.refs_3_) | copy-start | bytes 786436
  52.8 13.2 %collective-permute-start.10 = (bf16[2,256,256]{2,1,0:T(8,128)(2,1)}, bf16[2,256,256]{2,1,0:T(8,128)(2,1)S(1)}, u32[]{:S(2)}, u32[]{:S(2)}) collective-permute-start(bf16[2,256,256]{2,1,0:T(8,128)(2,1)} %get-tuple-element.76), channel_id=1, source_target_pairs={{0,12},{4,8},{8,4},{12,0},{1,13},{5,9},{9,5},{13,1},{2,14},{6,10},... | collective-permute-start | bytes 786440 | tf_op jit(solution)/shard_map/ppermute | solution.py:347
  66.1 2.2 %collective-permute-start.11 = (bf16[1024,256]{1,0:T(8,128)(2,1)}, bf16[1024,256]{1,0:T(8,128)(2,1)S(1)}, u32[]{:S(2)}, u32[]{:S(2)}) collective-permute-start(bf16[1024,256]{1,0:T(8,128)(2,1)} %bitcast.114), channel_id=1, source_target_pairs={{0,1},{1,0},{2,3},{3,2},{4,5},{5,4},{6,7},{7,6},{8,9},{9,8},{10,11... | collective-permute-start | bytes 1572872 | tf_op jit(solution)/shard_map/ppermute | solution.py:347
  66.3 20.0 %collective-permute-start.9 = (bf16[2,256,256]{2,1,0:T(8,128)(2,1)}, bf16[2,256,256]{2,1,0:T(8,128)(2,1)S(1)}, u32[]{:S(2)}, u32[]{:S(2)}) collective-permute-start(bf16[2,256,256]{2,1,0:T(8,128)(2,1)} %get-tuple-element.74), channel_id=1, source_target_pairs={{0,8},{4,12},{8,0},{12,4},{1,9},{5,13},{9,1},{13,5},{2,10},{6,14},... | collective-permute-start | bytes 786440 | tf_op jit(solution)/shard_map/ppermute | solution.py:347
  68.3 6.2 %copy-start.15 = (bf16[2,256,256]{2,1,0:T(8,128)(2,1)S(1)}, bf16[2,256,256]{2,1,0:T(8,128)(2,1)}, u32[]{:S(2)}) copy-start(bf16[2,256,256]{2,1,0:T(8,128)(2,1)} %get-tuple-element.73) | copy-start | bytes 786436
  68.3 8.1 %copy-start.14 = (bf16[2,256,256]{2,1,0:T(8,128)(2,1)S(1)}, bf16[2,256,256]{2,1,0:T(8,128)(2,1)}, u32[]{:S(2)}) copy-start(bf16[2,256,256]{2,1,0:T(8,128)(2,1)} %get-tuple-element.81) | copy-start | bytes 786436
  69.7 4.7 %collective-permute-start.12 = (bf16[128,256]{1,0:T(8,128)(2,1)S(1)}, bf16[128,256]{1,0:T(8,128)(2,1)S(1)}, u32[]{:S(2)}, u32[]{:S(2)}) collective-permute-start(bf16[128,256]{1,0:T(8,128)(2,1)S(1)} %get-tuple-element.105), channel_id=1, source_target_pairs={{0,2},{2,0},{1,3},{3,1},{4,6},{6,4},{5,7},{7,5},{8,10},{10,8},{9,1... | collective-permute-start | bytes 196616 | tf_op jit(solution)/shard_map/ppermute | solution.py:347
  71.3 5.0 %collective-permute-start.13 = (bf16[128,256]{1,0:T(8,128)(2,1)S(1)}, bf16[128,256]{1,0:T(8,128)(2,1)S(1)}, u32[]{:S(2)}, u32[]{:S(2)}) collective-permute-start(bf16[128,256]{1,0:T(8,128)(2,1)S(1)} %get-tuple-element.108), channel_id=1, source_target_pairs={{0,2},{2,0},{1,3},{3,1},{4,6},{6,4},{5,7},{7,5},{8,10},{10,8},{9,1... | collective-permute-start | bytes 196616 | tf_op jit(solution)/shard_map/ppermute | solution.py:347
  71.8 5.8 %collective-permute-start.14 = (bf16[128,256]{1,0:T(8,128)(2,1)S(1)}, bf16[128,256]{1,0:T(8,128)(2,1)S(1)}, u32[]{:S(2)}, u32[]{:S(2)}) collective-permute-start(bf16[128,256]{1,0:T(8,128)(2,1)S(1)} %get-tuple-element.107), channel_id=1, source_target_pairs={{0,2},{2,0},{1,3},{3,1},{4,6},{6,4},{5,7},{7,5},{8,10},{10,8},{9,1... | collective-permute-start | bytes 196616 | tf_op jit(solution)/shard_map/ppermute | solution.py:347
  73.4 27.3 %copy-start.13 = (bf16[2,256,256]{2,1,0:T(8,128)(2,1)S(1)}, bf16[2,256,256]{2,1,0:T(8,128)(2,1)}, u32[]{:S(2)}) copy-start(bf16[2,256,256]{2,1,0:T(8,128)(2,1)} %get-tuple-element.71) | copy-start | bytes 786436
  73.4 28.4 %copy-start.12 = (bf16[2,256,256]{2,1,0:T(8,128)(2,1)S(1)}, bf16[2,256,256]{2,1,0:T(8,128)(2,1)}, u32[]{:S(2)}) copy-start(bf16[2,256,256]{2,1,0:T(8,128)(2,1)} %get-tuple-element.72) | copy-start | bytes 786436
  73.4 4.9 %collective-permute-start.15 = (bf16[128,256]{1,0:T(8,128)(2,1)S(1)}, bf16[128,256]{1,0:T(8,128)(2,1)S(1)}, u32[]{:S(2)}, u32[]{:S(2)}) collective-permute-start(bf16[128,256]{1,0:T(8,128)(2,1)S(1)} %get-tuple-element.106), channel_id=1, source_target_pairs={{0,2},{2,0},{1,3},{3,1},{4,6},{6,4},{5,7},{7,5},{8,10},{10,8},{9,1... | collective-permute-start | bytes 196616 | tf_op jit(solution)/shard_map/ppermute | solution.py:347
  74.5 21.7 %collective-permute-start.8 = (bf16[2,256,256]{2,1,0:T(8,128)(2,1)S(1)}, bf16[2,256,256]{2,1,0:T(8,128)(2,1)S(1)}, u32[]{:S(2)}, u32[]{:S(2)}) collective-permute-start(bf16[2,256,256]{2,1,0:T(8,128)(2,1)S(1)} %copy-done.15), channel_id=1, source_target_pairs={{0,12},{4,8},{8,4},{12,0},{1,13},{5,9},{9,5},{13,1},{2,14},{6,10},... | collective-permute-start | bytes 786440 | tf_op jit(solution)/shard_map/ppermute | solution.py:347
  76.3 19.8 %collective-permute-start.19 = (bf16[2,256,256]{2,1,0:T(8,128)(2,1)S(1)}, bf16[2,256,256]{2,1,0:T(8,128)(2,1)S(1)}, u32[]{:S(2)}, u32[]{:S(2)}) collective-permute-start(bf16[2,256,256]{2,1,0:T(8,128)(2,1)S(1)} %copy-done.14), channel_id=1, source_target_pairs={{0,4},{4,0},{8,12},{12,8},{1,5},{5,1},{9,13},{13,9},{2,6},{6,2},{1... | collective-permute-start | bytes 786440 | tf_op jit(solution)/shard_map/ppermute | solution.py:347
  78.3 31.1 %copy-start.1 = (bf16[2,256,256]{2,1,0:T(8,128)(2,1)S(1)}, bf16[2,256,256]{2,1,0:T(8,128)(2,1)}, u32[]{:S(2)}) copy-start(bf16[2,256,256]{2,1,0:T(8,128)(2,1)} %get-tuple-element.88.refs_0_) | copy-start | bytes 786436
  86.4 6.9 %collective-permute-start.16 = (bf16[128,256]{1,0:T(8,128)(2,1)S(1)}, bf16[128,256]{1,0:T(8,128)(2,1)S(1)}, u32[]{:S(2)}, u32[]{:S(2)}) collective-permute-start(bf16[128,256]{1,0:T(8,128)(2,1)S(1)} %get-tuple-element.102), channel_id=1, source_target_pairs={{0,4},{4,0},{8,12},{12,8},{1,5},{5,1},{9,13},{13,9},{2,6},{6,2},{1... | collective-permute-start | bytes 196616 | tf_op jit(solution)/shard_map/ppermute | solution.py:347
  86.4 9.7 %collective-permute-start.17 = (bf16[128,256]{1,0:T(8,128)(2,1)S(1)}, bf16[128,256]{1,0:T(8,128)(2,1)S(1)}, u32[]{:S(2)}, u32[]{:S(2)}) collective-permute-start(bf16[128,256]{1,0:T(8,128)(2,1)S(1)} %get-tuple-element.104), channel_id=1, source_target_pairs={{0,8},{4,12},{8,0},{12,4},{1,9},{5,13},{9,1},{13,5},{2,10},{6,14},... | collective-permute-start | bytes 196616 | tf_op jit(solution)/shard_map/ppermute | solution.py:347
  89.3 6.8 %collective-permute-start.18 = (bf16[128,256]{1,0:T(8,128)(2,1)S(1)}, bf16[128,256]{1,0:T(8,128)(2,1)S(1)}, u32[]{:S(2)}, u32[]{:S(2)}) collective-permute-start(bf16[128,256]{1,0:T(8,128)(2,1)S(1)} %get-tuple-element.103), channel_id=1, source_target_pairs={{0,12},{4,8},{8,4},{12,0},{1,13},{5,9},{9,5},{13,1},{2,14},{6,10},... | collective-permute-start | bytes 196616 | tf_op jit(solution)/shard_map/ppermute | solution.py:347
  96.2 7.4 %collective-permute-start.20 = (bf16[128,256]{1,0:T(8,128)(2,1)S(1)}, bf16[128,256]{1,0:T(8,128)(2,1)S(1)}, u32[]{:S(2)}, u32[]{:S(2)}) collective-permute-start(bf16[128,256]{1,0:T(8,128)(2,1)S(1)} %fusion.3), channel_id=1, source_target_pairs={{0,4},{4,0},{8,12},{12,8},{1,5},{5,1},{9,13},{13,9},{2,6},{6,2},{1... | collective-permute-start | bytes 196616 | tf_op jit(solution)/shard_map/ppermute | solution.py:347
  98.2 8.2 %collective-permute-start.21 = (bf16[128,256]{1,0:T(8,128)(2,1)S(1)}, bf16[128,256]{1,0:T(8,128)(2,1)S(1)}, u32[]{:S(2)}, u32[]{:S(2)}) collective-permute-start(bf16[128,256]{1,0:T(8,128)(2,1)S(1)} %fusion.3), channel_id=1, source_target_pairs={{0,8},{4,12},{8,0},{12,4},{1,9},{5,13},{9,1},{13,5},{2,10},{6,14},... | collective-permute-start | bytes 196616 | tf_op jit(solution)/shard_map/ppermute | solution.py:347
  99.1 7.3 %collective-permute-start.22 = (bf16[128,256]{1,0:T(8,128)(2,1)S(1)}, bf16[128,256]{1,0:T(8,128)(2,1)S(1)}, u32[]{:S(2)}, u32[]{:S(2)}) collective-permute-start(bf16[128,256]{1,0:T(8,128)(2,1)S(1)} %fusion.3), channel_id=1, source_target_pairs={{0,12},{4,8},{8,4},{12,0},{1,13},{5,9},{9,5},{13,1},{2,14},{6,10},... | collective-permute-start | bytes 196616 | tf_op jit(solution)/shard_map/ppermute | solution.py:347
  100.7 19.3 %collective-permute-start.6 = (bf16[2,256,256]{2,1,0:T(8,128)(2,1)S(1)}, bf16[2,256,256]{2,1,0:T(8,128)(2,1)S(1)}, u32[]{:S(2)}, u32[]{:S(2)}) collective-permute-start(bf16[2,256,256]{2,1,0:T(8,128)(2,1)S(1)} %copy-done.13), channel_id=1, source_target_pairs={{0,4},{4,0},{8,12},{12,8},{1,5},{5,1},{9,13},{13,9},{2,6},{6,2},{1... | collective-permute-start | bytes 786440 | tf_op jit(solution)/shard_map/ppermute | solution.py:347
  101.7 18.2 %collective-permute-start.7 = (bf16[2,256,256]{2,1,0:T(8,128)(2,1)S(1)}, bf16[2,256,256]{2,1,0:T(8,128)(2,1)S(1)}, u32[]{:S(2)}, u32[]{:S(2)}) collective-permute-start(bf16[2,256,256]{2,1,0:T(8,128)(2,1)S(1)} %copy-done.12), channel_id=1, source_target_pairs={{0,8},{4,12},{8,0},{12,4},{1,9},{5,13},{9,1},{13,5},{2,10},{6,14},... | collective-permute-start | bytes 786440 | tf_op jit(solution)/shard_map/ppermute | solution.py:347
  106.4 13.6 %copy-start = (bf16[2,256,256]{2,1,0:T(8,128)(2,1)S(1)}, bf16[2,256,256]{2,1,0:T(8,128)(2,1)}, u32[]{:S(2)}) copy-start(bf16[2,256,256]{2,1,0:T(8,128)(2,1)} %get-tuple-element.70.refs_0_) | copy-start | bytes 786436
  107.1 8.9 %collective-permute-start.23 = (bf16[512,256]{1,0:T(8,128)(2,1)S(1)}, bf16[512,256]{1,0:T(8,128)(2,1)S(1)}, u32[]{:S(2)}, u32[]{:S(2)}) collective-permute-start(bf16[512,256]{1,0:T(8,128)(2,1)S(1)} %bitcast_select_fusion), channel_id=1, source_target_pairs={{0,2},{2,0},{1,3},{3,1},{4,6},{6,4},{5,7},{7,5},{8,10},{10,8},{9,1... | collective-permute-start | bytes 786440 | tf_op jit(solution)/shard_map/ppermute | solution.py:347
  108.7 7.3 %collective-permute-start.24 = (bf16[512,256]{1,0:T(8,128)(2,1)S(1)}, bf16[512,256]{1,0:T(8,128)(2,1)S(1)}, u32[]{:S(2)}, u32[]{:S(2)}) collective-permute-start(bf16[512,256]{1,0:T(8,128)(2,1)S(1)} %bitcast_select_fusion), channel_id=1, source_target_pairs={{0,1},{1,0},{2,3},{3,2},{4,5},{5,4},{6,7},{7,6},{8,9},{9,8},{10,11... | collective-permute-start | bytes 786440 | tf_op jit(solution)/shard_map/ppermute | solution.py:347
  108.7 9.8 %collective-permute-start.25 = (bf16[512,256]{1,0:T(8,128)(2,1)S(1)}, bf16[512,256]{1,0:T(8,128)(2,1)S(1)}, u32[]{:S(2)}, u32[]{:S(2)}) collective-permute-start(bf16[512,256]{1,0:T(8,128)(2,1)S(1)} %bitcast_select_fusion), channel_id=1, source_target_pairs={{0,3},{1,2},{2,1},{3,0},{4,7},{5,6},{6,5},{7,4},{8,11},{9,10},{10,... | collective-permute-start | bytes 786440 | tf_op jit(solution)/shard_map/ppermute | solution.py:446

commit v6 on v5

--- a/solution.py
+++ b/solution.py
@@ -79,29 +79,29 @@
     wait_all(out)
 
 
-def pick_kernel(n, chunk, inputs, cotangent, *refs):
+def pick_kernel(n, chunk, order, inputs, cotangent, *refs):
     pieces, (held, sems) = refs[:-2], refs[-2:]
     me = lax.axis_index("chain")
     moves = [
-        (source.at[chunk * n + (me ^ s)], pieces[s - 1].at[k])
-        for s in reversed(range(1, n))
+        (source.at[chunk * n + (me ^ s)], pieces[i].at[k])
+        for i, s in enumerate(order)
         for k, source in enumerate((inputs, cotangent))
     ]
     stage(moves, held, sems)
 
 
-def pick(inputs, cotangent, n, chunk):
+def pick(inputs, cotangent, n, chunk, order):
     _, rows, width = inputs.shape
     piece = jax.ShapeDtypeStruct((2, rows, width), BF16)
     return pl.pallas_call(
-        functools.partial(pick_kernel, n, chunk),
+        functools.partial(pick_kernel, n, chunk, order),
         name="pick",
         in_specs=in_place(2),
-        out_specs=in_place(n - 1),
-        out_shape=[piece] * (n - 1),
+        out_specs=in_place(len(order)),
+        out_shape=[piece] * len(order),
         scratch_shapes=[
-            pltpu.VMEM((2 * (n - 1), rows, width), BF16),
-            pltpu.SemaphoreType.DMA((2, 2 * (n - 1))),
+            pltpu.VMEM((2 * len(order), rows, width), BF16),
+            pltpu.SemaphoreType.DMA((2, 2 * len(order))),
         ],
         cost_estimate=small_cost(),
     )(inputs, cotangent)
@@ -394,11 +394,15 @@
     )
     order = [s for part in (far, middle, near) for s in reversed(part)]
 
-    picked = [pick(inputs, cotangent, n, chunk) for chunk in range(CHUNKS)]
-    first = {s: swap(picked[0][s - 1], "chain", s) for s in order}
+    picked = [
+        dict(zip(part, pick(inputs, cotangent, n, chunk, part)))
+        for chunk, part in ((0, order[:third]), (0, order[third:]), (1, order))
+    ]
+    picked = [{**picked[0], **picked[1]}, picked[2]]
+    first = {s: swap(picked[0][s], "chain", s) for s in order}
     second = {}
     for s in order:
-        block = picked[1][s - 1]
+        block = picked[1][s]
         if s in middle:
             partner = s + third
             first[partner], block = lax.optimization_barrier((first[partner], block))

time: 123 us -> 123 us (level)
  Pallas kernels: 31.3 us -> 32.8 us
    pallas_call x2 -> x3, Pallas kernels: 3.98 us -> 5.44 us  [pick(): pl.pallas_call(functools.partial(pick_kernel, n, chunk, order), name='pic...]
  transfers between devices with their start and end apart: 26 -> 26, of which waited for: 14 -> 13; matrix products, arithmetic and copies ran while one was open for 5% -> 5% of each run, Pallas kernels for 22% -> 23%
where the time goes in v6:
time: 123 us; the launch traced here: 122 us
  waiting for transfers between devices  43.6 us (35%)
  starting transfers between devices  37.6 us (31%)
  Pallas kernels  32.8 us (27%)
  local copies, waits for them, and re-layouts  4.99 us (4%)
  other arithmetic  1.88 us (2%)
    ppermute x25, waiting for transfers between devices, swap(): lax.ppermute(values, axis, [(i, i ^ s) for i in range(lax.axis_size(axis))])  41.1 us
    ppermute x25, starting transfers between devices, swap(): lax.ppermute(values, axis, [(i, i ^ s) for i in range(lax.axis_size(axis))])  37 us
    pallas_call x2, Pallas kernels, run_chunk(): pl.pallas_call(functools.partial(chunk_kernel, n, hops, chunk, last), nam...  21 us
    pallas_call x3, Pallas kernels, pick(): pl.pallas_call(functools.partial(pick_kernel, n, chunk, order), name='pic...  5.44 us
    pallas_call x2, Pallas kernels, put(): pl.pallas_call(functools.partial(put_kernel, n, chunk, into is None), nam...  4.92 us
    ppermute x1, waiting for transfers between devices, on_device(): lax.ppermute(own, ('pair', 'core'), [(i, i ^ 3) for i in range(4)])  2.49 us
  transfers between devices with their start and end apart: 26, of which 13 were waited for; matrix products, arithmetic and copies ran while one was open for 5% of the time, Pallas kernels for 23%

profile of v6, /device:TPU:0, one launch (start us, length us, event | category | flops | bytes accessed | tf_op | source)
XLA Modules:
  0.0 122.1 jit_solution(180713402004447796)
XLA Ops:
  0.6 1.7 %pick.4 = bf16[2,256,256]{2,1,0:T(8,128)(2,1)} custom-call(bf16[8,256,256]{2,1,0:T(8,128)(2,1)} %bitcast.73, bf16[8,256,256]{2,1,0:T(8,128)(2,1)} %bitcast.78), custom_call_target="tpu_custom_call" | custom-call | flops 1000 | bytes 1000 | tf_op jit(solution)/shard_map/pick/pallas_call | solution.py:96
  2.3 5.1 %collective-permute-start.2 = (bf16[2,256,256]{2,1,0:T(8,128)(2,1)}, bf16[2,256,256]{2,1,0:T(8,128)(2,1)S(1)}, u32[]{:S(2)}, u32[]{:S(2)}) collective-permute-start(bf16[2,256,256]{2,1,0:T(8,128)(2,1)} %pick.4), channel_id=1, source_target_pairs={{0,12},{4,8},{8,4},{12,0},{1,13},{5,9},{9,5},{13,1},{2,14},{6,10},... | collective-permute-start | bytes 786440 | tf_op jit(solution)/shard_map/ppermute | solution.py:347
  7.4 1.8 %pick.3 = (bf16[2,256,256]{2,1,0:T(8,128)(2,1)}, bf16[2,256,256]{2,1,0:T(8,128)(2,1)}) custom-call(bf16[8,256,256]{2,1,0:T(8,128)(2,1)} %bitcast.74, bf16[8,256,256]{2,1,0:T(8,128)(2,1)} %bitcast.79), custom_call_target="tpu_custom_call" | custom-call | flops 1000 | bytes 1000 | tf_op jit(solution)/shard_map/pick/pallas_call | solution.py:96
  9.3 0.6 collective-permute-start.1
  10.0 2.0 %pick.5 = (bf16[2,256,256]{2,1,0:T(8,128)(2,1)}, bf16[2,256,256]{2,1,0:T(8,128)(2,1)}, bf16[2,256,256]{2,1,0:T(8,128)(2,1)}) custom-call(bf16[8,256,256]{2,1,0:T(8,128)(2,1)} %bitcast.75, bf16[8,256,256]{2,1,0:T(8,128)(2,1)} %bitcast.80), custom_call_target="tpu_custom_call" | custom-call | flops 1000 | bytes 1000 | tf_op jit(solution)/shard_map/pick/pallas_call | solution.py:96
  11.9 1.5 %collective-permute-start.3 = (bf16[2,256,256]{2,1,0:T(8,128)(2,1)}, bf16[2,256,256]{2,1,0:T(8,128)(2,1)S(1)}, u32[]{:S(2)}, u32[]{:S(2)}) collective-permute-start(bf16[2,256,256]{2,1,0:T(8,128)(2,1)} %get-tuple-element.61), channel_id=1, source_target_pairs={{0,4},{4,0},{8,12},{12,8},{1,5},{5,1},{9,13},{13,9},{2,6},{6,2},{1... | collective-permute-start | bytes 786440 | tf_op jit(solution)/shard_map/ppermute | solution.py:347
  13.4 2.4 %collective-permute-start.5 = (bf16[2,256,256]{2,1,0:T(8,128)(2,1)}, bf16[2,256,256]{2,1,0:T(8,128)(2,1)S(1)}, u32[]{:S(2)}, u32[]{:S(2)}) collective-permute-start(bf16[2,256,256]{2,1,0:T(8,128)(2,1)} %get-tuple-element.63), channel_id=1, source_target_pairs={{0,12},{4,8},{8,4},{12,0},{1,13},{5,9},{9,5},{13,1},{2,14},{6,10},... | collective-permute-start | bytes 786440 | tf_op jit(solution)/shard_map/ppermute | solution.py:347
  15.9 5.8 %collective-permute-start.4 = (bf16[2,256,256]{2,1,0:T(8,128)(2,1)}, bf16[2,256,256]{2,1,0:T(8,128)(2,1)S(1)}, u32[]{:S(2)}, u32[]{:S(2)}) collective-permute-start(bf16[2,256,256]{2,1,0:T(8,128)(2,1)} %get-tuple-element.62), channel_id=1, source_target_pairs={{0,8},{4,12},{8,0},{12,4},{1,9},{5,13},{9,1},{13,5},{2,10},{6,14},... | collective-permute-start | bytes 786440 | tf_op jit(solution)/shard_map/ppermute | solution.py:347
  21.7 0.9 copy.20
  22.7 0.9 copy.18
  23.6 0.7 copy.19
  24.3 0.8 copy.21
  25.1 6.7 %collective-permute-done.1.refs_3_ = bf16[2,256,256]{2,1,0:T(8,128)(2,1)S(1)} collective-permute-done((bf16[2,256,256]{2,1,0:T(8,128)(2,1)}, bf16[2,256,256]{2,1,0:T(8,128)(2,1)S(1)}, u32[]{:S(2)}, u32[]{:S(2)}) %collective-permute-start.1) | collective-permute-done | bytes 262176 | tf_op jit(solution)/shard_map/ppermute | solution.py:347
  31.8 0.7 copy-done.11
  32.5 10.2 %chunk.2 = (bf16[2,256,256]{2,1,0:T(8,128)(2,1)}, bf16[2,256,256]{2,1,0:T(8,128)(2,1)}, bf16[2,256,256]{2,1,0:T(8,128)(2,1)}, bf16[2,256,256]{2,1,0:T(8,128)(2,1)}, f32[8,256,256]{2,1,0:T(8,128)}) custom-call(bf16[8,256,256]{2,1,0:T(8,128)(2,1)} %bitcast.76, bf16[8,256,256]{2,1,0:T(8,128)(2,1)} %bitcast.81, bf16[2,256,256]{2,1,0:T(8,128)(2,1)} %copy-done.10, ...), custom_call_target="tpu_custom_call" | custom-call | flops 1000 | bytes 1000 | tf_op jit(solution)/shard_map/chunk/pallas_call | solution.py:315
  42.8 9.7 %collective-permute-done.4.refs_3_ = bf16[2,256,256]{2,1,0:T(8,128)(2,1)S(1)} collective-permute-done((bf16[2,256,256]{2,1,0:T(8,128)(2,1)}, bf16[2,256,256]{2,1,0:T(8,128)(2,1)S(1)}, u32[]{:S(2)}, u32[]{:S(2)}) %collective-permute-start.4) | collective-permute-done | bytes 262176 | tf_op jit(solution)/shard_map/ppermute | solution.py:347
  52.5 2.5 %collective-permute-start.10 = (bf16[2,256,256]{2,1,0:T(8,128)(2,1)}, bf16[2,256,256]{2,1,0:T(8,128)(2,1)S(1)}, u32[]{:S(2)}, u32[]{:S(2)}) collective-permute-start(bf16[2,256,256]{2,1,0:T(8,128)(2,1)} %get-tuple-element.74), channel_id=1, source_target_pairs={{0,12},{4,8},{8,4},{12,0},{1,13},{5,9},{9,5},{13,1},{2,14},{6,10},... | collective-permute-start | bytes 786440 | tf_op jit(solution)/shard_map/ppermute | solution.py:347
  55.0 10.8 %chunk.3 = (bf16[2,256,256]{2,1,0:T(8,128)(2,1)}, bf16[2,256,256]{2,1,0:T(8,128)(2,1)}, bf16[2,256,256]{2,1,0:T(8,128)(2,1)}, bf16[2,256,256]{2,1,0:T(8,128)(2,1...) custom-call(bf16[8,256,256]{2,1,0:T(8,128)(2,1)} %bitcast.77, bf16[8,256,256]{2,1,0:T(8,128)(2,1)} %bitcast.82, ...), custom_call_target="tpu_custom_call" | custom-call | flops 1000 | bytes 1000 | tf_op jit(solution)/shard_map/chunk/pallas_call | solution.py:315
  66.0 2.0 %collective-permute-done.11 = bf16[1024,256]{1,0:T(8,128)(2,1)S(1)} collective-permute-done((bf16[1024,256]{1,0:T(8,128)(2,1)}, bf16[1024,256]{1,0:T(8,128)(2,1)S(1)}, u32[]{:S(2)}, u32[]{:S(2)}) %collective-permute-start.11) | collective-permute-done | bytes 524320 | tf_op jit(solution)/shard_map/ppermute | solution.py:347
  67.9 1.4 %convert_add_fusion = f32[4,256,256]{2,1,0:T(8,128)S(1)} fusion(f32[4,256,256]{2,1,0:T(8,128)} %get-tuple-element.73, bf16[4,256,256]{2,1,0:T(8,128)(2,1)S(1)} %bitcast.102), kind=kLoop, calls=%fused_computation.1 | loop fusion | flops 524288 | bytes 2621440 | tf_op jit(solution)/shard_map/add | solution.py:434
  69.4 1.6 %collective-permute-start.12 = (bf16[128,256]{1,0:T(8,128)(2,1)S(1)}, bf16[128,256]{1,0:T(8,128)(2,1)S(1)}, u32[]{:S(2)}, u32[]{:S(2)}) collective-permute-start(bf16[128,256]{1,0:T(8,128)(2,1)S(1)} %get-tuple-element.103), channel_id=1, source_target_pairs={{0,2},{2,0},{1,3},{3,1},{4,6},{6,4},{5,7},{7,5},{8,10},{10,8},{9,1... | collective-permute-start | bytes 196616 | tf_op jit(solution)/shard_map/ppermute | solution.py:347
  71.0 0.5 collective-permute-start.13
  71.5 1.5 %collective-permute-start.14 = (bf16[128,256]{1,0:T(8,128)(2,1)S(1)}, bf16[128,256]{1,0:T(8,128)(2,1)S(1)}, u32[]{:S(2)}, u32[]{:S(2)}) collective-permute-start(bf16[128,256]{1,0:T(8,128)(2,1)S(1)} %get-tuple-element.105), channel_id=1, source_target_pairs={{0,2},{2,0},{1,3},{3,1},{4,6},{6,4},{5,7},{7,5},{8,10},{10,8},{9,1... | collective-permute-start | bytes 196616 | tf_op jit(solution)/shard_map/ppermute | solution.py:347
  73.0 0.5 collective-permute-start.15
  73.6 0.6 collective-permute-done.12
  74.1 1.3 %collective-permute-start.8 = (bf16[2,256,256]{2,1,0:T(8,128)(2,1)S(1)}, bf16[2,256,256]{2,1,0:T(8,128)(2,1)S(1)}, u32[]{:S(2)}, u32[]{:S(2)}) collective-permute-start(bf16[2,256,256]{2,1,0:T(8,128)(2,1)S(1)} %copy-done.15), channel_id=1, source_target_pairs={{0,12},{4,8},{8,4},{12,0},{1,13},{5,9},{9,5},{13,1},{2,14},{6,10},... | collective-permute-start | bytes 786440 | tf_op jit(solution)/shard_map/ppermute | solution.py:347
  75.5 0.5 collective-permute-done.13
  76.0 1.3 %collective-permute-done.14 = bf16[128,256]{1,0:T(8,128)(2,1)S(1)} collective-permute-done((bf16[128,256]{1,0:T(8,128)(2,1)S(1)}, bf16[128,256]{1,0:T(8,128)(2,1)S(1)}, u32[]{:S(2)}, u32[]{:S(2)}) %collective-permute-start.14) | collective-permute-done | bytes 65568 | tf_op jit(solution)/shard_map/ppermute | solution.py:347
  77.2 0.7 collective-permute-done.15
  78.0 7.7 %collective-permute-done.9.refs_2_ = bf16[2,256,256]{2,1,0:T(8,128)(2,1)S(1)} collective-permute-done((bf16[2,256,256]{2,1,0:T(8,128)(2,1)S(1)}, bf16[2,256,256]{2,1,0:T(8,128)(2,1)S(1)}, u32[]{:S(2)}, u32[]{:S(2)}) %collective-permute-start.9) | collective-permute-done | bytes 262176 | tf_op jit(solution)/shard_map/ppermute | solution.py:347
  85.9 2.9 %collective-permute-start.17 = (bf16[128,256]{1,0:T(8,128)(2,1)S(1)}, bf16[128,256]{1,0:T(8,128)(2,1)S(1)}, u32[]{:S(2)}, u32[]{:S(2)}) collective-permute-start(bf16[128,256]{1,0:T(8,128)(2,1)S(1)} %get-tuple-element.102), channel_id=1, source_target_pairs={{0,8},{4,12},{8,0},{12,4},{1,9},{5,13},{9,1},{13,5},{2,10},{6,14},... | collective-permute-start | bytes 196616 | tf_op jit(solution)/shard_map/ppermute | solution.py:347
  88.7 1.5 %collective-permute-start.18 = (bf16[128,256]{1,0:T(8,128)(2,1)S(1)}, bf16[128,256]{1,0:T(8,128)(2,1)S(1)}, u32[]{:S(2)}, u32[]{:S(2)}) collective-permute-start(bf16[128,256]{1,0:T(8,128)(2,1)S(1)} %get-tuple-element.101), channel_id=1, source_target_pairs={{0,12},{4,8},{8,4},{12,0},{1,13},{5,9},{9,5},{13,1},{2,14},{6,10},... | collective-permute-start | bytes 196616 | tf_op jit(solution)/shard_map/ppermute | solution.py:347
  90.3 2.4 %collective-permute-done.16 = bf16[128,256]{1,0:T(8,128)(2,1)S(1)} collective-permute-done((bf16[128,256]{1,0:T(8,128)(2,1)S(1)}, bf16[128,256]{1,0:T(8,128)(2,1)S(1)}, u32[]{:S(2)}, u32[]{:S(2)}) %collective-permute-start.16) | collective-permute-done | bytes 65568 | tf_op jit(solution)/shard_map/ppermute | solution.py:347
  92.7 2.9 %collective-permute-done.17 = bf16[128,256]{1,0:T(8,128)(2,1)S(1)} collective-permute-done((bf16[128,256]{1,0:T(8,128)(2,1)S(1)}, bf16[128,256]{1,0:T(8,128)(2,1)S(1)}, u32[]{:S(2)}, u32[]{:S(2)}) %collective-permute-start.17) | collective-permute-done | bytes 65568 | tf_op jit(solution)/shard_map/ppermute | solution.py:347
  95.6 2.0 %collective-permute-start.20 = (bf16[128,256]{1,0:T(8,128)(2,1)S(1)}, bf16[128,256]{1,0:T(8,128)(2,1)S(1)}, u32[]{:S(2)}, u32[]{:S(2)}) collective-permute-start(bf16[128,256]{1,0:T(8,128)(2,1)S(1)} %fusion.3), channel_id=1, source_target_pairs={{0,4},{4,0},{8,12},{12,8},{1,5},{5,1},{9,13},{13,9},{2,6},{6,2},{1... | collective-permute-start | bytes 196616 | tf_op jit(solution)/shard_map/ppermute | solution.py:347
  97.6 1.0 collective-permute-start.21
  98.6 1.5 %collective-permute-start.22 = (bf16[128,256]{1,0:T(8,128)(2,1)S(1)}, bf16[128,256]{1,0:T(8,128)(2,1)S(1)}, u32[]{:S(2)}, u32[]{:S(2)}) collective-permute-start(bf16[128,256]{1,0:T(8,128)(2,1)S(1)} %fusion.3), channel_id=1, source_target_pairs={{0,12},{4,8},{8,4},{12,0},{1,13},{5,9},{9,5},{13,1},{2,14},{6,10},... | collective-permute-start | bytes 196616 | tf_op jit(solution)/shard_map/ppermute | solution.py:347
  100.1 1.1 collective-permute-start.6
  101.2 1.9 %collective-permute-start.7 = (bf16[2,256,256]{2,1,0:T(8,128)(2,1)S(1)}, bf16[2,256,256]{2,1,0:T(8,128)(2,1)S(1)}, u32[]{:S(2)}, u32[]{:S(2)}) collective-permute-start(bf16[2,256,256]{2,1,0:T(8,128)(2,1)S(1)} %copy-done.12), channel_id=1, source_target_pairs={{0,8},{4,12},{8,0},{12,4},{1,9},{5,13},{9,1},{13,5},{2,10},{6,14},... | collective-permute-start | bytes 786440 | tf_op jit(solution)/shard_map/ppermute | solution.py:347
  103.0 2.8 %collective-permute-done.21 = bf16[128,256]{1,0:T(8,128)(2,1)S(1)} collective-permute-done((bf16[128,256]{1,0:T(8,128)(2,1)S(1)}, bf16[128,256]{1,0:T(8,128)(2,1)S(1)}, u32[]{:S(2)}, u32[]{:S(2)}) %collective-permute-start.21) | collective-permute-done | bytes 65568 | tf_op jit(solution)/shard_map/ppermute | solution.py:347
  105.8 0.6 gather_fusion
  106.6 1.6 %collective-permute-start.23 = (bf16[512,256]{1,0:T(8,128)(2,1)S(1)}, bf16[512,256]{1,0:T(8,128)(2,1)S(1)}, u32[]{:S(2)}, u32[]{:S(2)}) collective-permute-start(bf16[512,256]{1,0:T(8,128)(2,1)S(1)} %bitcast_select_fusion), channel_id=1, source_target_pairs={{0,2},{2,0},{1,3},{3,1},{4,6},{6,4},{5,7},{7,5},{8,10},{10,8},{9,1... | collective-permute-start | bytes 786440 | tf_op jit(solution)/shard_map/ppermute | solution.py:347
  108.1 0.6 collective-permute-start.25
  108.8 2.5 %put.2 = (bf16[8,256,256]{2,1,0:T(8,128)(2,1)}, bf16[8,256,256]{2,1,0:T(8,128)(2,1)}) custom-call(bf16[2,256,256]{2,1,0:T(8,128)(2,1)S(1)} %copy-done.1, bf16[2,256,256]{2,1,0:T(8,128)(2,1)S(1)} %collective-permute-done.19.refs_1_, bf16[2,256,256]{2,1,0:T(8,128)(2,1)S(1)} %collective-permute-done.9.refs_2_, ...), custom_call_target="tpu_custom_call" | custom-call | bytes 4194304 | tf_op jit(solution)/shard_map/put/pallas_call | solution.py:123
  111.5 4.0 %collective-permute-done.23 = bf16[512,256]{1,0:T(8,128)(2,1)S(1)} collective-permute-done((bf16[512,256]{1,0:T(8,128)(2,1)S(1)}, bf16[512,256]{1,0:T(8,128)(2,1)S(1)}, u32[]{:S(2)}, u32[]{:S(2)}) %collective-permute-start.23) | collective-permute-done | bytes 262176 | tf_op jit(solution)/shard_map/ppermute | solution.py:347
  115.4 2.5 %collective-permute-done.25 = bf16[512,256]{1,0:T(8,128)(2,1)S(1)} collective-permute-done((bf16[512,256]{1,0:T(8,128)(2,1)S(1)}, bf16[512,256]{1,0:T(8,128)(2,1)S(1)}, u32[]{:S(2)}, u32[]{:S(2)}) %collective-permute-start.25) | collective-permute-done | bytes 262176 | tf_op jit(solution)/shard_map/ppermute | solution.py:450
  117.9 1.5 %finish.1 = (f32[3,256,256]{2,1,0:T(8,128)}, f32[3,256,256]{2,1,0:T(8,128)}, f32[256,256]{1,0:T(8,128)}, f32[256,256]{1,0:T(8,128)}) custom-call(bf16[2,256,256]{2,1,0:T(8,128)(2,1)S(1)} %bitcast_select_fusion.1.own, bf16[2,256,256]{2,1,0:T(8,128)(2,1)S(1)} %bitcast.70, bf16[2,256,256]{2,1,0:T(8,128)(2,1)S(1)} %bitcast.71, bf16[2,256,256]{2,1,0:T(8,128)(2,1)S(1)} %bitcast.72), custom_call_target="tpu_custom_call" | custom-call | flops 1000 | bytes 1000 | tf_op jit(solution)/shard_map/finish/pallas_call | solution.py:167
  119.5 2.5 %put.3 = (bf16[8,256,256]{2,1,0:T(8,128)(2,1)}, bf16[8,256,256]{2,1,0:T(8,128)(2,1)}) custom-call(bf16[2,256,256]{2,1,0:T(8,128)(2,1)S(1)} %copy-done, bf16[2,256,256]{2,1,0:T(8,128)(2,1)S(1)} %collective-permute-done.6.refs_1_, bf16[2,256,256]{2,1,0:T(8,128)(2,1)S(1)} %collective-permute-done.7.refs_2_, ...), custom_call_target="tpu_custom_call", output_to_operand_aliasing={{0}: (4, {}), {1}: (5, {})} | custom-call | bytes 4194304 | tf_op jit(solution)/shard_map/put/pallas_call | solution.py:123
  (72 shorter events, 1.1 us)
Async XLA Ops:
  2.3 19.4 %copy-start.3 = (bf16[3,256,256]{2,1,0:T(8,128)(2,1)S(1)}, bf16[3,256,256]{2,1,0:T(8,128)(2,1)}, u32[]{:S(2)}) copy-start(bf16[3,256,256]{2,1,0:T(8,128)(2,1)} %param.13) | copy-start | bytes 1179652
  2.3 13.5 %collective-permute-start.2 = (bf16[2,256,256]{2,1,0:T(8,128)(2,1)}, bf16[2,256,256]{2,1,0:T(8,128)(2,1)S(1)}, u32[]{:S(2)}, u32[]{:S(2)}) collective-permute-start(bf16[2,256,256]{2,1,0:T(8,128)(2,1)} %pick.4), channel_id=1, source_target_pairs={{0,12},{4,8},{8,4},{12,0},{1,13},{5,9},{9,5},{13,1},{2,14},{6,10},... | collective-permute-start | bytes 786440 | tf_op jit(solution)/shard_map/ppermute | solution.py:347
  9.3 13.4 %copy-start.2 = (bf16[3,256,256]{2,1,0:T(8,128)(2,1)S(1)}, bf16[3,256,256]{2,1,0:T(8,128)(2,1)}, u32[]{:S(2)}) copy-start(bf16[3,256,256]{2,1,0:T(8,128)(2,1)} %param.12) | copy-start | bytes 1179652
  9.3 15.8 %collective-permute-start = (bf16[2,256,256]{2,1,0:T(8,128)(2,1)}, bf16[2,256,256]{2,1,0:T(8,128)(2,1)S(1)}, u32[]{:S(2)}, u32[]{:S(2)}) collective-permute-start(bf16[2,256,256]{2,1,0:T(8,128)(2,1)} %get-tuple-element.53), channel_id=1, source_target_pairs={{0,4},{4,0},{8,12},{12,8},{1,5},{5,1},{9,13},{13,9},{2,6},{6,2},{1... | collective-permute-start | bytes 786440 | tf_op jit(solution)/shard_map/ppermute | solution.py:347
  9.3 22.5 %collective-permute-start.1 = (bf16[2,256,256]{2,1,0:T(8,128)(2,1)}, bf16[2,256,256]{2,1,0:T(8,128)(2,1)S(1)}, u32[]{:S(2)}, u32[]{:S(2)}) collective-permute-start(bf16[2,256,256]{2,1,0:T(8,128)(2,1)} %get-tuple-element.54), channel_id=1, source_target_pairs={{0,8},{4,12},{8,0},{12,4},{1,9},{5,13},{9,1},{13,5},{2,10},{6,14},... | collective-permute-start | bytes 786440 | tf_op jit(solution)/shard_map/ppermute | solution.py:347
  11.9 11.7 %copy-start.4 = (bf16[256,256]{1,0:T(8,128)(2,1)S(1)}, bf16[256,256]{1,0:T(8,128)(2,1)}, u32[]{:S(2)}) copy-start(bf16[256,256]{1,0:T(8,128)(2,1)} %refs_7_.3) | copy-start | bytes 393220
  11.9 12.4 %copy-start.5 = (bf16[256,256]{1,0:T(8,128)(2,1)S(1)}, bf16[256,256]{1,0:T(8,128)(2,1)}, u32[]{:S(2)}) copy-start(bf16[256,256]{1,0:T(8,128)(2,1)} %refs_11_.3) | copy-start | bytes 393220
  11.9 30.8 %collective-permute-start.3 = (bf16[2,256,256]{2,1,0:T(8,128)(2,1)}, bf16[2,256,256]{2,1,0:T(8,128)(2,1)S(1)}, u32[]{:S(2)}, u32[]{:S(2)}) collective-permute-start(bf16[2,256,256]{2,1,0:T(8,128)(2,1)} %get-tuple-element.61), channel_id=1, source_target_pairs={{0,4},{4,0},{8,12},{12,8},{1,5},{5,1},{9,13},{13,9},{2,6},{6,2},{1... | collective-permute-start | bytes 786440 | tf_op jit(solution)/shard_map/ppermute | solution.py:347
  13.4 29.3 %collective-permute-start.5 = (bf16[2,256,256]{2,1,0:T(8,128)(2,1)}, bf16[2,256,256]{2,1,0:T(8,128)(2,1)S(1)}, u32[]{:S(2)}, u32[]{:S(2)}) collective-permute-start(bf16[2,256,256]{2,1,0:T(8,128)(2,1)} %get-tuple-element.63), channel_id=1, source_target_pairs={{0,12},{4,8},{8,4},{12,0},{1,13},{5,9},{9,5},{13,1},{2,14},{6,10},... | collective-permute-start | bytes 786440 | tf_op jit(solution)/shard_map/ppermute | solution.py:347
  15.9 15.9 %copy-start.8 = (bf16[2,256,256]{2,1,0:T(8,128)(2,1)}, bf16[2,256,256]{2,1,0:T(8,128)(2,1)S(1)}, u32[]{:S(2)}) copy-start(bf16[2,256,256]{2,1,0:T(8,128)(2,1)S(1)} %collective-permute-done.2.refs_4_) | copy-start | bytes 786436
  15.9 36.6 %collective-permute-start.4 = (bf16[2,256,256]{2,1,0:T(8,128)(2,1)}, bf16[2,256,256]{2,1,0:T(8,128)(2,1)S(1)}, u32[]{:S(2)}, u32[]{:S(2)}) collective-permute-start(bf16[2,256,256]{2,1,0:T(8,128)(2,1)} %get-tuple-element.62), channel_id=1, source_target_pairs={{0,8},{4,12},{8,0},{12,4},{1,9},{5,13},{9,1},{13,5},{2,10},{6,14},... | collective-permute-start | bytes 786440 | tf_op jit(solution)/shard_map/ppermute | solution.py:347
  25.1 6.7 %copy-start.10 = (bf16[2,256,256]{2,1,0:T(8,128)(2,1)}, bf16[2,256,256]{2,1,0:T(8,128)(2,1)S(1)}, u32[]{:S(2)}) copy-start(bf16[2,256,256]{2,1,0:T(8,128)(2,1)S(1)} %collective-permute-done.refs_2_) | copy-start | bytes 786436
  31.8 0.7 copy-start.11
  42.7 12.2 %copy-start.6 = (bf16[2,256,256]{2,1,0:T(8,128)(2,1)}, bf16[2,256,256]{2,1,0:T(8,128)(2,1)S(1)}, u32[]{:S(2)}) copy-start(bf16[2,256,256]{2,1,0:T(8,128)(2,1)S(1)} %collective-permute-done.3.refs_2_) | copy-start | bytes 786436
  42.8 12.2 %copy-start.7 = (bf16[2,256,256]{2,1,0:T(8,128)(2,1)}, bf16[2,256,256]{2,1,0:T(8,128)(2,1)S(1)}, u32[]{:S(2)}) copy-start(bf16[2,256,256]{2,1,0:T(8,128)(2,1)S(1)} %collective-permute-done.5.refs_4_) | copy-start | bytes 786436
  52.5 2.5 %copy-start.9 = (bf16[2,256,256]{2,1,0:T(8,128)(2,1)}, bf16[2,256,256]{2,1,0:T(8,128)(2,1)S(1)}, u32[]{:S(2)}) copy-start(bf16[2,256,256]{2,1,0:T(8,128)(2,1)S(1)} %collective-permute-done.4.refs_3_) | copy-start | bytes 786436
  52.5 13.3 %collective-permute-start.10 = (bf16[2,256,256]{2,1,0:T(8,128)(2,1)}, bf16[2,256,256]{2,1,0:T(8,128)(2,1)S(1)}, u32[]{:S(2)}, u32[]{:S(2)}) collective-permute-start(bf16[2,256,256]{2,1,0:T(8,128)(2,1)} %get-tuple-element.74), channel_id=1, source_target_pairs={{0,12},{4,8},{8,4},{12,0},{1,13},{5,9},{9,5},{13,1},{2,14},{6,10},... | collective-permute-start | bytes 786440 | tf_op jit(solution)/shard_map/ppermute | solution.py:347
  55.0 11.0 %copy-start.16 = (bf16[2,256,256]{2,1,0:T(8,128)(2,1)S(1)}, bf16[2,256,256]{2,1,0:T(8,128)(2,1)}, u32[]{:S(2)}) copy-start(bf16[2,256,256]{2,1,0:T(8,128)(2,1)} %get-tuple-element.72) | copy-start | bytes 786436
  65.7 2.2 %collective-permute-start.11 = (bf16[1024,256]{1,0:T(8,128)(2,1)}, bf16[1024,256]{1,0:T(8,128)(2,1)S(1)}, u32[]{:S(2)}, u32[]{:S(2)}) collective-permute-start(bf16[1024,256]{1,0:T(8,128)(2,1)} %bitcast.116), channel_id=1, source_target_pairs={{0,1},{1,0},{2,3},{3,2},{4,5},{5,4},{6,7},{7,6},{8,9},{9,8},{10,11... | collective-permute-start | bytes 1572872 | tf_op jit(solution)/shard_map/ppermute | solution.py:347
  65.9 19.8 %collective-permute-start.9 = (bf16[2,256,256]{2,1,0:T(8,128)(2,1)S(1)}, bf16[2,256,256]{2,1,0:T(8,128)(2,1)S(1)}, u32[]{:S(2)}, u32[]{:S(2)}) collective-permute-start(bf16[2,256,256]{2,1,0:T(8,128)(2,1)S(1)} %copy-done.16), channel_id=1, source_target_pairs={{0,8},{4,12},{8,0},{12,4},{1,9},{5,13},{9,1},{13,5},{2,10},{6,14},... | collective-permute-start | bytes 786440 | tf_op jit(solution)/shard_map/ppermute | solution.py:347
  67.9 6.2 %copy-start.15 = (bf16[2,256,256]{2,1,0:T(8,128)(2,1)S(1)}, bf16[2,256,256]{2,1,0:T(8,128)(2,1)}, u32[]{:S(2)}) copy-start(bf16[2,256,256]{2,1,0:T(8,128)(2,1)} %get-tuple-element.71) | copy-start | bytes 786436
  67.9 8.1 %copy-start.14 = (bf16[2,256,256]{2,1,0:T(8,128)(2,1)S(1)}, bf16[2,256,256]{2,1,0:T(8,128)(2,1)}, u32[]{:S(2)}) copy-start(bf16[2,256,256]{2,1,0:T(8,128)(2,1)} %get-tuple-element.79) | copy-start | bytes 786436
  69.4 4.7 %collective-permute-start.12 = (bf16[128,256]{1,0:T(8,128)(2,1)S(1)}, bf16[128,256]{1,0:T(8,128)(2,1)S(1)}, u32[]{:S(2)}, u32[]{:S(2)}) collective-permute-start(bf16[128,256]{1,0:T(8,128)(2,1)S(1)} %get-tuple-element.103), channel_id=1, source_target_pairs={{0,2},{2,0},{1,3},{3,1},{4,6},{6,4},{5,7},{7,5},{8,10},{10,8},{9,1... | collective-permute-start | bytes 196616 | tf_op jit(solution)/shard_map/ppermute | solution.py:347
  71.0 5.0 %collective-permute-start.13 = (bf16[128,256]{1,0:T(8,128)(2,1)S(1)}, bf16[128,256]{1,0:T(8,128)(2,1)S(1)}, u32[]{:S(2)}, u32[]{:S(2)}) collective-permute-start(bf16[128,256]{1,0:T(8,128)(2,1)S(1)} %get-tuple-element.106), channel_id=1, source_target_pairs={{0,2},{2,0},{1,3},{3,1},{4,6},{6,4},{5,7},{7,5},{8,10},{10,8},{9,1... | collective-permute-start | bytes 196616 | tf_op jit(solution)/shard_map/ppermute | solution.py:347
  71.5 5.8 %collective-permute-start.14 = (bf16[128,256]{1,0:T(8,128)(2,1)S(1)}, bf16[128,256]{1,0:T(8,128)(2,1)S(1)}, u32[]{:S(2)}, u32[]{:S(2)}) collective-permute-start(bf16[128,256]{1,0:T(8,128)(2,1)S(1)} %get-tuple-element.105), channel_id=1, source_target_pairs={{0,2},{2,0},{1,3},{3,1},{4,6},{6,4},{5,7},{7,5},{8,10},{10,8},{9,1... | collective-permute-start | bytes 196616 | tf_op jit(solution)/shard_map/ppermute | solution.py:347
  73.0 27.1 %copy-start.13 = (bf16[2,256,256]{2,1,0:T(8,128)(2,1)S(1)}, bf16[2,256,256]{2,1,0:T(8,128)(2,1)}, u32[]{:S(2)}) copy-start(bf16[2,256,256]{2,1,0:T(8,128)(2,1)} %get-tuple-element.69) | copy-start | bytes 786436
  73.0 28.1 %copy-start.12 = (bf16[2,256,256]{2,1,0:T(8,128)(2,1)S(1)}, bf16[2,256,256]{2,1,0:T(8,128)(2,1)}, u32[]{:S(2)}) copy-start(bf16[2,256,256]{2,1,0:T(8,128)(2,1)} %get-tuple-element.70) | copy-start | bytes 786436
  73.0 4.9 %collective-permute-start.15 = (bf16[128,256]{1,0:T(8,128)(2,1)S(1)}, bf16[128,256]{1,0:T(8,128)(2,1)S(1)}, u32[]{:S(2)}, u32[]{:S(2)}) collective-permute-start(bf16[128,256]{1,0:T(8,128)(2,1)S(1)} %get-tuple-element.104), channel_id=1, source_target_pairs={{0,2},{2,0},{1,3},{3,1},{4,6},{6,4},{5,7},{7,5},{8,10},{10,8},{9,1... | collective-permute-start | bytes 196616 | tf_op jit(solution)/shard_map/ppermute | solution.py:347
  74.1 21.5 %collective-permute-start.8 = (bf16[2,256,256]{2,1,0:T(8,128)(2,1)S(1)}, bf16[2,256,256]{2,1,0:T(8,128)(2,1)S(1)}, u32[]{:S(2)}, u32[]{:S(2)}) collective-permute-start(bf16[2,256,256]{2,1,0:T(8,128)(2,1)S(1)} %copy-done.15), channel_id=1, source_target_pairs={{0,12},{4,8},{8,4},{12,0},{1,13},{5,9},{9,5},{13,1},{2,14},{6,10},... | collective-permute-start | bytes 786440 | tf_op jit(solution)/shard_map/ppermute | solution.py:347
  76.0 19.6 %collective-permute-start.19 = (bf16[2,256,256]{2,1,0:T(8,128)(2,1)S(1)}, bf16[2,256,256]{2,1,0:T(8,128)(2,1)S(1)}, u32[]{:S(2)}, u32[]{:S(2)}) collective-permute-start(bf16[2,256,256]{2,1,0:T(8,128)(2,1)S(1)} %copy-done.14), channel_id=1, source_target_pairs={{0,4},{4,0},{8,12},{12,8},{1,5},{5,1},{9,13},{13,9},{2,6},{6,2},{1... | collective-permute-start | bytes 786440 | tf_op jit(solution)/shard_map/ppermute | solution.py:347
  78.0 30.9 %copy-start.1 = (bf16[2,256,256]{2,1,0:T(8,128)(2,1)S(1)}, bf16[2,256,256]{2,1,0:T(8,128)(2,1)}, u32[]{:S(2)}) copy-start(bf16[2,256,256]{2,1,0:T(8,128)(2,1)} %get-tuple-element.86.refs_0_) | copy-start | bytes 786436
  85.8 6.9 %collective-permute-start.16 = (bf16[128,256]{1,0:T(8,128)(2,1)S(1)}, bf16[128,256]{1,0:T(8,128)(2,1)S(1)}, u32[]{:S(2)}, u32[]{:S(2)}) collective-permute-start(bf16[128,256]{1,0:T(8,128)(2,1)S(1)} %get-tuple-element.100), channel_id=1, source_target_pairs={{0,4},{4,0},{8,12},{12,8},{1,5},{5,1},{9,13},{13,9},{2,6},{6,2},{1... | collective-permute-start | bytes 196616 | tf_op jit(solution)/shard_map/ppermute | solution.py:347
  85.9 9.7 %collective-permute-start.17 = (bf16[128,256]{1,0:T(8,128)(2,1)S(1)}, bf16[128,256]{1,0:T(8,128)(2,1)S(1)}, u32[]{:S(2)}, u32[]{:S(2)}) collective-permute-start(bf16[128,256]{1,0:T(8,128)(2,1)S(1)} %get-tuple-element.102), channel_id=1, source_target_pairs={{0,8},{4,12},{8,0},{12,4},{1,9},{5,13},{9,1},{13,5},{2,10},{6,14},... | collective-permute-start | bytes 196616 | tf_op jit(solution)/shard_map/ppermute | solution.py:347
  88.7 6.8 %collective-permute-start.18 = (bf16[128,256]{1,0:T(8,128)(2,1)S(1)}, bf16[128,256]{1,0:T(8,128)(2,1)S(1)}, u32[]{:S(2)}, u32[]{:S(2)}) collective-permute-start(bf16[128,256]{1,0:T(8,128)(2,1)S(1)} %get-tuple-element.101), channel_id=1, source_target_pairs={{0,12},{4,8},{8,4},{12,0},{1,13},{5,9},{9,5},{13,1},{2,14},{6,10},... | collective-permute-start | bytes 196616 | tf_op jit(solution)/shard_map/ppermute | solution.py:347
  95.6 7.4 %collective-permute-start.20 = (bf16[128,256]{1,0:T(8,128)(2,1)S(1)}, bf16[128,256]{1,0:T(8,128)(2,1)S(1)}, u32[]{:S(2)}, u32[]{:S(2)}) collective-permute-start(bf16[128,256]{1,0:T(8,128)(2,1)S(1)} %fusion.3), channel_id=1, source_target_pairs={{0,4},{4,0},{8,12},{12,8},{1,5},{5,1},{9,13},{13,9},{2,6},{6,2},{1... | collective-permute-start | bytes 196616 | tf_op jit(solution)/shard_map/ppermute | solution.py:347
  97.6 8.2 %collective-permute-start.21 = (bf16[128,256]{1,0:T(8,128)(2,1)S(1)}, bf16[128,256]{1,0:T(8,128)(2,1)S(1)}, u32[]{:S(2)}, u32[]{:S(2)}) collective-permute-start(bf16[128,256]{1,0:T(8,128)(2,1)S(1)} %fusion.3), channel_id=1, source_target_pairs={{0,8},{4,12},{8,0},{12,4},{1,9},{5,13},{9,1},{13,5},{2,10},{6,14},... | collective-permute-start | bytes 196616 | tf_op jit(solution)/shard_map/ppermute | solution.py:347
  98.6 7.2 %collective-permute-start.22 = (bf16[128,256]{1,0:T(8,128)(2,1)S(1)}, bf16[128,256]{1,0:T(8,128)(2,1)S(1)}, u32[]{:S(2)}, u32[]{:S(2)}) collective-permute-start(bf16[128,256]{1,0:T(8,128)(2,1)S(1)} %fusion.3), channel_id=1, source_target_pairs={{0,12},{4,8},{8,4},{12,0},{1,13},{5,9},{9,5},{13,1},{2,14},{6,10},... | collective-permute-start | bytes 196616 | tf_op jit(solution)/shard_map/ppermute | solution.py:347
  100.1 19.3 %collective-permute-start.6 = (bf16[2,256,256]{2,1,0:T(8,128)(2,1)S(1)}, bf16[2,256,256]{2,1,0:T(8,128)(2,1)S(1)}, u32[]{:S(2)}, u32[]{:S(2)}) collective-permute-start(bf16[2,256,256]{2,1,0:T(8,128)(2,1)S(1)} %copy-done.13), channel_id=1, source_target_pairs={{0,4},{4,0},{8,12},{12,8},{1,5},{5,1},{9,13},{13,9},{2,6},{6,2},{1... | collective-permute-start | bytes 786440 | tf_op jit(solution)/shard_map/ppermute | solution.py:347
  101.2 18.3 %collective-permute-start.7 = (bf16[2,256,256]{2,1,0:T(8,128)(2,1)S(1)}, bf16[2,256,256]{2,1,0:T(8,128)(2,1)S(1)}, u32[]{:S(2)}, u32[]{:S(2)}) collective-permute-start(bf16[2,256,256]{2,1,0:T(8,128)(2,1)S(1)} %copy-done.12), channel_id=1, source_target_pairs={{0,8},{4,12},{8,0},{12,4},{1,9},{5,13},{9,1},{13,5},{2,10},{6,14},... | collective-permute-start | bytes 786440 | tf_op jit(solution)/shard_map/ppermute | solution.py:347
  105.8 13.6 %copy-start = (bf16[2,256,256]{2,1,0:T(8,128)(2,1)S(1)}, bf16[2,256,256]{2,1,0:T(8,128)(2,1)}, u32[]{:S(2)}) copy-start(bf16[2,256,256]{2,1,0:T(8,128)(2,1)} %get-tuple-element.68.refs_0_) | copy-start | bytes 786436
  106.6 8.9 %collective-permute-start.23 = (bf16[512,256]{1,0:T(8,128)(2,1)S(1)}, bf16[512,256]{1,0:T(8,128)(2,1)S(1)}, u32[]{:S(2)}, u32[]{:S(2)}) collective-permute-start(bf16[512,256]{1,0:T(8,128)(2,1)S(1)} %bitcast_select_fusion), channel_id=1, source_target_pairs={{0,2},{2,0},{1,3},{3,1},{4,6},{6,4},{5,7},{7,5},{8,10},{10,8},{9,1... | collective-permute-start | bytes 786440 | tf_op jit(solution)/shard_map/ppermute | solution.py:347
  108.1 7.3 %collective-permute-start.24 = (bf16[512,256]{1,0:T(8,128)(2,1)S(1)}, bf16[512,256]{1,0:T(8,128)(2,1)S(1)}, u32[]{:S(2)}, u32[]{:S(2)}) collective-permute-start(bf16[512,256]{1,0:T(8,128)(2,1)S(1)} %bitcast_select_fusion), channel_id=1, source_target_pairs={{0,1},{1,0},{2,3},{3,2},{4,5},{5,4},{6,7},{7,6},{8,9},{9,8},{10,11... | collective-permute-start | bytes 786440 | tf_op jit(solution)/shard_map/ppermute | solution.py:347
  108.1 9.8 %collective-permute-start.25 = (bf16[512,256]{1,0:T(8,128)(2,1)S(1)}, bf16[512,256]{1,0:T(8,128)(2,1)S(1)}, u32[]{:S(2)}, u32[]{:S(2)}) collective-permute-start(bf16[512,256]{1,0:T(8,128)(2,1)S(1)} %bitcast_select_fusion), channel_id=1, source_target_pairs={{0,3},{1,2},{2,1},{3,0},{4,7},{5,6},{6,5},{7,4},{8,11},{9,10},{10,... | collective-permute-start | bytes 786440 | tf_op jit(solution)/shard_map/ppermute | solution.py:450

commit v7 on v6

--- a/solution.py
+++ b/solution.py
@@ -107,33 +107,37 @@
     )(inputs, cotangent)
 
 
-def put_kernel(n, chunk, fresh, *refs):
-    pieces, refs = refs[:n], refs[n if fresh else n + 2 :]
+def put_kernel(n, chunk, order, fresh, *refs):
+    count = len(order)
+    pieces, refs = refs[:count], refs[count if fresh else count + 2 :]
     outs, (held, sems) = refs[:2], refs[2:]
     me = lax.axis_index("chain")
     moves = [
-        (pieces[s].at[k], outs[k].at[chunk * n + (me ^ s)]) for s in range(n) for k in range(2)
+        (pieces[i].at[k], outs[k].at[chunk * n + (me ^ s)])
+        for i, s in enumerate(order)
+        for k in range(2)
     ]
     stage(moves, held, sems)
 
 
-def put(pieces, chunk, into):
+def put(pieces, chunk, into, order):
     n, (_, rows, width) = len(pieces), pieces[0].shape
+    pieces, count = [pieces[s] for s in order], len(order)
     full = jax.ShapeDtypeStruct((CHUNKS * n, rows, width), BF16)
     return pl.pallas_call(
-        functools.partial(put_kernel, n, chunk, into is None),
+        functools.partial(put_kernel, n, chunk, order, into is None),
         name="put",
-        in_specs=in_place(n if into is None else n + 2),
+        in_specs=in_place(count if into is None else count + 2),
         out_specs=in_place(2),
         out_shape=[full, full],
-        input_output_aliases={} if into is None else {n: 0, n + 1: 1},
+        input_output_aliases={} if into is None else {count: 0, count + 1: 1},
         scratch_shapes=[
-            pltpu.VMEM((2 * n, rows, width), BF16),
-            pltpu.SemaphoreType.DMA((2, 2 * n)),
+            pltpu.VMEM((2 * count, rows, width), BF16),
+            pltpu.SemaphoreType.DMA((2, 2 * count)),
         ],
         compiler_params=pltpu.CompilerParams(vmem_limit_bytes=8 << 20),
         cost_estimate=pl.CostEstimate(
-            flops=0, bytes_accessed=16 * n * rows * width, transcendentals=0
+            flops=0, bytes_accessed=16 * count * rows * width, transcendentals=0
         ),
     )(*pieces, *(into or ()))
 
@@ -446,11 +450,12 @@
     own = assemble([total] + [swap(total, "chain", s) for s in range(1, n)], place)
     own = own.reshape(2 * width, width)
     by_pair, by_core = swap(own, "pair"), swap(own, "core")
-    partial = put(results_a, 0, None)
+    partial = put(results_a, 0, None, range(n))
     by_both = lax.ppermute(own, ("pair", "core"), [(i, i ^ 3) for i in range(4)])
     sums = finish((own, by_pair, by_core, by_both), width)
+    partial = put(results_b, 1, partial, [0, *far])
     sums, partial = lax.optimization_barrier((sums, partial))
-    outputs, input_grad = put(results_b, 1, partial)
+    outputs, input_grad = put(results_b, 1, partial, [*near, *middle])
     return (outputs.reshape(shape), input_grad.reshape(shape), *sums)
 
 

time: 123 us -> 122 us (level)
  waiting for transfers between devices: 43.6 us -> 42.1 us
    ppermute x25, waiting for transfers between devices: 41.1 us -> 39.6 us  [swap(): lax.ppermute(values, axis, [(i, i ^ s) for i in range(lax.axis_size(axis))])]
    pallas_call x2 -> x3, Pallas kernels: 4.92 us -> 5.54 us  [put(): pl.pallas_call(functools.partial(put_kernel, n, chunk, order, into is Non...]
  transfers between devices with their start and end apart: 26 -> 26, of which waited for: 13 -> 13; matrix products, arithmetic and copies ran while one was open for 5% -> 5% of each run, Pallas kernels for 23% -> 25%
where the time goes in v7:
time: 122 us; the launch traced here: 121 us
  waiting for transfers between devices  42.1 us (35%)
  starting transfers between devices  37.6 us (31%)
  Pallas kernels  33.4 us (27%)
  local copies, waits for them, and re-layouts  4.99 us (4%)
  other arithmetic  1.87 us (2%)
    ppermute x25, waiting for transfers between devices, swap(): lax.ppermute(values, axis, [(i, i ^ s) for i in range(lax.axis_size(axis))])  39.6 us
    ppermute x25, starting transfers between devices, swap(): lax.ppermute(values, axis, [(i, i ^ s) for i in range(lax.axis_size(axis))])  37 us
    pallas_call x2, Pallas kernels, run_chunk(): pl.pallas_call(functools.partial(chunk_kernel, n, hops, chunk, last), nam...  21 us
    pallas_call x3, Pallas kernels, put(): pl.pallas_call(functools.partial(put_kernel, n, chunk, order, into is Non...  5.54 us
    pallas_call x3, Pallas kernels, pick(): pl.pallas_call(functools.partial(pick_kernel, n, chunk, order), name='pic...  5.44 us
    ppermute x1, waiting for transfers between devices, on_device(): lax.ppermute(own, ('pair', 'core'), [(i, i ^ 3) for i in range(4)])  2.49 us
  transfers between devices with their start and end apart: 26, of which 13 were waited for; matrix products, arithmetic and copies ran while one was open for 5% of the time, Pallas kernels for 25%

profile of v7, /device:TPU:0, one launch (start us, length us, event | category | flops | bytes accessed | tf_op | source)
XLA Modules:
  0.0 121.1 jit_solution(3504883329126884683)
XLA Ops:
  0.6 1.7 %pick.4 = bf16[2,256,256]{2,1,0:T(8,128)(2,1)} custom-call(bf16[8,256,256]{2,1,0:T(8,128)(2,1)} %bitcast.73, bf16[8,256,256]{2,1,0:T(8,128)(2,1)} %bitcast.78), custom_call_target="tpu_custom_call" | custom-call | flops 1000 | bytes 1000 | tf_op jit(solution)/shard_map/pick/pallas_call | solution.py:96
  2.3 5.1 %collective-permute-start.2 = (bf16[2,256,256]{2,1,0:T(8,128)(2,1)}, bf16[2,256,256]{2,1,0:T(8,128)(2,1)S(1)}, u32[]{:S(2)}, u32[]{:S(2)}) collective-permute-start(bf16[2,256,256]{2,1,0:T(8,128)(2,1)} %pick.4), channel_id=1, source_target_pairs={{0,12},{4,8},{8,4},{12,0},{1,13},{5,9},{9,5},{13,1},{2,14},{6,10},... | collective-permute-start | bytes 786440 | tf_op jit(solution)/shard_map/ppermute | solution.py:351
  7.4 1.8 %pick.3 = (bf16[2,256,256]{2,1,0:T(8,128)(2,1)}, bf16[2,256,256]{2,1,0:T(8,128)(2,1)}) custom-call(bf16[8,256,256]{2,1,0:T(8,128)(2,1)} %bitcast.74, bf16[8,256,256]{2,1,0:T(8,128)(2,1)} %bitcast.79), custom_call_target="tpu_custom_call" | custom-call | flops 1000 | bytes 1000 | tf_op jit(solution)/shard_map/pick/pallas_call | solution.py:96
  9.3 0.6 collective-permute-start.1
  10.0 2.0 %pick.5 = (bf16[2,256,256]{2,1,0:T(8,128)(2,1)}, bf16[2,256,256]{2,1,0:T(8,128)(2,1)}, bf16[2,256,256]{2,1,0:T(8,128)(2,1)}) custom-call(bf16[8,256,256]{2,1,0:T(8,128)(2,1)} %bitcast.75, bf16[8,256,256]{2,1,0:T(8,128)(2,1)} %bitcast.80), custom_call_target="tpu_custom_call" | custom-call | flops 1000 | bytes 1000 | tf_op jit(solution)/shard_map/pick/pallas_call | solution.py:96
  11.9 1.5 %collective-permute-start.3 = (bf16[2,256,256]{2,1,0:T(8,128)(2,1)}, bf16[2,256,256]{2,1,0:T(8,128)(2,1)S(1)}, u32[]{:S(2)}, u32[]{:S(2)}) collective-permute-start(bf16[2,256,256]{2,1,0:T(8,128)(2,1)} %get-tuple-element.63), channel_id=1, source_target_pairs={{0,4},{4,0},{8,12},{12,8},{1,5},{5,1},{9,13},{13,9},{2,6},{6,2},{1... | collective-permute-start | bytes 786440 | tf_op jit(solution)/shard_map/ppermute | solution.py:351
  13.4 2.4 %collective-permute-start.5 = (bf16[2,256,256]{2,1,0:T(8,128)(2,1)}, bf16[2,256,256]{2,1,0:T(8,128)(2,1)S(1)}, u32[]{:S(2)}, u32[]{:S(2)}) collective-permute-start(bf16[2,256,256]{2,1,0:T(8,128)(2,1)} %get-tuple-element.65), channel_id=1, source_target_pairs={{0,12},{4,8},{8,4},{12,0},{1,13},{5,9},{9,5},{13,1},{2,14},{6,10},... | collective-permute-start | bytes 786440 | tf_op jit(solution)/shard_map/ppermute | solution.py:351
  15.9 5.8 %collective-permute-start.4 = (bf16[2,256,256]{2,1,0:T(8,128)(2,1)}, bf16[2,256,256]{2,1,0:T(8,128)(2,1)S(1)}, u32[]{:S(2)}, u32[]{:S(2)}) collective-permute-start(bf16[2,256,256]{2,1,0:T(8,128)(2,1)} %get-tuple-element.64), channel_id=1, source_target_pairs={{0,8},{4,12},{8,0},{12,4},{1,9},{5,13},{9,1},{13,5},{2,10},{6,14},... | collective-permute-start | bytes 786440 | tf_op jit(solution)/shard_map/ppermute | solution.py:351
  21.7 0.9 copy.22
  22.7 0.9 copy.20
  23.6 0.7 copy.21
  24.3 0.8 copy.23
  25.1 6.7 %collective-permute-done.1.refs_3_ = bf16[2,256,256]{2,1,0:T(8,128)(2,1)S(1)} collective-permute-done((bf16[2,256,256]{2,1,0:T(8,128)(2,1)}, bf16[2,256,256]{2,1,0:T(8,128)(2,1)S(1)}, u32[]{:S(2)}, u32[]{:S(2)}) %collective-permute-start.1) | collective-permute-done | bytes 262176 | tf_op jit(solution)/shard_map/ppermute | solution.py:351
  31.8 0.7 copy-done.11
  32.5 10.2 %chunk.2 = (bf16[2,256,256]{2,1,0:T(8,128)(2,1)}, bf16[2,256,256]{2,1,0:T(8,128)(2,1)}, bf16[2,256,256]{2,1,0:T(8,128)(2,1)}, bf16[2,256,256]{2,1,0:T(8,128)(2,1)}, f32[8,256,256]{2,1,0:T(8,128)}) custom-call(bf16[8,256,256]{2,1,0:T(8,128)(2,1)} %bitcast.76, bf16[8,256,256]{2,1,0:T(8,128)(2,1)} %bitcast.81, bf16[2,256,256]{2,1,0:T(8,128)(2,1)} %copy-done.10, ...), custom_call_target="tpu_custom_call" | custom-call | flops 1000 | bytes 1000 | tf_op jit(solution)/shard_map/chunk/pallas_call | solution.py:319
  42.8 9.7 %collective-permute-done.4.refs_3_ = bf16[2,256,256]{2,1,0:T(8,128)(2,1)S(1)} collective-permute-done((bf16[2,256,256]{2,1,0:T(8,128)(2,1)}, bf16[2,256,256]{2,1,0:T(8,128)(2,1)S(1)}, u32[]{:S(2)}, u32[]{:S(2)}) %collective-permute-start.4) | collective-permute-done | bytes 262176 | tf_op jit(solution)/shard_map/ppermute | solution.py:351
  52.5 2.5 %collective-permute-start.11 = (bf16[2,256,256]{2,1,0:T(8,128)(2,1)}, bf16[2,256,256]{2,1,0:T(8,128)(2,1)S(1)}, u32[]{:S(2)}, u32[]{:S(2)}) collective-permute-start(bf16[2,256,256]{2,1,0:T(8,128)(2,1)} %get-tuple-element.76), channel_id=1, source_target_pairs={{0,12},{4,8},{8,4},{12,0},{1,13},{5,9},{9,5},{13,1},{2,14},{6,10},... | collective-permute-start | bytes 786440 | tf_op jit(solution)/shard_map/ppermute | solution.py:351
  55.0 10.8 %chunk.3 = (bf16[2,256,256]{2,1,0:T(8,128)(2,1)}, bf16[2,256,256]{2,1,0:T(8,128)(2,1)}, bf16[2,256,256]{2,1,0:T(8,128)(2,1)}, bf16[2,256,256]{2,1,0:T(8,128)(2,1...) custom-call(bf16[8,256,256]{2,1,0:T(8,128)(2,1)} %bitcast.77, bf16[8,256,256]{2,1,0:T(8,128)(2,1)} %bitcast.82, ...), custom_call_target="tpu_custom_call" | custom-call | flops 1000 | bytes 1000 | tf_op jit(solution)/shard_map/chunk/pallas_call | solution.py:319
  66.0 2.0 %collective-permute-done.12 = bf16[1024,256]{1,0:T(8,128)(2,1)S(1)} collective-permute-done((bf16[1024,256]{1,0:T(8,128)(2,1)}, bf16[1024,256]{1,0:T(8,128)(2,1)S(1)}, u32[]{:S(2)}, u32[]{:S(2)}) %collective-permute-start.12) | collective-permute-done | bytes 524320 | tf_op jit(solution)/shard_map/ppermute | solution.py:351
  67.9 1.4 %convert_add_fusion = f32[4,256,256]{2,1,0:T(8,128)S(1)} fusion(f32[4,256,256]{2,1,0:T(8,128)} %get-tuple-element.75, bf16[4,256,256]{2,1,0:T(8,128)(2,1)S(1)} %bitcast.102), kind=kLoop, calls=%fused_computation.1 | loop fusion | flops 524288 | bytes 2621440 | tf_op jit(solution)/shard_map/add | solution.py:438
  69.4 1.6 %collective-permute-start.13 = (bf16[128,256]{1,0:T(8,128)(2,1)S(1)}, bf16[128,256]{1,0:T(8,128)(2,1)S(1)}, u32[]{:S(2)}, u32[]{:S(2)}) collective-permute-start(bf16[128,256]{1,0:T(8,128)(2,1)S(1)} %get-tuple-element.107), channel_id=1, source_target_pairs={{0,2},{2,0},{1,3},{3,1},{4,6},{6,4},{5,7},{7,5},{8,10},{10,8},{9,1... | collective-permute-start | bytes 196616 | tf_op jit(solution)/shard_map/ppermute | solution.py:351
  71.0 0.5 collective-permute-start.14
  71.5 1.5 %collective-permute-start.15 = (bf16[128,256]{1,0:T(8,128)(2,1)S(1)}, bf16[128,256]{1,0:T(8,128)(2,1)S(1)}, u32[]{:S(2)}, u32[]{:S(2)}) collective-permute-start(bf16[128,256]{1,0:T(8,128)(2,1)S(1)} %get-tuple-element.109), channel_id=1, source_target_pairs={{0,2},{2,0},{1,3},{3,1},{4,6},{6,4},{5,7},{7,5},{8,10},{10,8},{9,1... | collective-permute-start | bytes 196616 | tf_op jit(solution)/shard_map/ppermute | solution.py:351
  73.5 0.6 collective-permute-done.13
  74.1 1.3 %collective-permute-start.9 = (bf16[2,256,256]{2,1,0:T(8,128)(2,1)}, bf16[2,256,256]{2,1,0:T(8,128)(2,1)S(1)}, u32[]{:S(2)}, u32[]{:S(2)}) collective-permute-start(bf16[2,256,256]{2,1,0:T(8,128)(2,1)} %get-tuple-element.73), channel_id=1, source_target_pairs={{0,12},{4,8},{8,4},{12,0},{1,13},{5,9},{9,5},{13,1},{2,14},{6,10},... | collective-permute-start | bytes 786440 | tf_op jit(solution)/shard_map/ppermute | solution.py:351
  75.5 0.5 collective-permute-done.14
  76.0 1.3 %collective-permute-done.15 = bf16[128,256]{1,0:T(8,128)(2,1)S(1)} collective-permute-done((bf16[128,256]{1,0:T(8,128)(2,1)S(1)}, bf16[128,256]{1,0:T(8,128)(2,1)S(1)}, u32[]{:S(2)}, u32[]{:S(2)}) %collective-permute-start.15) | collective-permute-done | bytes 65568 | tf_op jit(solution)/shard_map/ppermute | solution.py:351
  77.2 0.7 collective-permute-done.16
  78.0 7.7 %collective-permute-done.10.refs_2_ = bf16[2,256,256]{2,1,0:T(8,128)(2,1)S(1)} collective-permute-done((bf16[2,256,256]{2,1,0:T(8,128)(2,1)S(1)}, bf16[2,256,256]{2,1,0:T(8,128)(2,1)S(1)}, u32[]{:S(2)}, u32[]{:S(2)}) %collective-permute-start.10) | collective-permute-done | bytes 262176 | tf_op jit(solution)/shard_map/ppermute | solution.py:351
  85.9 2.9 %collective-permute-start.18 = (bf16[128,256]{1,0:T(8,128)(2,1)S(1)}, bf16[128,256]{1,0:T(8,128)(2,1)S(1)}, u32[]{:S(2)}, u32[]{:S(2)}) collective-permute-start(bf16[128,256]{1,0:T(8,128)(2,1)S(1)} %get-tuple-element.106), channel_id=1, source_target_pairs={{0,8},{4,12},{8,0},{12,4},{1,9},{5,13},{9,1},{13,5},{2,10},{6,14},... | collective-permute-start | bytes 196616 | tf_op jit(solution)/shard_map/ppermute | solution.py:351
  88.7 1.5 %collective-permute-start.19 = (bf16[128,256]{1,0:T(8,128)(2,1)S(1)}, bf16[128,256]{1,0:T(8,128)(2,1)S(1)}, u32[]{:S(2)}, u32[]{:S(2)}) collective-permute-start(bf16[128,256]{1,0:T(8,128)(2,1)S(1)} %get-tuple-element.105), channel_id=1, source_target_pairs={{0,12},{4,8},{8,4},{12,0},{1,13},{5,9},{9,5},{13,1},{2,14},{6,10},... | collective-permute-start | bytes 196616 | tf_op jit(solution)/shard_map/ppermute | solution.py:351
  90.3 2.4 %collective-permute-done.17 = bf16[128,256]{1,0:T(8,128)(2,1)S(1)} collective-permute-done((bf16[128,256]{1,0:T(8,128)(2,1)S(1)}, bf16[128,256]{1,0:T(8,128)(2,1)S(1)}, u32[]{:S(2)}, u32[]{:S(2)}) %collective-permute-start.17) | collective-permute-done | bytes 65568 | tf_op jit(solution)/shard_map/ppermute | solution.py:351
  92.7 2.9 %collective-permute-done.18 = bf16[128,256]{1,0:T(8,128)(2,1)S(1)} collective-permute-done((bf16[128,256]{1,0:T(8,128)(2,1)S(1)}, bf16[128,256]{1,0:T(8,128)(2,1)S(1)}, u32[]{:S(2)}, u32[]{:S(2)}) %collective-permute-start.18) | collective-permute-done | bytes 65568 | tf_op jit(solution)/shard_map/ppermute | solution.py:351
  95.6 2.0 %collective-permute-start.20 = (bf16[128,256]{1,0:T(8,128)(2,1)S(1)}, bf16[128,256]{1,0:T(8,128)(2,1)S(1)}, u32[]{:S(2)}, u32[]{:S(2)}) collective-permute-start(bf16[128,256]{1,0:T(8,128)(2,1)S(1)} %fusion.3), channel_id=1, source_target_pairs={{0,4},{4,0},{8,12},{12,8},{1,5},{5,1},{9,13},{13,9},{2,6},{6,2},{1... | collective-permute-start | bytes 196616 | tf_op jit(solution)/shard_map/ppermute | solution.py:351
  97.6 1.0 collective-permute-start.21
  98.6 1.5 %collective-permute-start.22 = (bf16[128,256]{1,0:T(8,128)(2,1)S(1)}, bf16[128,256]{1,0:T(8,128)(2,1)S(1)}, u32[]{:S(2)}, u32[]{:S(2)}) collective-permute-start(bf16[128,256]{1,0:T(8,128)(2,1)S(1)} %fusion.3), channel_id=1, source_target_pairs={{0,12},{4,8},{8,4},{12,0},{1,13},{5,9},{9,5},{13,1},{2,14},{6,10},... | collective-permute-start | bytes 196616 | tf_op jit(solution)/shard_map/ppermute | solution.py:351
  100.1 1.1 collective-permute-start.6
  101.2 1.9 %collective-permute-start.7 = (bf16[2,256,256]{2,1,0:T(8,128)(2,1)S(1)}, bf16[2,256,256]{2,1,0:T(8,128)(2,1)S(1)}, u32[]{:S(2)}, u32[]{:S(2)}) collective-permute-start(bf16[2,256,256]{2,1,0:T(8,128)(2,1)S(1)} %copy-done.12), channel_id=1, source_target_pairs={{0,8},{4,12},{8,0},{12,4},{1,9},{5,13},{9,1},{13,5},{2,10},{6,14},... | collective-permute-start | bytes 786440 | tf_op jit(solution)/shard_map/ppermute | solution.py:351
  103.0 2.8 %collective-permute-done.21 = bf16[128,256]{1,0:T(8,128)(2,1)S(1)} collective-permute-done((bf16[128,256]{1,0:T(8,128)(2,1)S(1)}, bf16[128,256]{1,0:T(8,128)(2,1)S(1)}, u32[]{:S(2)}, u32[]{:S(2)}) %collective-permute-start.21) | collective-permute-done | bytes 65568 | tf_op jit(solution)/shard_map/ppermute | solution.py:351
  105.8 0.6 gather_fusion
  106.6 1.6 %collective-permute-start.23 = (bf16[512,256]{1,0:T(8,128)(2,1)S(1)}, bf16[512,256]{1,0:T(8,128)(2,1)S(1)}, u32[]{:S(2)}, u32[]{:S(2)}) collective-permute-start(bf16[512,256]{1,0:T(8,128)(2,1)S(1)} %bitcast_select_fusion), channel_id=1, source_target_pairs={{0,2},{2,0},{1,3},{3,1},{4,6},{6,4},{5,7},{7,5},{8,10},{10,8},{9,1... | collective-permute-start | bytes 786440 | tf_op jit(solution)/shard_map/ppermute | solution.py:351
  108.1 0.6 collective-permute-start.25
  108.8 2.5 %put.3 = (bf16[8,256,256]{2,1,0:T(8,128)(2,1)}, bf16[8,256,256]{2,1,0:T(8,128)(2,1)}) custom-call(bf16[2,256,256]{2,1,0:T(8,128)(2,1)S(1)} %copy-done.1, bf16[2,256,256]{2,1,0:T(8,128)(2,1)S(1)} %collective-permute-done.8.refs_1_, bf16[2,256,256]{2,1,0:T(8,128)(2,1)S(1)} %collective-permute-done.10.refs_2_, ...), custom_call_target="tpu_custom_call" | custom-call | bytes 4194304 | tf_op jit(solution)/shard_map/put/pallas_call | solution.py:127
  111.3 1.5 %put.4 = (bf16[8,256,256]{2,1,0:T(8,128)(2,1)}, bf16[8,256,256]{2,1,0:T(8,128)(2,1)}) custom-call(bf16[2,256,256]{2,1,0:T(8,128)(2,1)S(1)} %copy-done, bf16[2,256,256]{2,1,0:T(8,128)(2,1)S(1)} %collective-permute-done.9.refs_1_, bf16[8,256,256]{2,1,0:T(8,128)(2,1)} %get-tuple-element.92.refs_2_, ...), custom_call_target="tpu_custom_call", output_to_operand_aliasing={{0}: (2, {}), {1}: (3, {})} | custom-call | bytes 2097152 | tf_op jit(solution)/shard_map/put/pallas_call | solution.py:127
  113.0 2.4 %collective-permute-done.23 = bf16[512,256]{1,0:T(8,128)(2,1)S(1)} collective-permute-done((bf16[512,256]{1,0:T(8,128)(2,1)S(1)}, bf16[512,256]{1,0:T(8,128)(2,1)S(1)}, u32[]{:S(2)}, u32[]{:S(2)}) %collective-permute-start.23) | collective-permute-done | bytes 262176 | tf_op jit(solution)/shard_map/ppermute | solution.py:351
  115.4 2.5 %collective-permute-done.25 = bf16[512,256]{1,0:T(8,128)(2,1)S(1)} collective-permute-done((bf16[512,256]{1,0:T(8,128)(2,1)S(1)}, bf16[512,256]{1,0:T(8,128)(2,1)S(1)}, u32[]{:S(2)}, u32[]{:S(2)}) %collective-permute-start.25) | collective-permute-done | bytes 262176 | tf_op jit(solution)/shard_map/ppermute | solution.py:454
  117.9 1.5 %finish.1 = (f32[3,256,256]{2,1,0:T(8,128)}, f32[3,256,256]{2,1,0:T(8,128)}, f32[256,256]{1,0:T(8,128)}, f32[256,256]{1,0:T(8,128)}) custom-call(bf16[2,256,256]{2,1,0:T(8,128)(2,1)S(1)} %bitcast_select_fusion.1.own, bf16[2,256,256]{2,1,0:T(8,128)(2,1)S(1)} %bitcast.70, bf16[2,256,256]{2,1,0:T(8,128)(2,1)S(1)} %bitcast.71, bf16[2,256,256]{2,1,0:T(8,128)(2,1)S(1)} %bitcast.72), custom_call_target="tpu_custom_call" | custom-call | flops 1000 | bytes 1000 | tf_op jit(solution)/shard_map/finish/pallas_call | solution.py:171
  119.4 1.5 %put.5 = (bf16[8,256,256]{2,1,0:T(8,128)(2,1)}, bf16[8,256,256]{2,1,0:T(8,128)(2,1)}) custom-call(bf16[2,256,256]{2,1,0:T(8,128)(2,1)S(1)} %collective-permute-done.6.refs_0_, bf16[2,256,256]{2,1,0:T(8,128)(2,1)S(1)} %collective-permute-done.7.refs_1_, bf16[8,256,256]{2,1,0:T(8,128)(2,1)} %get-tuple-element.96.refs_2_, ...), custom_call_target="tpu_custom_call", output_to_operand_aliasing={{0}: (2, {}), {1}: (3, {})} | custom-call | bytes 2097152 | tf_op jit(solution)/shard_map/put/pallas_call | solution.py:127
  (71 shorter events, 1.6 us)
Async XLA Ops:
  2.3 19.4 %copy-start.3 = (bf16[3,256,256]{2,1,0:T(8,128)(2,1)S(1)}, bf16[3,256,256]{2,1,0:T(8,128)(2,1)}, u32[]{:S(2)}) copy-start(bf16[3,256,256]{2,1,0:T(8,128)(2,1)} %param.13) | copy-start | bytes 1179652
  2.3 13.5 %collective-permute-start.2 = (bf16[2,256,256]{2,1,0:T(8,128)(2,1)}, bf16[2,256,256]{2,1,0:T(8,128)(2,1)S(1)}, u32[]{:S(2)}, u32[]{:S(2)}) collective-permute-start(bf16[2,256,256]{2,1,0:T(8,128)(2,1)} %pick.4), channel_id=1, source_target_pairs={{0,12},{4,8},{8,4},{12,0},{1,13},{5,9},{9,5},{13,1},{2,14},{6,10},... | collective-permute-start | bytes 786440 | tf_op jit(solution)/shard_map/ppermute | solution.py:351
  9.3 13.4 %copy-start.2 = (bf16[3,256,256]{2,1,0:T(8,128)(2,1)S(1)}, bf16[3,256,256]{2,1,0:T(8,128)(2,1)}, u32[]{:S(2)}) copy-start(bf16[3,256,256]{2,1,0:T(8,128)(2,1)} %param.12) | copy-start | bytes 1179652
  9.3 15.8 %collective-permute-start = (bf16[2,256,256]{2,1,0:T(8,128)(2,1)}, bf16[2,256,256]{2,1,0:T(8,128)(2,1)S(1)}, u32[]{:S(2)}, u32[]{:S(2)}) collective-permute-start(bf16[2,256,256]{2,1,0:T(8,128)(2,1)} %get-tuple-element.55), channel_id=1, source_target_pairs={{0,4},{4,0},{8,12},{12,8},{1,5},{5,1},{9,13},{13,9},{2,6},{6,2},{1... | collective-permute-start | bytes 786440 | tf_op jit(solution)/shard_map/ppermute | solution.py:351
  9.3 22.5 %collective-permute-start.1 = (bf16[2,256,256]{2,1,0:T(8,128)(2,1)}, bf16[2,256,256]{2,1,0:T(8,128)(2,1)S(1)}, u32[]{:S(2)}, u32[]{:S(2)}) collective-permute-start(bf16[2,256,256]{2,1,0:T(8,128)(2,1)} %get-tuple-element.56), channel_id=1, source_target_pairs={{0,8},{4,12},{8,0},{12,4},{1,9},{5,13},{9,1},{13,5},{2,10},{6,14},... | collective-permute-start | bytes 786440 | tf_op jit(solution)/shard_map/ppermute | solution.py:351
  11.9 11.7 %copy-start.4 = (bf16[256,256]{1,0:T(8,128)(2,1)S(1)}, bf16[256,256]{1,0:T(8,128)(2,1)}, u32[]{:S(2)}) copy-start(bf16[256,256]{1,0:T(8,128)(2,1)} %refs_7_.3) | copy-start | bytes 393220
  11.9 12.4 %copy-start.5 = (bf16[256,256]{1,0:T(8,128)(2,1)S(1)}, bf16[256,256]{1,0:T(8,128)(2,1)}, u32[]{:S(2)}) copy-start(bf16[256,256]{1,0:T(8,128)(2,1)} %refs_11_.3) | copy-start | bytes 393220
  11.9 30.8 %collective-permute-start.3 = (bf16[2,256,256]{2,1,0:T(8,128)(2,1)}, bf16[2,256,256]{2,1,0:T(8,128)(2,1)S(1)}, u32[]{:S(2)}, u32[]{:S(2)}) collective-permute-start(bf16[2,256,256]{2,1,0:T(8,128)(2,1)} %get-tuple-element.63), channel_id=1, source_target_pairs={{0,4},{4,0},{8,12},{12,8},{1,5},{5,1},{9,13},{13,9},{2,6},{6,2},{1... | collective-permute-start | bytes 786440 | tf_op jit(solution)/shard_map/ppermute | solution.py:351
  13.4 29.3 %collective-permute-start.5 = (bf16[2,256,256]{2,1,0:T(8,128)(2,1)}, bf16[2,256,256]{2,1,0:T(8,128)(2,1)S(1)}, u32[]{:S(2)}, u32[]{:S(2)}) collective-permute-start(bf16[2,256,256]{2,1,0:T(8,128)(2,1)} %get-tuple-element.65), channel_id=1, source_target_pairs={{0,12},{4,8},{8,4},{12,0},{1,13},{5,9},{9,5},{13,1},{2,14},{6,10},... | collective-permute-start | bytes 786440 | tf_op jit(solution)/shard_map/ppermute | solution.py:351
  15.9 15.9 %copy-start.8 = (bf16[2,256,256]{2,1,0:T(8,128)(2,1)}, bf16[2,256,256]{2,1,0:T(8,128)(2,1)S(1)}, u32[]{:S(2)}) copy-start(bf16[2,256,256]{2,1,0:T(8,128)(2,1)S(1)} %collective-permute-done.2.refs_4_) | copy-start | bytes 786436
  15.9 36.6 %collective-permute-start.4 = (bf16[2,256,256]{2,1,0:T(8,128)(2,1)}, bf16[2,256,256]{2,1,0:T(8,128)(2,1)S(1)}, u32[]{:S(2)}, u32[]{:S(2)}) collective-permute-start(bf16[2,256,256]{2,1,0:T(8,128)(2,1)} %get-tuple-element.64), channel_id=1, source_target_pairs={{0,8},{4,12},{8,0},{12,4},{1,9},{5,13},{9,1},{13,5},{2,10},{6,14},... | collective-permute-start | bytes 786440 | tf_op jit(solution)/shard_map/ppermute | solution.py:351
  25.1 6.7 %copy-start.10 = (bf16[2,256,256]{2,1,0:T(8,128)(2,1)}, bf16[2,256,256]{2,1,0:T(8,128)(2,1)S(1)}, u32[]{:S(2)}) copy-start(bf16[2,256,256]{2,1,0:T(8,128)(2,1)S(1)} %collective-permute-done.refs_2_) | copy-start | bytes 786436
  31.8 0.7 copy-start.11
  42.7 12.2 %copy-start.6 = (bf16[2,256,256]{2,1,0:T(8,128)(2,1)}, bf16[2,256,256]{2,1,0:T(8,128)(2,1)S(1)}, u32[]{:S(2)}) copy-start(bf16[2,256,256]{2,1,0:T(8,128)(2,1)S(1)} %collective-permute-done.3.refs_2_) | copy-start | bytes 786436
  42.8 12.2 %copy-start.7 = (bf16[2,256,256]{2,1,0:T(8,128)(2,1)}, bf16[2,256,256]{2,1,0:T(8,128)(2,1)S(1)}, u32[]{:S(2)}) copy-start(bf16[2,256,256]{2,1,0:T(8,128)(2,1)S(1)} %collective-permute-done.5.refs_4_) | copy-start | bytes 786436
  52.5 2.5 %copy-start.9 = (bf16[2,256,256]{2,1,0:T(8,128)(2,1)}, bf16[2,256,256]{2,1,0:T(8,128)(2,1)S(1)}, u32[]{:S(2)}) copy-start(bf16[2,256,256]{2,1,0:T(8,128)(2,1)S(1)} %collective-permute-done.4.refs_3_) | copy-start | bytes 786436
  52.5 13.3 %collective-permute-start.11 = (bf16[2,256,256]{2,1,0:T(8,128)(2,1)}, bf16[2,256,256]{2,1,0:T(8,128)(2,1)S(1)}, u32[]{:S(2)}, u32[]{:S(2)}) collective-permute-start(bf16[2,256,256]{2,1,0:T(8,128)(2,1)} %get-tuple-element.76), channel_id=1, source_target_pairs={{0,12},{4,8},{8,4},{12,0},{1,13},{5,9},{9,5},{13,1},{2,14},{6,10},... | collective-permute-start | bytes 786440 | tf_op jit(solution)/shard_map/ppermute | solution.py:351
  55.0 11.0 %copy-start.15 = (bf16[2,256,256]{2,1,0:T(8,128)(2,1)S(1)}, bf16[2,256,256]{2,1,0:T(8,128)(2,1)}, u32[]{:S(2)}) copy-start(bf16[2,256,256]{2,1,0:T(8,128)(2,1)} %get-tuple-element.74) | copy-start | bytes 786436
  65.7 2.2 %collective-permute-start.12 = (bf16[1024,256]{1,0:T(8,128)(2,1)}, bf16[1024,256]{1,0:T(8,128)(2,1)S(1)}, u32[]{:S(2)}, u32[]{:S(2)}) collective-permute-start(bf16[1024,256]{1,0:T(8,128)(2,1)} %bitcast.116), channel_id=1, source_target_pairs={{0,1},{1,0},{2,3},{3,2},{4,5},{5,4},{6,7},{7,6},{8,9},{9,8},{10,11... | collective-permute-start | bytes 1572872 | tf_op jit(solution)/shard_map/ppermute | solution.py:351
  65.9 19.8 %collective-permute-start.10 = (bf16[2,256,256]{2,1,0:T(8,128)(2,1)S(1)}, bf16[2,256,256]{2,1,0:T(8,128)(2,1)S(1)}, u32[]{:S(2)}, u32[]{:S(2)}) collective-permute-start(bf16[2,256,256]{2,1,0:T(8,128)(2,1)S(1)} %copy-done.15), channel_id=1, source_target_pairs={{0,8},{4,12},{8,0},{12,4},{1,9},{5,13},{9,1},{13,5},{2,10},{6,14},... | collective-permute-start | bytes 786440 | tf_op jit(solution)/shard_map/ppermute | solution.py:351
  67.9 8.1 %copy-start.14 = (bf16[2,256,256]{2,1,0:T(8,128)(2,1)S(1)}, bf16[2,256,256]{2,1,0:T(8,128)(2,1)}, u32[]{:S(2)}) copy-start(bf16[2,256,256]{2,1,0:T(8,128)(2,1)} %get-tuple-element.72) | copy-start | bytes 786436
  69.4 4.7 %collective-permute-start.13 = (bf16[128,256]{1,0:T(8,128)(2,1)S(1)}, bf16[128,256]{1,0:T(8,128)(2,1)S(1)}, u32[]{:S(2)}, u32[]{:S(2)}) collective-permute-start(bf16[128,256]{1,0:T(8,128)(2,1)S(1)} %get-tuple-element.107), channel_id=1, source_target_pairs={{0,2},{2,0},{1,3},{3,1},{4,6},{6,4},{5,7},{7,5},{8,10},{10,8},{9,1... | collective-permute-start | bytes 196616 | tf_op jit(solution)/shard_map/ppermute | solution.py:351
  71.0 5.0 %collective-permute-start.14 = (bf16[128,256]{1,0:T(8,128)(2,1)S(1)}, bf16[128,256]{1,0:T(8,128)(2,1)S(1)}, u32[]{:S(2)}, u32[]{:S(2)}) collective-permute-start(bf16[128,256]{1,0:T(8,128)(2,1)S(1)} %get-tuple-element.110), channel_id=1, source_target_pairs={{0,2},{2,0},{1,3},{3,1},{4,6},{6,4},{5,7},{7,5},{8,10},{10,8},{9,1... | collective-permute-start | bytes 196616 | tf_op jit(solution)/shard_map/ppermute | solution.py:351
  71.5 5.8 %collective-permute-start.15 = (bf16[128,256]{1,0:T(8,128)(2,1)S(1)}, bf16[128,256]{1,0:T(8,128)(2,1)S(1)}, u32[]{:S(2)}, u32[]{:S(2)}) collective-permute-start(bf16[128,256]{1,0:T(8,128)(2,1)S(1)} %get-tuple-element.109), channel_id=1, source_target_pairs={{0,2},{2,0},{1,3},{3,1},{4,6},{6,4},{5,7},{7,5},{8,10},{10,8},{9,1... | collective-permute-start | bytes 196616 | tf_op jit(solution)/shard_map/ppermute | solution.py:351
  73.0 27.1 %copy-start.13 = (bf16[2,256,256]{2,1,0:T(8,128)(2,1)S(1)}, bf16[2,256,256]{2,1,0:T(8,128)(2,1)}, u32[]{:S(2)}) copy-start(bf16[2,256,256]{2,1,0:T(8,128)(2,1)} %get-tuple-element.70) | copy-start | bytes 786436
  73.0 28.2 %copy-start.12 = (bf16[2,256,256]{2,1,0:T(8,128)(2,1)S(1)}, bf16[2,256,256]{2,1,0:T(8,128)(2,1)}, u32[]{:S(2)}) copy-start(bf16[2,256,256]{2,1,0:T(8,128)(2,1)} %get-tuple-element.71) | copy-start | bytes 786436
  73.0 4.9 %collective-permute-start.16 = (bf16[128,256]{1,0:T(8,128)(2,1)S(1)}, bf16[128,256]{1,0:T(8,128)(2,1)S(1)}, u32[]{:S(2)}, u32[]{:S(2)}) collective-permute-start(bf16[128,256]{1,0:T(8,128)(2,1)S(1)} %get-tuple-element.108), channel_id=1, source_target_pairs={{0,2},{2,0},{1,3},{3,1},{4,6},{6,4},{5,7},{7,5},{8,10},{10,8},{9,1... | collective-permute-start | bytes 196616 | tf_op jit(solution)/shard_map/ppermute | solution.py:351
  74.1 21.5 %collective-permute-start.9 = (bf16[2,256,256]{2,1,0:T(8,128)(2,1)}, bf16[2,256,256]{2,1,0:T(8,128)(2,1)S(1)}, u32[]{:S(2)}, u32[]{:S(2)}) collective-permute-start(bf16[2,256,256]{2,1,0:T(8,128)(2,1)} %get-tuple-element.73), channel_id=1, source_target_pairs={{0,12},{4,8},{8,4},{12,0},{1,13},{5,9},{9,5},{13,1},{2,14},{6,10},... | collective-permute-start | bytes 786440 | tf_op jit(solution)/shard_map/ppermute | solution.py:351
  76.0 19.6 %collective-permute-start.8 = (bf16[2,256,256]{2,1,0:T(8,128)(2,1)S(1)}, bf16[2,256,256]{2,1,0:T(8,128)(2,1)S(1)}, u32[]{:S(2)}, u32[]{:S(2)}) collective-permute-start(bf16[2,256,256]{2,1,0:T(8,128)(2,1)S(1)} %copy-done.14), channel_id=1, source_target_pairs={{0,4},{4,0},{8,12},{12,8},{1,5},{5,1},{9,13},{13,9},{2,6},{6,2},{1... | collective-permute-start | bytes 786440 | tf_op jit(solution)/shard_map/ppermute | solution.py:351
  78.0 30.9 %copy-start.1 = (bf16[2,256,256]{2,1,0:T(8,128)(2,1)S(1)}, bf16[2,256,256]{2,1,0:T(8,128)(2,1)}, u32[]{:S(2)}) copy-start(bf16[2,256,256]{2,1,0:T(8,128)(2,1)} %get-tuple-element.88.refs_0_) | copy-start | bytes 786436
  78.0 33.3 %copy-start = (bf16[2,256,256]{2,1,0:T(8,128)(2,1)S(1)}, bf16[2,256,256]{2,1,0:T(8,128)(2,1)}, u32[]{:S(2)}) copy-start(bf16[2,256,256]{2,1,0:T(8,128)(2,1)} %get-tuple-element.86.refs_0_) | copy-start | bytes 786436
  85.8 6.9 %collective-permute-start.17 = (bf16[128,256]{1,0:T(8,128)(2,1)S(1)}, bf16[128,256]{1,0:T(8,128)(2,1)S(1)}, u32[]{:S(2)}, u32[]{:S(2)}) collective-permute-start(bf16[128,256]{1,0:T(8,128)(2,1)S(1)} %get-tuple-element.104), channel_id=1, source_target_pairs={{0,4},{4,0},{8,12},{12,8},{1,5},{5,1},{9,13},{13,9},{2,6},{6,2},{1... | collective-permute-start | bytes 196616 | tf_op jit(solution)/shard_map/ppermute | solution.py:351
  85.9 9.7 %collective-permute-start.18 = (bf16[128,256]{1,0:T(8,128)(2,1)S(1)}, bf16[128,256]{1,0:T(8,128)(2,1)S(1)}, u32[]{:S(2)}, u32[]{:S(2)}) collective-permute-start(bf16[128,256]{1,0:T(8,128)(2,1)S(1)} %get-tuple-element.106), channel_id=1, source_target_pairs={{0,8},{4,12},{8,0},{12,4},{1,9},{5,13},{9,1},{13,5},{2,10},{6,14},... | collective-permute-start | bytes 196616 | tf_op jit(solution)/shard_map/ppermute | solution.py:351
  88.7 6.8 %collective-permute-start.19 = (bf16[128,256]{1,0:T(8,128)(2,1)S(1)}, bf16[128,256]{1,0:T(8,128)(2,1)S(1)}, u32[]{:S(2)}, u32[]{:S(2)}) collective-permute-start(bf16[128,256]{1,0:T(8,128)(2,1)S(1)} %get-tuple-element.105), channel_id=1, source_target_pairs={{0,12},{4,8},{8,4},{12,0},{1,13},{5,9},{9,5},{13,1},{2,14},{6,10},... | collective-permute-start | bytes 196616 | tf_op jit(solution)/shard_map/ppermute | solution.py:351
  95.6 7.4 %collective-permute-start.20 = (bf16[128,256]{1,0:T(8,128)(2,1)S(1)}, bf16[128,256]{1,0:T(8,128)(2,1)S(1)}, u32[]{:S(2)}, u32[]{:S(2)}) collective-permute-start(bf16[128,256]{1,0:T(8,128)(2,1)S(1)} %fusion.3), channel_id=1, source_target_pairs={{0,4},{4,0},{8,12},{12,8},{1,5},{5,1},{9,13},{13,9},{2,6},{6,2},{1... | collective-permute-start | bytes 196616 | tf_op jit(solution)/shard_map/ppermute | solution.py:351
  97.6 8.2 %collective-permute-start.21 = (bf16[128,256]{1,0:T(8,128)(2,1)S(1)}, bf16[128,256]{1,0:T(8,128)(2,1)S(1)}, u32[]{:S(2)}, u32[]{:S(2)}) collective-permute-start(bf16[128,256]{1,0:T(8,128)(2,1)S(1)} %fusion.3), channel_id=1, source_target_pairs={{0,8},{4,12},{8,0},{12,4},{1,9},{5,13},{9,1},{13,5},{2,10},{6,14},... | collective-permute-start | bytes 196616 | tf_op jit(solution)/shard_map/ppermute | solution.py:351
  98.6 7.2 %collective-permute-start.22 = (bf16[128,256]{1,0:T(8,128)(2,1)S(1)}, bf16[128,256]{1,0:T(8,128)(2,1)S(1)}, u32[]{:S(2)}, u32[]{:S(2)}) collective-permute-start(bf16[128,256]{1,0:T(8,128)(2,1)S(1)} %fusion.3), channel_id=1, source_target_pairs={{0,12},{4,8},{8,4},{12,0},{1,13},{5,9},{9,5},{13,1},{2,14},{6,10},... | collective-permute-start | bytes 196616 | tf_op jit(solution)/shard_map/ppermute | solution.py:351
  100.1 19.3 %collective-permute-start.6 = (bf16[2,256,256]{2,1,0:T(8,128)(2,1)S(1)}, bf16[2,256,256]{2,1,0:T(8,128)(2,1)S(1)}, u32[]{:S(2)}, u32[]{:S(2)}) collective-permute-start(bf16[2,256,256]{2,1,0:T(8,128)(2,1)S(1)} %copy-done.13), channel_id=1, source_target_pairs={{0,4},{4,0},{8,12},{12,8},{1,5},{5,1},{9,13},{13,9},{2,6},{6,2},{1... | collective-permute-start | bytes 786440 | tf_op jit(solution)/shard_map/ppermute | solution.py:351
  101.2 18.3 %collective-permute-start.7 = (bf16[2,256,256]{2,1,0:T(8,128)(2,1)S(1)}, bf16[2,256,256]{2,1,0:T(8,128)(2,1)S(1)}, u32[]{:S(2)}, u32[]{:S(2)}) collective-permute-start(bf16[2,256,256]{2,1,0:T(8,128)(2,1)S(1)} %copy-done.12), channel_id=1, source_target_pairs={{0,8},{4,12},{8,0},{12,4},{1,9},{5,13},{9,1},{13,5},{2,10},{6,14},... | collective-permute-start | bytes 786440 | tf_op jit(solution)/shard_map/ppermute | solution.py:351
  106.6 8.9 %collective-permute-start.23 = (bf16[512,256]{1,0:T(8,128)(2,1)S(1)}, bf16[512,256]{1,0:T(8,128)(2,1)S(1)}, u32[]{:S(2)}, u32[]{:S(2)}) collective-permute-start(bf16[512,256]{1,0:T(8,128)(2,1)S(1)} %bitcast_select_fusion), channel_id=1, source_target_pairs={{0,2},{2,0},{1,3},{3,1},{4,6},{6,4},{5,7},{7,5},{8,10},{10,8},{9,1... | collective-permute-start | bytes 786440 | tf_op jit(solution)/shard_map/ppermute | solution.py:351
  108.1 7.3 %collective-permute-start.24 = (bf16[512,256]{1,0:T(8,128)(2,1)S(1)}, bf16[512,256]{1,0:T(8,128)(2,1)S(1)}, u32[]{:S(2)}, u32[]{:S(2)}) collective-permute-start(bf16[512,256]{1,0:T(8,128)(2,1)S(1)} %bitcast_select_fusion), channel_id=1, source_target_pairs={{0,1},{1,0},{2,3},{3,2},{4,5},{5,4},{6,7},{7,6},{8,9},{9,8},{10,11... | collective-permute-start | bytes 786440 | tf_op jit(solution)/shard_map/ppermute | solution.py:351
  108.1 9.8 %collective-permute-start.25 = (bf16[512,256]{1,0:T(8,128)(2,1)S(1)}, bf16[512,256]{1,0:T(8,128)(2,1)S(1)}, u32[]{:S(2)}, u32[]{:S(2)}) collective-permute-start(bf16[512,256]{1,0:T(8,128)(2,1)S(1)} %bitcast_select_fusion), channel_id=1, source_target_pairs={{0,3},{1,2},{2,1},{3,0},{4,7},{5,6},{6,5},{7,4},{8,11},{9,10},{10,... | collective-permute-start | bytes 786440 | tf_op jit(solution)/shard_map/ppermute | solution.py:454
